TPU v7x, 256 devices: a whole 4x4x8 slice. The times are simulated.
256 devices in a mesh: dp: 8 (over y_hi, x), ctx: 32 (over y_lo, z, core).
Axes of the slice: x: 4, y: 4 (y_hi: 2, y_lo: 2; y = y_hi * 2 + y_lo), z: 8, core: 2. Of those that a mesh axis runs over, the one named last changes fastest.
Arguments:
- queries: bfloat16 [8, 4096, 1024], P('dp', 'ctx'), may hold values from -180 to 180
- keys: bfloat16 [8, 16384, 128], P('dp', 'ctx'), may hold values from -6 to 6
- values: bfloat16 [8, 16384, 128], P('dp', 'ctx'), may hold values from -6 to 6
- grad_out: bfloat16 [8, 4096, 1024], P('dp', 'ctx'), may hold values from -6 to 6
- saved_out: bfloat16 [8, 4096, 1024], P('dp', 'ctx'), may hold values from -1.796875 to 1.796875
- segment_ids: int32 [8, 16384], P('dp', 'ctx'), may hold values from 0 to 127, never falling along the last dimension, each value on 1 to 1024 neighbouring positions
- frame_flags: int32 [8, 128], P('dp'), may hold values 0 or 1
Outputs:
- grad_queries: bfloat16 [8, 4096, 1024], P('dp', 'ctx')
- grad_keys: bfloat16 [8, 16384, 128], P('dp', 'ctx')
- grad_values: bfloat16 [8, 16384, 128], P('dp', 'ctx')
All inputs are finite; a program needn't handle non-finite values. No bound on the sum of `frame_flags` on one device may be relied on, other than what follows from the above.
Results may differ from a plain program's by a relative error of at most 0.0051.
Values may be sent and summed in bfloat16 or wider, within the bound.
No kernel may reach another device: no remote copies, remote signals or barrier semaphores. Data moves between devices by JAX's collectives and lax.ppermute only.
A program may use at most 64 MiB of HBM per device.

v0:
```python
import functools
import math

import jax
import jax.numpy as jnp
from jax import lax
from jax.experimental import pallas as pl
from jax.experimental.pallas import tpu as pltpu
from jax.sharding import PartitionSpec as P


H = 8
HD = 128
NQ = 128
NK = 512
NZ = 8
SCALE = 1.0 / math.sqrt(HD)
C2 = SCALE * math.log2(math.e)
NEG = -1e30
F32 = jnp.float32
BF16 = jnp.bfloat16
VM = pl.BlockSpec(memory_space=pltpu.VMEM)
SM = pl.BlockSpec(memory_space=pltpu.SMEM)
MIB = 1 << 20


def flip(rho):
    mask = (rho & 1) | ((rho >> 1) << 4)
    return [(i, i ^ mask) for i in range(32)]


def turn(step):
    return [(i, (i // 16) * 16 + (i % 16 + 2 * step) % 16) for i in range(32)]


def dot_nn(left, right):
    return lax.dot_general(left, right, (((1,), (0,)), ((), ())), preferred_element_type=F32)


def dot_tn(left, right):
    return lax.dot_general(left, right, (((0,), (0,)), ((), ())), preferred_element_type=F32)


def call(body, out, specs, scratch=(), vmem=8, flops=0, nbytes=0, alias=None):
    return pl.pallas_call(
        body,
        out_shape=out,
        in_specs=specs,
        out_specs=jax.tree.map(lambda _: VM, out),
        scratch_shapes=list(scratch),
        input_output_aliases=alias or {},
        cost_estimate=pl.CostEstimate(flops=flops, bytes_accessed=nbytes, transcendentals=0),
        compiler_params=pltpu.CompilerParams(vmem_limit_bytes=vmem * MIB),
    )


def shape(dims, dtype=BF16):
    return jax.ShapeDtypeStruct(dims, dtype)


def each(count, body):
    lax.fori_loop(0, count, lambda t, _: (body(t), 0)[1], 0)


def lanes(t):
    return pl.ds(pl.multiple_of(t * 128, 128), 128)


def take_sets(kv, kvs):
    def rows(t):
        part = pl.ds(pl.multiple_of(t * 48, 16), 48)
        for n in range(len(kvs)):
            kv[n, part, :] = kvs[n][part, :]

    each(11, rows)


def column(row):
    return jnp.broadcast_to(row, (128, 128)).T


def begin_body(tab, k_hbm, v_hbm, seg_hbm, flag_hbm, q_hbm, o0, o1, o2, o3, q_out, k_ref, v_ref, seg_ref, flag_ref, sems):
    moves = [
        pltpu.make_async_copy(source, target, sems.at[n])
        for n, (source, target) in enumerate(
            [(seg_hbm, seg_ref), (flag_hbm, flag_ref), (k_hbm, k_ref), (v_hbm, v_ref), (q_hbm, q_out.at[0:NQ, :])]
        )
    ]
    for move in moves:
        move.start()
    moves[0].wait()
    moves[1].wait()
    own = seg_ref[:, NK - NQ :]
    ident = lax.broadcasted_iota(jnp.int32, (128, 128), 0)
    framed = jnp.sum(jnp.where(ident == own, column(flag_ref[...]), 0), axis=0, keepdims=True)
    tag = jnp.where(framed == 1, own, -1).astype(F32)
    q_out[NQ:, :] = jnp.broadcast_to(jnp.concatenate([tag] * H, axis=1), (16, H * HD)).astype(BF16)
    moves[2].wait()
    moves[3].wait()
    for rho, out in enumerate((o0, o1, o2, o3)):
        first = pl.multiple_of((tab[1] ^ rho) * 128, 128)
        out[0:128, 0:HD] = k_ref[pl.ds(first, 128), :]
        out[0:128, HD:] = v_ref[pl.ds(first, 128), :]
        seg = seg_ref[:, pl.ds(first, 128)].astype(F32)
        out[128:, :] = jnp.broadcast_to(jnp.concatenate([seg, seg], axis=1), (16, 256)).astype(BF16)
    moves[4].wait()


def join_body(p0, p1, p2, p3, out):
    row = lax.broadcasted_iota(jnp.int32, (16, 256), 0)
    seg = jnp.zeros((16, 256), F32)
    for rho, part in enumerate((p0, p1, p2, p3)):
        out[128 * rho : 128 * rho + 128, :] = part[0:128, :]
        seg = jnp.where(row == rho, part[128:, :].astype(F32), seg)
    out[NK:, :] = seg.astype(BF16)


def cotangent_body(g_ref, saved_ref, out_ref):
    out_ref[0:NQ, :] = g_ref[...]
    row = lax.broadcasted_iota(jnp.int32, (16, HD), 0)
    for h in range(H):
        cols = slice(h * HD, h * HD + HD)
        both = g_ref[:, cols].astype(F32) * saved_ref[:, cols].astype(F32)
        mean = jnp.sum(both.T, axis=0, keepdims=True)
        top = mean.astype(BF16).astype(F32)
        mid = (mean - top).astype(BF16).astype(F32)
        low = mean - top - mid
        out_ref[NQ:, cols] = jnp.where(row == 0, top, jnp.where(row == 1, mid, low)).astype(BF16)


def turn_body(pieces, q0, q1, q2, q3, tall_ref, wide_ref, row_ref):
    def head(h):
        for rho, q in enumerate((q0, q1, q2, q3)):
            tile = q[0:NQ, lanes(h)]
            tall_ref[rho, lanes(h), :] = tile
            wide_ref[rho, :, lanes(h)] = tile.astype(F32).T.astype(BF16)

    each(H, head)
    for rho, q in enumerate((q0, q1, q2, q3)):
        extra = q[NQ:, :].astype(F32)
        row = extra[0:1, :]
        for n in range(1, pieces):
            row = row + extra[n : n + 1, :]
        row_ref[rho] = row


def item_kind(tab, z_keys, half, rho):
    z, col = tab[0], tab[1]
    own = col ^ rho
    block = 16 * (own >> 1) + 2 * z + (own & 1)
    b0 = col ^ (2 * half)
    b1 = b0 ^ 1
    p0 = (16 * (b0 >> 1) + 2 * z_keys + (b0 & 1)) * NK + 128 * col
    p1 = (16 * (b1 >> 1) + 2 * z_keys + (b1 & 1)) * NK + 128 * col
    first = block * NK + NK - NQ
    full = jnp.maximum(p0, p1) + 127 <= first
    some = jnp.minimum(p0, p1) <= first + NQ - 1 + 1023
    return p0, p1, first, full, some


def visible_of(kv, n, half, p0, p1, first, tag):
    row = lax.broadcasted_iota(jnp.int32, (128, NQ), 0)
    query = lax.broadcasted_iota(jnp.int32, (128, NQ), 1) + first
    seg = kv[n, NK:, 0:128].astype(F32)
    which = lax.broadcasted_iota(jnp.int32, (16, 128), 0)
    parts = []
    for c, p in enumerate((p0, p1)):
        line = jnp.sum(jnp.where(which == 2 * half + c, seg, 0.0), axis=0, keepdims=True)
        parts.append(jnp.where((p + row <= query) | (column(line) == tag), 1.0, 0.0))
    both = jnp.concatenate(parts, axis=0)
    return jnp.concatenate([both, both], axis=1) > 0.5


def items(ks, rhos, tab, body, masks):
    edge = 0 in ks or 1 in ks
    own = ks == (0,)

    def item(t, _):
        n = t // len(rhos)
        rho = rhos[0] + t % len(rhos)
        k = ks[0] if len(ks) == 1 else jnp.where(n == 0, ks[0], ks[1])
        z_keys = (tab[0] + k + NZ) & (NZ - 1)

        def one(half, _):
            kind = item_kind(tab, z_keys, half, rho)
            full, some = kind[3:]
            if edge:
                pl.when(full | some)(lambda: body(n, rho, half, NK // 2, kind, masks))
            else:
                pl.when(full)(lambda: body(n, rho, half, NK // 2, kind, False))
            return 0

        if own:
            lax.fori_loop(0, 2, one, 0)
        else:
            both = item_kind(tab, z_keys, 0, rho)[3] & item_kind(tab, z_keys, 1, rho)[3]
            pl.when(both)(lambda: body(n, rho, 0, NK, None, False))

            @pl.when(jnp.logical_not(both))
            def _():
                lax.fori_loop(0, 2, one, 0)

        return 0

    lax.fori_loop(0, len(rhos) * len(ks), item, 0)


def stats_body(ks, *refs):
    n_sets = len(ks)
    tab, tag_ref, wide_ref = refs[:3]
    kvs = refs[5 : 5 + n_sets]
    m_ref, l_ref, e_ref, t_ref, kv = refs[5 + n_sets :]
    m_ref[...] = refs[3][...]
    l_ref[...] = refs[4][...]
    take_sets(kv, kvs)

    def body(n, rho, half, size, kind, masked):
        rows = pl.ds(pl.multiple_of(half * 256, 256), size)
        keys = kv[n, rows, 0:HD]
        if masked:
            vis = visible_of(kv, n, half, *kind[:3], tag_ref[rho, :, 0:128])
        for p in range(4):
            cols = slice(256 * p, 256 * p + 256)
            s = dot_nn(keys, wide_ref[rho, :, cols])
            if masked:
                s = jnp.where(vis, s, NEG)
            m_old = m_ref[rho, :, cols]
            m_new = jnp.maximum(m_old, jnp.max(s, axis=0, keepdims=True))
            e = jnp.exp2((s - m_new) * C2)
            if masked:
                e = jnp.where(vis, e, 0.0)
            e_ref[n * 4 + rho, rows, cols] = e.astype(BF16)
            t_ref[(n * 4 + rho) * 2 + half, :, cols] = m_new
            l_ref[rho, :, cols] = l_ref[rho, :, cols] * jnp.exp2((m_old - m_new) * C2) + jnp.sum(
                e, axis=0, keepdims=True
            )
            m_ref[rho, :, cols] = m_new

    items(ks, (0, 1, 2, 3), tab, body, True)


def grads_body(ks, rhos, first, last, *refs):
    n_sets = len(ks)
    tab, mean_ref, log_ref, qt_ref, gw_ref, gt_ref, e_ref, t_ref = refs[:8]
    kvs, rest = refs[8 : 8 + n_sets], refs[8 + n_sets :]
    if first:
        dq_ref, acc, kv, p_all, d_all = rest

        def wipe(t):
            dq_ref[:, :, lanes(t)] = jnp.zeros((4, HD, 128), F32)

        each(H, wipe)
    elif last:
        dq_in, o0, o1, acc, kv, p_all, d_all, dq_ref = rest

        def fetch(t):
            dq_ref[:, :, lanes(t)] = dq_in[rhos[0] : rhos[0] + 2, :, lanes(t)]

        each(H, fetch)
    else:
        _, dq_ref, acc, kv, p_all, d_all = rest
    take_sets(kv, kvs)

    def clear(t):
        acc[:, lanes(t), :] = jnp.zeros((n_sets, 128, 2 * HD), F32)

    each(NK // 128, clear)

    def body(n, rho, half, size, kind, masked):
        rows = pl.ds(pl.multiple_of(half * 256, 256), size)
        keys = kv[n, rows, 0:HD]
        vals = kv[n, rows, HD:]
        for p in range(4):
            cols = slice(256 * p, 256 * p + 256)
            dp = dot_nn(vals, gw_ref[rho, :, cols])
            share = jnp.exp2((t_ref[(n * 4 + rho) * 2 + half, :, cols] - log_ref[rho, :, cols]) * C2)
            prob = e_ref[n * 4 + rho, rows, cols].astype(F32) * share
            p_all[0:size, cols] = prob.astype(BF16)
            d_all[0:size, cols] = (prob * (dp - mean_ref[rho, :, cols])).astype(BF16)
        d = d_all[0:size, :]
        acc[n, rows, 0:HD] += dot_nn(d, qt_ref[rho])
        acc[n, rows, HD:] += dot_nn(p_all[0:size, :], gt_ref[rho])
        dq_ref[rho - rhos[0]] += dot_tn(keys, d)

    items(ks, rhos, tab, body, False)
    if last:

        def head(h):
            for r, out in enumerate((o0, o1)):
                out[:, lanes(h)] = (dq_ref[r, :, lanes(h)].T * SCALE).astype(BF16)

        each(H, head)


def place_body(tab, a0, a1, a2, a3, q0, q1, q2, gq_ref, gk_ref, gv_ref):
    col = tab[1]
    for rho, part in enumerate((a0, a1, a2, a3)):
        rows = pl.ds(pl.multiple_of((col ^ rho) * 128, 128), 128)
        gk_ref[rows, :] = part[:, 0:HD]
        gv_ref[rows, :] = part[:, HD:]
    total = q0[...].astype(F32) + q1[...].astype(F32) + q2[...].astype(F32)
    gq_ref[...] = total.astype(BF16)


def per_device(queries, keys, values, grad_out, saved_out, segment_ids, frame_flags):
    hop = functools.partial(lax.ppermute, axis_name="ctx")
    rank = lax.axis_index("ctx").astype(jnp.int32)
    tab = jnp.stack([(rank >> 1) & 7, 2 * (rank >> 4) + (rank & 1)])
    hbm = pl.BlockSpec(memory_space=pltpu.HBM)

    *parts, q_own = call(
        begin_body, [shape((144, 256))] * 4 + [shape((NQ + 16, H * HD))], [SM] + [hbm] * 5, nbytes=MIB,
        scratch=[
            pltpu.VMEM((NK, HD), BF16), pltpu.VMEM((NK, HD), BF16), pltpu.VMEM((1, NK), jnp.int32),
            pltpu.VMEM((1, 128), jnp.int32), pltpu.SemaphoreType.DMA((5,)),
        ],
        vmem=58,
    )(tab, keys[0], values[0], segment_ids, frame_flags, queries[0])
    got = [hop(parts[r], perm=flip(r)) for r in (1, 2, 3)]
    own_set = call(join_body, shape((NK + 16, 256)), [VM] * 4, nbytes=MIB)(parts[0], *got)

    def four(x):
        other = hop(x, perm=flip(2))
        return (x, hop(x, perm=flip(1)), other, hop(other, perm=flip(1)))

    q_four = four(q_own)
    g_own = call(cotangent_body, shape((NQ + 16, H * HD)), [VM] * 2, nbytes=MIB)(grad_out[0], saved_out[0])
    forms = [shape((4, NQ * H, HD)), shape((4, HD, NQ * H)), shape((4, 1, NQ * H), F32)]

    def turned(four_of, pieces):
        return call(functools.partial(turn_body, pieces), forms, [VM] * 4, vmem=16, nbytes=4 * MIB)(*four_of)

    q_tall, q_wide, tag = turned(q_four, 1)
    stat = shape((4, 1, NQ * H), F32)
    m = jnp.full((4, 1, NQ * H), NEG, F32)
    l = jnp.zeros((4, 1, NQ * H), F32)
    sets = {0: own_set}
    kept = {}
    fwd = bwd = own_set
    for step in range(5):
        ks = (0,) if step == 0 else (4,) if step == 4 else (step, -step)
        n = len(ks)
        if step < 3:
            fwd, bwd = hop(fwd, perm=turn(1)), hop(bwd, perm=turn(-1))
        elif step == 3:
            bwd = hop(bwd, perm=turn(-1))
        m, l, *kept[ks] = call(
            functools.partial(stats_body, ks),
            [stat, stat, shape((4 * n, NK, NQ * H)), shape((8 * n, 1, NQ * H), F32)],
            [SM] + [VM] * (4 + n), vmem=3,
            scratch=[pltpu.VMEM((n, NK + 16, 256), BF16)], flops=n * (1 << 29), nbytes=2 * MIB,
        )(tab, tag, q_wide, m, l, *[sets[k] for k in ks])
        if step < 4:
            fwd, bwd, m, l = lax.optimization_barrier((fwd, bwd, m, l))
            sets[step + 1] = bwd
            if step < 3:
                sets[-step - 1] = fwd
        if step == 0:
            g_four = four(g_own)
    g_tall, g_wide, mean = turned(g_four, 3)

    ml = jnp.concatenate([m, l], axis=0)
    tops, sums = [m], [l]
    for r in (1, 2, 3):
        got = hop(ml, perm=flip(r))
        tops.append(jnp.concatenate([got[rho ^ r : (rho ^ r) + 1] for rho in range(4)], axis=0))
        sums.append(jnp.concatenate([got[4 + (rho ^ r) : 5 + (rho ^ r)] for rho in range(4)], axis=0))
    top = functools.reduce(jnp.maximum, tops)
    total = sum(s * jnp.exp2((t - top) * C2) for s, t in zip(sums, tops))
    log_total = top + jnp.log2(total) * (1.0 / C2)

    dq = None
    up = down = None
    dq_shape = shape((4, HD, NQ * H), F32)

    def grads(ks, rhos, dq):
        n = len(ks)
        first, last = dq is None, ks == (0,)
        args = [tab, mean, log_total, q_tall, g_wide, g_tall, *kept[ks]] + [sets[k] for k in ks]
        args += [] if first else [dq]
        piece = shape((NQ, H * HD))
        scratch = [pltpu.VMEM((n, NK + 16, 256), BF16)] + [pltpu.VMEM((NK, NQ * H), BF16)] * 2
        return call(
            functools.partial(grads_body, ks, rhos, first, last),
            ([piece, piece] if last else [dq_shape]) + [shape((n, NK, 2 * HD), F32)],
            [SM] + [VM] * (len(args) - 1),
            scratch=scratch + ([pltpu.VMEM((2, HD, NQ * H), F32)] if last else []),
            vmem=5, flops=n * 5 * (1 << 29), nbytes=8 * MIB,
            alias={} if first or last else {len(args) - 1: 0},
        )(*args)

    for ks in ((4,), (3, -3), (2, -2), (1, -1)):
        n = len(ks)
        dq, adds = grads(ks, (0, 1, 2, 3), dq)
        sends = [(adds[0] if up is None else adds[0] + up.astype(F32)).astype(BF16)]
        if n == 2:
            sends.append((adds[1] if down is None else adds[1] + down.astype(F32)).astype(BF16))
        dq, *sends = lax.optimization_barrier((dq, *sends))
        up = hop(sends[0], perm=turn(1))
        if n == 2:
            down = hop(sends[1], perm=turn(-1))
    dq2, dq3, far_adds = grads((0,), (2, 3), dq)
    dq3 = hop(dq3, perm=flip(1))
    across = (dq2.astype(F32) + dq3.astype(F32)).astype(BF16)
    dq_far = hop(across, perm=flip(2))
    dq0, dq1, near_adds = grads((0,), (0, 1), dq)
    own = far_adds[0] + near_adds[0] + up.astype(F32) + down.astype(F32)
    scales = jnp.where(jnp.arange(2 * HD) < HD, SCALE, 1.0).astype(F32)
    own = (own * scales[None, :]).astype(BF16)
    q_back = [dq0, hop(dq1, perm=flip(1)), dq_far]
    a_back = [own[0:128]] + [hop(own[128 * r : 128 * r + 128], perm=flip(r)) for r in (1, 2, 3)]
    gq, gk, gv = call(
        place_body, [shape((NQ, H * HD)), shape((NK, HD)), shape((NK, HD))], [SM] + [VM] * 7,
        nbytes=2 * MIB,
    )(tab, *a_back, *q_back)
    return gq[None], gk[None], gv[None]


def solution(mesh):
    row = P("dp", "ctx", None)
    return jax.shard_map(
        per_device,
        mesh=mesh,
        in_specs=(row, row, row, row, row, P("dp", "ctx"), P("dp", None)),
        out_specs=(row, row, row),
        check_vma=False,
    )
```

profile of v0, /device:TPU:1, one launch (start us, length us, event | category | flops | bytes accessed | tf_op | source)
XLA Modules:
  0.0 133.9 jit_solution(16794693625840630877)
XLA Ops:
  1.3 2.6 %shard_map.96 = (bf16[144,256]{1,0:T(8,128)(2,1)}, bf16[144,256]{1,0:T(8,128)(2,1)}, bf16[144,256]{1,0:T(8,128)(2,1)}, bf16[144,256]{1,0:T(8,128)(2,1)}, bf16[144,1024]{1,0:T(8,128)(2,1)}) custom-call(s32[2]{0:T(128)} %pad_add_fusion.tab.refs_0_, bf16[512,128]{1,0:T(8,128)(2,1)} %bitcast.45, bf16[512,128]{1,0:T(8,128)(2,1)} %bitcast.46, s32[1,512]{1,0:T(1,128)} %seg_hbm.1, ...), custom_call_target="tpu_custom_call" | custom-call | bytes 1048576 | tf_op jit(solution)/shard_map/pallas_call | solution.py:311
  4.0 2.2 %collective-permute-start.4 = (bf16[144,1024]{1,0:T(8,128)(2,1)}, bf16[144,1024]{1,0:T(8,128)(2,1)S(1)}, u32[]{:S(2)}, u32[]{:S(2)}) collective-permute-start(bf16[144,1024]{1,0:T(8,128)(2,1)} %get-tuple-element.78.q0), channel_id=1, source_target_pairs={{0,16},{1,17},{2,18},{3,19},{4,20},{5,21},{6,22},{7,23},{8,24},{9,... | collective-permute-start | bytes 884744 | tf_op jit(solution)/shard_map/ppermute | solution.py:323
  6.2 1.2 collective-permute-start.3
  7.3 4.7 %collective-permute-done.4.q2 = bf16[144,1024]{1,0:T(8,128)(2,1)S(1)} collective-permute-done((bf16[144,1024]{1,0:T(8,128)(2,1)}, bf16[144,1024]{1,0:T(8,128)(2,1)S(1)}, u32[]{:S(2)}, u32[]{:S(2)}) %collective-permute-start.4) | collective-permute-done | bytes 294944 | tf_op jit(solution)/shard_map/ppermute | solution.py:323
  12.0 2.3 %collective-permute-start.5 = (bf16[144,1024]{1,0:T(8,128)(2,1)S(1)}, bf16[144,1024]{1,0:T(8,128)(2,1)S(1)}, u32[]{:S(2)}, u32[]{:S(2)}) collective-permute-start(bf16[144,1024]{1,0:T(8,128)(2,1)S(1)} %collective-permute-done.4.q2), channel_id=1, source_target_pairs={{0,1},{1,0},{2,3},{3,2},{4,5},{5,4},{6,7},{7,6},{8,9},{9,8},{10,11... | collective-permute-start | bytes 884744 | tf_op jit(solution)/shard_map/ppermute | solution.py:324
  14.3 1.5 %collective-permute-start.7 = (bf16[144,256]{1,0:T(8,128)(2,1)}, bf16[144,256]{1,0:T(8,128)(2,1)S(1)}, u32[]{:S(2)}, u32[]{:S(2)}) collective-permute-start(bf16[144,256]{1,0:T(8,128)(2,1)} %get-tuple-element.83), channel_id=1, source_target_pairs={{0,16},{1,17},{2,18},{3,19},{4,20},{5,21},{6,22},{7,23},{8,24},{9,... | collective-permute-start | bytes 221192 | tf_op jit(solution)/shard_map/ppermute | solution.py:319
  16.5 1.3 collective-permute-done.7.p2
  17.7 3.0 %collective-permute-done.8.p3 = bf16[144,256]{1,0:T(8,128)(2,1)S(1)} collective-permute-done((bf16[144,256]{1,0:T(8,128)(2,1)}, bf16[144,256]{1,0:T(8,128)(2,1)S(1)}, u32[]{:S(2)}, u32[]{:S(2)}) %collective-permute-start.8) | collective-permute-done | bytes 73760 | tf_op jit(solution)/shard_map/ppermute | solution.py:319
  20.8 0.9 copy-done.3
  21.7 1.7 %collective-permute-start.9 = (bf16[528,256]{1,0:T(8,128)(2,1)S(1)}, bf16[528,256]{1,0:T(8,128)(2,1)S(1)}, u32[]{:S(2)}, u32[]{:S(2)}) collective-permute-start(bf16[528,256]{1,0:T(8,128)(2,1)S(1)} %shard_map.98.refs_5_.refs_8_), channel_id=1, source_target_pairs={{0,2},{1,3},{2,4},{3,5},{4,6},{5,7},{6,8},{7,9},{8,10},{9,11},{10,... | collective-permute-start | bytes 811016 | tf_op jit(solution)/shard_map/ppermute | solution.py:344
  23.4 4.0 %collective-permute-start.10 = (bf16[528,256]{1,0:T(8,128)(2,1)S(1)}, bf16[528,256]{1,0:T(8,128)(2,1)S(1)}, u32[]{:S(2)}, u32[]{:S(2)}) collective-permute-start(bf16[528,256]{1,0:T(8,128)(2,1)S(1)} %shard_map.98.refs_5_.refs_8_), channel_id=1, source_target_pairs={{0,14},{1,15},{2,0},{3,1},{4,2},{5,3},{6,4},{7,5},{8,6},{9,7},{10,... | collective-permute-start | bytes 811016 | tf_op jit(solution)/shard_map/ppermute | solution.py:344
  27.4 1.0 copy-done
  28.4 0.9 shard_map.97
  30.0 4.0 %shard_map.99 = (f32[4,1,1024]{2,1,0:T(1,128)S(1)}, f32[4,1,1024]{2,1,0:T(1,128)S(1)}, bf16[4,512,1024]{2,1,0:T(8,128)(2,1)S(1)}, f32[8,1,1024]{2,1,0:T(1,128)S(1)}) custom-call(s32[2]{0:T(128)S(1)} %copy-done.4, f32[4,1,1024]{2,1,0:T(1,128)S(1)} %get-tuple-element.79.refs_1_, bf16[4,128,1024]{2,1,0:T(8,128)(2,1)S(1)} %get-tuple-element.80.refs_2_, ...), custom_call_target="tpu_custom_call" | custom-call | flops 536870912 | bytes 2097152 | tf_op jit(solution)/shard_map/pallas_call | solution.py:347
  34.1 2.7 %collective-permute-start.12 = (bf16[528,256]{1,0:T(8,128)(2,1)S(1)}, bf16[528,256]{1,0:T(8,128)(2,1)S(1)}, u32[]{:S(2)}, u32[]{:S(2)}) collective-permute-start(bf16[528,256]{1,0:T(8,128)(2,1)S(1)} %collective-permute-done.10.refs_5_.refs_8_), channel_id=1, source_target_pairs={{0,14},{1,15},{2,0},{3,1},{4,2},{5,3},{6,4},{7,5},{8,6},{9,7},{10,... | collective-permute-start | bytes 811016 | tf_op jit(solution)/shard_map/ppermute | solution.py:344
  36.8 5.4 %shard_map.100 = (f32[4,1,1024]{2,1,0:T(1,128)S(1)}, f32[4,1,1024]{2,1,0:T(1,128)S(1)}, bf16[8,512,1024]{2,1,0:T(8,128)(2,1)S(1)}, f32[16,1,1024]{2,1,0:T(1,128)S(1)}) custom-call(s32[2]{0:T(128)S(1)} %copy-done.4, f32[4,1,1024]{2,1,0:T(1,128)S(1)} %get-tuple-element.79.refs_1_, bf16[4,128,1024]{2,1,0:T(8,128)(2,1)S(1)} %get-tuple-element.80.refs_2_, ...), custom_call_target="tpu_custom_call" | custom-call | flops 1073741824 | bytes 2097152 | tf_op jit(solution)/shard_map/pallas_call | solution.py:347
  42.9 2.3 %collective-permute-start.14 = (bf16[528,256]{1,0:T(8,128)(2,1)S(1)}, bf16[528,256]{1,0:T(8,128)(2,1)S(1)}, u32[]{:S(2)}, u32[]{:S(2)}) collective-permute-start(bf16[528,256]{1,0:T(8,128)(2,1)S(1)} %collective-permute-done.12.refs_5_.refs_8_), channel_id=1, source_target_pairs={{0,14},{1,15},{2,0},{3,1},{4,2},{5,3},{6,4},{7,5},{8,6},{9,7},{10,... | collective-permute-start | bytes 811016 | tf_op jit(solution)/shard_map/ppermute | solution.py:344
  45.5 1.5 %collective-permute-start.1 = (bf16[144,1024]{1,0:T(8,128)(2,1)S(1)}, bf16[144,1024]{1,0:T(8,128)(2,1)S(1)}, u32[]{:S(2)}, u32[]{:S(2)}) collective-permute-start(bf16[144,1024]{1,0:T(8,128)(2,1)S(1)} %shard_map.94.q0), channel_id=1, source_target_pairs={{0,16},{1,17},{2,18},{3,19},{4,20},{5,21},{6,22},{7,23},{8,24},{9,... | collective-permute-start | bytes 884744 | tf_op jit(solution)/shard_map/ppermute | solution.py:323
  46.9 3.1 %shard_map.101 = (f32[4,1,1024]{2,1,0:T(1,128)S(1)}, f32[4,1,1024]{2,1,0:T(1,128)S(1)}, bf16[8,512,1024]{2,1,0:T(8,128)(2,1)S(1)}, f32[16,1,1024]{2,1,0:T(1,128)S(1)}) custom-call(s32[2]{0:T(128)S(1)} %copy-done.5, f32[4,1,1024]{2,1,0:T(1,128)S(1)} %get-tuple-element.79.refs_1_, bf16[4,128,1024]{2,1,0:T(8,128)(2,1)S(1)} %get-tuple-element.80.refs_2_, ...), custom_call_target="tpu_custom_call" | custom-call | flops 1073741824 | bytes 2097152 | tf_op jit(solution)/shard_map/pallas_call | solution.py:347
  50.2 4.4 %collective-permute-start.15 = (bf16[528,256]{1,0:T(8,128)(2,1)S(1)}, bf16[528,256]{1,0:T(8,128)(2,1)S(1)}, u32[]{:S(2)}, u32[]{:S(2)}) collective-permute-start(bf16[528,256]{1,0:T(8,128)(2,1)S(1)} %collective-permute-done.14.refs_5_.refs_8_), channel_id=1, source_target_pairs={{0,14},{1,15},{2,0},{3,1},{4,2},{5,3},{6,4},{7,5},{8,6},{9,7},{10,... | collective-permute-start | bytes 811016 | tf_op jit(solution)/shard_map/ppermute | solution.py:346
  54.6 2.5 %collective-permute-start = (bf16[144,1024]{1,0:T(8,128)(2,1)S(1)}, bf16[144,1024]{1,0:T(8,128)(2,1)S(1)}, u32[]{:S(2)}, u32[]{:S(2)}) collective-permute-start(bf16[144,1024]{1,0:T(8,128)(2,1)S(1)} %shard_map.94.q0), channel_id=1, source_target_pairs={{0,1},{1,0},{2,3},{3,2},{4,5},{5,4},{6,7},{7,6},{8,9},{9,8},{10,11... | collective-permute-start | bytes 884744 | tf_op jit(solution)/shard_map/ppermute | solution.py:324
  57.1 3.1 %shard_map.102 = (f32[4,1,1024]{2,1,0:T(1,128)S(1)}, f32[4,1,1024]{2,1,0:T(1,128)S(1)}, bf16[8,512,1024]{2,1,0:T(8,128)(2,1)S(1)}, f32[16,1,1024]{2,1,0:T(1,128)S(1)}) custom-call(s32[2]{0:T(128)S(1)} %copy-done.5, f32[4,1,1024]{2,1,0:T(1,128)S(1)} %get-tuple-element.79.refs_1_, bf16[4,128,1024]{2,1,0:T(8,128)(2,1)S(1)} %get-tuple-element.80.refs_2_, ...), custom_call_target="tpu_custom_call" | custom-call | flops 1073741824 | bytes 2097152 | tf_op jit(solution)/shard_map/pallas_call | solution.py:347
  60.2 1.8 %shard_map.103 = (f32[4,1,1024]{2,1,0:T(1,128)S(1)}, f32[4,1,1024]{2,1,0:T(1,128)S(1)}, bf16[4,512,1024]{2,1,0:T(8,128)(2,1)S(1)}, f32[8,1,1024]{2,1,0:T(1,128)S(1)}) custom-call(s32[2]{0:T(128)S(1)} %copy-done.5, f32[4,1,1024]{2,1,0:T(1,128)S(1)} %get-tuple-element.79.refs_1_, bf16[4,128,1024]{2,1,0:T(8,128)(2,1)S(1)} %get-tuple-element.80.refs_2_, ...), custom_call_target="tpu_custom_call" | custom-call | flops 536870912 | bytes 2097152 | tf_op jit(solution)/shard_map/pallas_call | solution.py:347
  62.7 0.9 shard_map.95
  63.6 2.3 %collective-permute-start.18 = (f32[8,1,1024]{2,1,0:T(1,128)S(1)}, f32[8,1,1024]{2,1,0:T(1,128)S(1)}, u32[]{:S(2)}, u32[]{:S(2)}) collective-permute-start(f32[8,1,1024]{2,1,0:T(1,128)S(1)} %constant_dynamic-update-slice_fusion), channel_id=1, source_target_pairs={{0,17},{1,16},{2,19},{3,18},{4,21},{5,20},{6,23},{7,22},{8,25},{9,... | collective-permute-start | bytes 98312 | tf_op jit(solution)/shard_map/ppermute | solution.py:365
  65.9 2.2 %collective-permute-done.18 = f32[8,1,1024]{2,1,0:T(1,128)S(1)} collective-permute-done((f32[8,1,1024]{2,1,0:T(1,128)S(1)}, f32[8,1,1024]{2,1,0:T(1,128)S(1)}, u32[]{:S(2)}, u32[]{:S(2)}) %collective-permute-start.18) | collective-permute-done | bytes 32800 | tf_op jit(solution)/shard_map/ppermute | solution.py:365
  68.3 2.5 %shard_map.104 = (f32[4,128,1024]{2,1,0:T(8,128)S(1)}, f32[1,512,256]{2,1,0:T(8,128)S(1)}) custom-call(s32[2]{0:T(128)S(1)} %copy-done.5, f32[4,1,1024]{2,1,0:T(1,128)S(1)} %get-tuple-element.77.refs_1_, f32[4,1,1024]{2,1,0:T(1,128)S(1)} %multiply_add_fusion.refs_2_, bf16[4,1024,128]{2,1,0:T(8,128)(2,1)S(1)} %get-tuple-element.110.refs_3_, ...), custom_call_target="tpu_custom_call" | custom-call | flops 2684354560 | bytes 8388608 | tf_op jit(solution)/shard_map/pallas_call | solution.py:383
  71.0 4.0 %shard_map.105 = (f32[4,128,1024]{2,1,0:T(8,128)S(1)}, f32[2,512,256]{2,1,0:T(8,128)S(1)}) custom-call(s32[2]{0:T(128)S(1)} %copy-done.5, f32[4,1,1024]{2,1,0:T(1,128)S(1)} %get-tuple-element.77.refs_1_, f32[4,1,1024]{2,1,0:T(1,128)S(1)} %multiply_add_fusion.refs_2_, ...), custom_call_target="tpu_custom_call", output_to_operand_aliasing={{0}: (10, {})} | custom-call | flops 5368709120 | bytes 8388608 | tf_op jit(solution)/shard_map/pallas_call | solution.py:383
  75.0 9.4 %collective-permute-done.19 = bf16[512,256]{1,0:T(8,128)(2,1)S(1)} collective-permute-done((bf16[512,256]{1,0:T(8,128)(2,1)S(1)}, bf16[512,256]{1,0:T(8,128)(2,1)S(1)}, u32[]{:S(2)}, u32[]{:S(2)}) %collective-permute-start.19) | collective-permute-done | bytes 262176 | tf_op jit(solution)/shard_map/ppermute | solution.py:399
  84.5 2.4 %collective-permute-start.21 = (bf16[512,256]{1,0:T(8,128)(2,1)S(1)}, bf16[512,256]{1,0:T(8,128)(2,1)S(1)}, u32[]{:S(2)}, u32[]{:S(2)}) collective-permute-start(bf16[512,256]{1,0:T(8,128)(2,1)S(1)} %fusion.8), channel_id=1, source_target_pairs={{0,14},{1,15},{2,0},{3,1},{4,2},{5,3},{6,4},{7,5},{8,6},{9,7},{10,... | collective-permute-start | bytes 786440 | tf_op jit(solution)/shard_map/ppermute | solution.py:401
  86.9 4.0 %shard_map.106 = (f32[4,128,1024]{2,1,0:T(8,128)S(1)}, f32[2,512,256]{2,1,0:T(8,128)S(1)}) custom-call(s32[2]{0:T(128)S(1)} %copy-done.5, f32[4,1,1024]{2,1,0:T(1,128)S(1)} %get-tuple-element.77.refs_1_, f32[4,1,1024]{2,1,0:T(1,128)S(1)} %multiply_add_fusion.refs_2_, ...), custom_call_target="tpu_custom_call", output_to_operand_aliasing={{0}: (10, {})} | custom-call | flops 5368709120 | bytes 8388608 | tf_op jit(solution)/shard_map/pallas_call | solution.py:383
  90.9 1.2 collective-permute-done.21
  92.1 3.1 %collective-permute-done.20 = bf16[512,256]{1,0:T(8,128)(2,1)S(1)} collective-permute-done((bf16[512,256]{1,0:T(8,128)(2,1)S(1)}, bf16[512,256]{1,0:T(8,128)(2,1)S(1)}, u32[]{:S(2)}, u32[]{:S(2)}) %collective-permute-start.20) | collective-permute-done | bytes 262176 | tf_op jit(solution)/shard_map/ppermute | solution.py:399
  95.4 3.0 %collective-permute-start.23 = (bf16[512,256]{1,0:T(8,128)(2,1)S(1)}, bf16[512,256]{1,0:T(8,128)(2,1)S(1)}, u32[]{:S(2)}, u32[]{:S(2)}) collective-permute-start(bf16[512,256]{1,0:T(8,128)(2,1)S(1)} %get-tuple-element.138), channel_id=1, source_target_pairs={{0,14},{1,15},{2,0},{3,1},{4,2},{5,3},{6,4},{7,5},{8,6},{9,7},{10,... | collective-permute-start | bytes 786440 | tf_op jit(solution)/shard_map/ppermute | solution.py:401
  98.4 6.7 %shard_map.107 = (f32[4,128,1024]{2,1,0:T(8,128)S(1)}, f32[2,512,256]{2,1,0:T(8,128)S(1)}) custom-call(s32[2]{0:T(128)S(1)} %copy-done.5, f32[4,1,1024]{2,1,0:T(1,128)S(1)} %get-tuple-element.77.refs_1_, f32[4,1,1024]{2,1,0:T(1,128)S(1)} %multiply_add_fusion.refs_2_, ...), custom_call_target="tpu_custom_call", output_to_operand_aliasing={{0}: (10, {})} | custom-call | flops 5368709120 | bytes 8388608 | tf_op jit(solution)/shard_map/pallas_call | solution.py:383
  105.1 1.1 collective-permute-done.22
  106.4 4.3 %shard_map.108 = (bf16[128,1024]{1,0:T(8,128)(2,1)S(1)}, bf16[128,1024]{1,0:T(8,128)(2,1)S(1)}, f32[1,512,256]{2,1,0:T(8,128)S(1)}) custom-call(s32[2]{0:T(128)S(1)} %copy-done.5, f32[4,1,1024]{2,1,0:T(1,128)S(1)} %get-tuple-element.77.refs_1_, f32[4,1,1024]{2,1,0:T(1,128)S(1)} %multiply_add_fusion.refs_2_, ...), custom_call_target="tpu_custom_call" | custom-call | flops 2684354560 | bytes 8388608 | tf_op jit(solution)/shard_map/pallas_call | solution.py:383
  110.7 2.2 %collective-permute-start.30 = (bf16[128,1024]{1,0:T(8,128)(2,1)S(1)}, bf16[128,1024]{1,0:T(8,128)(2,1)S(1)}, u32[]{:S(2)}, u32[]{:S(2)}) collective-permute-start(bf16[128,1024]{1,0:T(8,128)(2,1)S(1)} %get-tuple-element.147), channel_id=1, source_target_pairs={{0,1},{1,0},{2,3},{3,2},{4,5},{5,4},{6,7},{7,6},{8,9},{9,8},{10,11... | collective-permute-start | bytes 786440 | tf_op jit(solution)/shard_map/ppermute | solution.py:403
  112.9 4.2 %collective-permute-start.25 = (bf16[512,256]{1,0:T(8,128)(2,1)S(1)}, bf16[512,256]{1,0:T(8,128)(2,1)S(1)}, u32[]{:S(2)}, u32[]{:S(2)}) collective-permute-start(bf16[512,256]{1,0:T(8,128)(2,1)S(1)} %get-tuple-element.143), channel_id=1, source_target_pairs={{0,14},{1,15},{2,0},{3,1},{4,2},{5,3},{6,4},{7,5},{8,6},{9,7},{10,... | collective-permute-start | bytes 786440 | tf_op jit(solution)/shard_map/ppermute | solution.py:401
  117.1 3.0 %shard_map.109 = (bf16[128,1024]{1,0:T(8,128)(2,1)S(1)}, bf16[128,1024]{1,0:T(8,128)(2,1)S(1)}, f32[1,512,256]{2,1,0:T(8,128)S(1)}) custom-call(s32[2]{0:T(128)S(1)} %copy-done.5, f32[4,1,1024]{2,1,0:T(1,128)S(1)} %get-tuple-element.77.refs_1_, f32[4,1,1024]{2,1,0:T(1,128)S(1)} %multiply_add_fusion.refs_2_, ...), custom_call_target="tpu_custom_call" | custom-call | flops 2684354560 | bytes 8388608 | tf_op jit(solution)/shard_map/pallas_call | solution.py:383
  120.6 0.8 collective-permute-start.31
  121.5 1.2 collective-permute-done.25
  122.7 3.1 %collective-permute-done.24 = bf16[512,256]{1,0:T(8,128)(2,1)S(1)} collective-permute-done((bf16[512,256]{1,0:T(8,128)(2,1)S(1)}, bf16[512,256]{1,0:T(8,128)(2,1)S(1)}, u32[]{:S(2)}, u32[]{:S(2)}) %collective-permute-start.24) | collective-permute-done | bytes 262176 | tf_op jit(solution)/shard_map/ppermute | solution.py:399
  126.0 1.3 collective-permute-start.26
  127.3 1.7 %collective-permute-start.28 = (bf16[128,256]{1,0:T(8,128)(2,1)S(1)}, bf16[128,256]{1,0:T(8,128)(2,1)S(1)}, u32[]{:S(2)}, u32[]{:S(2)}) collective-permute-start(bf16[128,256]{1,0:T(8,128)(2,1)S(1)} %get-tuple-element.155), channel_id=1, source_target_pairs={{0,17},{1,16},{2,19},{3,18},{4,21},{5,20},{6,23},{7,22},{8,25},{9,... | collective-permute-start | bytes 196616 | tf_op jit(solution)/shard_map/ppermute | solution.py:411
  129.0 1.8 %collective-permute-done.27.a2 = bf16[128,256]{1,0:T(8,128)(2,1)S(1)} collective-permute-done((bf16[128,256]{1,0:T(8,128)(2,1)S(1)}, bf16[128,256]{1,0:T(8,128)(2,1)S(1)}, u32[]{:S(2)}, u32[]{:S(2)}) %collective-permute-start.27) | collective-permute-done | bytes 65568 | tf_op jit(solution)/shard_map/ppermute | solution.py:411
  130.8 1.7 %collective-permute-done.28.a3 = bf16[128,256]{1,0:T(8,128)(2,1)S(1)} collective-permute-done((bf16[128,256]{1,0:T(8,128)(2,1)S(1)}, bf16[128,256]{1,0:T(8,128)(2,1)S(1)}, u32[]{:S(2)}, u32[]{:S(2)}) %collective-permute-start.28) | collective-permute-done | bytes 65568 | tf_op jit(solution)/shard_map/ppermute | solution.py:411
  132.5 1.4 %shard_map.110 = (bf16[128,1024]{1,0:T(8,128)(2,1)}, bf16[512,128]{1,0:T(8,128)(2,1)}, bf16[512,128]{1,0:T(8,128)(2,1)}) custom-call(s32[2]{0:T(128)S(1)} %copy-done.5, bf16[128,256]{1,0:T(8,128)(2,1)S(1)} %get-tuple-element.158.a0, bf16[128,256]{1,0:T(8,128)(2,1)S(1)} %collective-permute-done.26.a1, bf16[128,256]{1,0:T(8,128)(2,1)S(1)} %collective-permute-done.27.a2, ...), custom_call_target="tpu_custom_call" | custom-call | bytes 2097152 | tf_op jit(solution)/shard_map/pallas_call | solution.py:412
  (63 shorter events, 5.4 us)
Async XLA Ops:
  0.6 44.6 %copy-start.1 = (bf16[1,128,1024]{2,1,0:T(8,128)(2,1)S(1)}, bf16[1,128,1024]{2,1,0:T(8,128)(2,1)}, u32[]{:S(2)}) copy-start(bf16[1,128,1024]{2,1,0:T(8,128)(2,1)} %param.10) | copy-start | bytes 786436
  0.6 44.6 %copy-start.2 = (bf16[1,128,1024]{2,1,0:T(8,128)(2,1)S(1)}, bf16[1,128,1024]{2,1,0:T(8,128)(2,1)}, u32[]{:S(2)}) copy-start(bf16[1,128,1024]{2,1,0:T(8,128)(2,1)} %param.11) | copy-start | bytes 786436
  4.0 8.1 %collective-permute-start.4 = (bf16[144,1024]{1,0:T(8,128)(2,1)}, bf16[144,1024]{1,0:T(8,128)(2,1)S(1)}, u32[]{:S(2)}, u32[]{:S(2)}) collective-permute-start(bf16[144,1024]{1,0:T(8,128)(2,1)} %get-tuple-element.78.q0), channel_id=1, source_target_pairs={{0,16},{1,17},{2,18},{3,19},{4,20},{5,21},{6,22},{7,23},{8,24},{9,... | collective-permute-start | bytes 884744 | tf_op jit(solution)/shard_map/ppermute | solution.py:323
  6.2 21.3 %collective-permute-start.3 = (bf16[144,1024]{1,0:T(8,128)(2,1)}, bf16[144,1024]{1,0:T(8,128)(2,1)S(1)}, u32[]{:S(2)}, u32[]{:S(2)}) collective-permute-start(bf16[144,1024]{1,0:T(8,128)(2,1)} %get-tuple-element.78.q0), channel_id=1, source_target_pairs={{0,1},{1,0},{2,3},{3,2},{4,5},{5,4},{6,7},{7,6},{8,9},{9,8},{10,11... | collective-permute-start | bytes 884744 | tf_op jit(solution)/shard_map/ppermute | solution.py:324
  12.0 15.4 %collective-permute-start.5 = (bf16[144,1024]{1,0:T(8,128)(2,1)S(1)}, bf16[144,1024]{1,0:T(8,128)(2,1)S(1)}, u32[]{:S(2)}, u32[]{:S(2)}) collective-permute-start(bf16[144,1024]{1,0:T(8,128)(2,1)S(1)} %collective-permute-done.4.q2), channel_id=1, source_target_pairs={{0,1},{1,0},{2,3},{3,2},{4,5},{5,4},{6,7},{7,6},{8,9},{9,8},{10,11... | collective-permute-start | bytes 884744 | tf_op jit(solution)/shard_map/ppermute | solution.py:324
  14.3 2.1 %collective-permute-start.6 = (bf16[144,256]{1,0:T(8,128)(2,1)}, bf16[144,256]{1,0:T(8,128)(2,1)S(1)}, u32[]{:S(2)}, u32[]{:S(2)}) collective-permute-start(bf16[144,256]{1,0:T(8,128)(2,1)} %get-tuple-element.82), channel_id=1, source_target_pairs={{0,1},{1,0},{2,3},{3,2},{4,5},{5,4},{6,7},{7,6},{8,9},{9,8},{10,11... | collective-permute-start | bytes 221192 | tf_op jit(solution)/shard_map/ppermute | solution.py:319
  14.3 3.4 %collective-permute-start.7 = (bf16[144,256]{1,0:T(8,128)(2,1)}, bf16[144,256]{1,0:T(8,128)(2,1)S(1)}, u32[]{:S(2)}, u32[]{:S(2)}) collective-permute-start(bf16[144,256]{1,0:T(8,128)(2,1)} %get-tuple-element.83), channel_id=1, source_target_pairs={{0,16},{1,17},{2,18},{3,19},{4,20},{5,21},{6,22},{7,23},{8,24},{9,... | collective-permute-start | bytes 221192 | tf_op jit(solution)/shard_map/ppermute | solution.py:319
  15.8 5.0 %collective-permute-start.8 = (bf16[144,256]{1,0:T(8,128)(2,1)}, bf16[144,256]{1,0:T(8,128)(2,1)S(1)}, u32[]{:S(2)}, u32[]{:S(2)}) collective-permute-start(bf16[144,256]{1,0:T(8,128)(2,1)} %get-tuple-element.84), channel_id=1, source_target_pairs={{0,17},{1,16},{2,19},{3,18},{4,21},{5,20},{6,23},{7,22},{8,25},{9,... | collective-permute-start | bytes 221192 | tf_op jit(solution)/shard_map/ppermute | solution.py:319
  20.8 0.9 copy-start.3
  21.7 25.3 %copy-start.5 = (s32[2]{0:T(128)S(1)}, s32[2]{0:T(128)}, u32[]{:S(2)}) copy-start(s32[2]{0:T(128)} %pad_add_fusion.tab.refs_0_) | copy-start | bytes 28
  21.7 12.3 %collective-permute-start.9 = (bf16[528,256]{1,0:T(8,128)(2,1)S(1)}, bf16[528,256]{1,0:T(8,128)(2,1)S(1)}, u32[]{:S(2)}, u32[]{:S(2)}) collective-permute-start(bf16[528,256]{1,0:T(8,128)(2,1)S(1)} %shard_map.98.refs_5_.refs_8_), channel_id=1, source_target_pairs={{0,2},{1,3},{2,4},{3,5},{4,6},{5,7},{6,8},{7,9},{8,10},{9,11},{10,... | collective-permute-start | bytes 811016 | tf_op jit(solution)/shard_map/ppermute | solution.py:344
  23.4 10.6 %collective-permute-start.10 = (bf16[528,256]{1,0:T(8,128)(2,1)S(1)}, bf16[528,256]{1,0:T(8,128)(2,1)S(1)}, u32[]{:S(2)}, u32[]{:S(2)}) collective-permute-start(bf16[528,256]{1,0:T(8,128)(2,1)S(1)} %shard_map.98.refs_5_.refs_8_), channel_id=1, source_target_pairs={{0,14},{1,15},{2,0},{3,1},{4,2},{5,3},{6,4},{7,5},{8,6},{9,7},{10,... | collective-permute-start | bytes 811016 | tf_op jit(solution)/shard_map/ppermute | solution.py:344
  27.4 1.0 copy-start
  29.3 0.7 copy-start.4
  34.0 8.6 %collective-permute-start.11 = (bf16[528,256]{1,0:T(8,128)(2,1)S(1)}, bf16[528,256]{1,0:T(8,128)(2,1)S(1)}, u32[]{:S(2)}, u32[]{:S(2)}) collective-permute-start(bf16[528,256]{1,0:T(8,128)(2,1)S(1)} %collective-permute-done.9.refs_6_.refs_9_), channel_id=1, source_target_pairs={{0,2},{1,3},{2,4},{3,5},{4,6},{5,7},{6,8},{7,9},{8,10},{9,11},{10,... | collective-permute-start | bytes 811016 | tf_op jit(solution)/shard_map/ppermute | solution.py:344
  34.1 8.5 %collective-permute-start.12 = (bf16[528,256]{1,0:T(8,128)(2,1)S(1)}, bf16[528,256]{1,0:T(8,128)(2,1)S(1)}, u32[]{:S(2)}, u32[]{:S(2)}) collective-permute-start(bf16[528,256]{1,0:T(8,128)(2,1)S(1)} %collective-permute-done.10.refs_5_.refs_8_), channel_id=1, source_target_pairs={{0,14},{1,15},{2,0},{3,1},{4,2},{5,3},{6,4},{7,5},{8,6},{9,7},{10,... | collective-permute-start | bytes 811016 | tf_op jit(solution)/shard_map/ppermute | solution.py:344
  42.6 7.6 %collective-permute-start.13 = (bf16[528,256]{1,0:T(8,128)(2,1)S(1)}, bf16[528,256]{1,0:T(8,128)(2,1)S(1)}, u32[]{:S(2)}, u32[]{:S(2)}) collective-permute-start(bf16[528,256]{1,0:T(8,128)(2,1)S(1)} %collective-permute-done.11.refs_6_.refs_9_), channel_id=1, source_target_pairs={{0,2},{1,3},{2,4},{3,5},{4,6},{5,7},{6,8},{7,9},{8,10},{9,11},{10,... | collective-permute-start | bytes 811016 | tf_op jit(solution)/shard_map/ppermute | solution.py:344
  42.9 7.2 %collective-permute-start.14 = (bf16[528,256]{1,0:T(8,128)(2,1)S(1)}, bf16[528,256]{1,0:T(8,128)(2,1)S(1)}, u32[]{:S(2)}, u32[]{:S(2)}) collective-permute-start(bf16[528,256]{1,0:T(8,128)(2,1)S(1)} %collective-permute-done.12.refs_5_.refs_8_), channel_id=1, source_target_pairs={{0,14},{1,15},{2,0},{3,1},{4,2},{5,3},{6,4},{7,5},{8,6},{9,7},{10,... | collective-permute-start | bytes 811016 | tf_op jit(solution)/shard_map/ppermute | solution.py:344
  45.5 11.7 %collective-permute-start.1 = (bf16[144,1024]{1,0:T(8,128)(2,1)S(1)}, bf16[144,1024]{1,0:T(8,128)(2,1)S(1)}, u32[]{:S(2)}, u32[]{:S(2)}) collective-permute-start(bf16[144,1024]{1,0:T(8,128)(2,1)S(1)} %shard_map.94.q0), channel_id=1, source_target_pairs={{0,16},{1,17},{2,18},{3,19},{4,20},{5,21},{6,22},{7,23},{8,24},{9,... | collective-permute-start | bytes 884744 | tf_op jit(solution)/shard_map/ppermute | solution.py:323
  50.2 10.0 %collective-permute-start.15 = (bf16[528,256]{1,0:T(8,128)(2,1)S(1)}, bf16[528,256]{1,0:T(8,128)(2,1)S(1)}, u32[]{:S(2)}, u32[]{:S(2)}) collective-permute-start(bf16[528,256]{1,0:T(8,128)(2,1)S(1)} %collective-permute-done.14.refs_5_.refs_8_), channel_id=1, source_target_pairs={{0,14},{1,15},{2,0},{3,1},{4,2},{5,3},{6,4},{7,5},{8,6},{9,7},{10,... | collective-permute-start | bytes 811016 | tf_op jit(solution)/shard_map/ppermute | solution.py:346
  54.6 8.1 %collective-permute-start = (bf16[144,1024]{1,0:T(8,128)(2,1)S(1)}, bf16[144,1024]{1,0:T(8,128)(2,1)S(1)}, u32[]{:S(2)}, u32[]{:S(2)}) collective-permute-start(bf16[144,1024]{1,0:T(8,128)(2,1)S(1)} %shard_map.94.q0), channel_id=1, source_target_pairs={{0,1},{1,0},{2,3},{3,2},{4,5},{5,4},{6,7},{7,6},{8,9},{9,8},{10,11... | collective-permute-start | bytes 884744 | tf_op jit(solution)/shard_map/ppermute | solution.py:324
  57.1 5.5 %collective-permute-start.2 = (bf16[144,1024]{1,0:T(8,128)(2,1)S(1)}, bf16[144,1024]{1,0:T(8,128)(2,1)S(1)}, u32[]{:S(2)}, u32[]{:S(2)}) collective-permute-start(bf16[144,1024]{1,0:T(8,128)(2,1)S(1)} %collective-permute-done.1.q2), channel_id=1, source_target_pairs={{0,1},{1,0},{2,3},{3,2},{4,5},{5,4},{6,7},{7,6},{8,9},{9,8},{10,11... | collective-permute-start | bytes 884744 | tf_op jit(solution)/shard_map/ppermute | solution.py:324
  62.1 3.8 %collective-permute-start.17 = (f32[8,1,1024]{2,1,0:T(1,128)S(1)}, f32[8,1,1024]{2,1,0:T(1,128)S(1)}, u32[]{:S(2)}, u32[]{:S(2)}) collective-permute-start(f32[8,1,1024]{2,1,0:T(1,128)S(1)} %constant_dynamic-update-slice_fusion), channel_id=1, source_target_pairs={{0,16},{1,17},{2,18},{3,19},{4,20},{5,21},{6,22},{7,23},{8,24},{9,... | collective-permute-start | bytes 98312 | tf_op jit(solution)/shard_map/ppermute | solution.py:365
  63.6 4.5 %collective-permute-start.18 = (f32[8,1,1024]{2,1,0:T(1,128)S(1)}, f32[8,1,1024]{2,1,0:T(1,128)S(1)}, u32[]{:S(2)}, u32[]{:S(2)}) collective-permute-start(f32[8,1,1024]{2,1,0:T(1,128)S(1)} %constant_dynamic-update-slice_fusion), channel_id=1, source_target_pairs={{0,17},{1,16},{2,19},{3,18},{4,21},{5,20},{6,23},{7,22},{8,25},{9,... | collective-permute-start | bytes 98312 | tf_op jit(solution)/shard_map/ppermute | solution.py:365
  65.9 2.2 %collective-permute-start.16 = (f32[8,1,1024]{2,1,0:T(1,128)S(1)}, f32[8,1,1024]{2,1,0:T(1,128)S(1)}, u32[]{:S(2)}, u32[]{:S(2)}) collective-permute-start(f32[8,1,1024]{2,1,0:T(1,128)S(1)} %constant_dynamic-update-slice_fusion), channel_id=1, source_target_pairs={{0,1},{1,0},{2,3},{3,2},{4,5},{5,4},{6,7},{7,6},{8,9},{9,8},{10,11... | collective-permute-start | bytes 98312 | tf_op jit(solution)/shard_map/ppermute | solution.py:365
  70.9 13.5 %collective-permute-start.19 = (bf16[512,256]{1,0:T(8,128)(2,1)S(1)}, bf16[512,256]{1,0:T(8,128)(2,1)S(1)}, u32[]{:S(2)}, u32[]{:S(2)}) collective-permute-start(bf16[512,256]{1,0:T(8,128)(2,1)S(1)} %convert_bitcast_fusion), channel_id=1, source_target_pairs={{0,2},{1,3},{2,4},{3,5},{4,6},{5,7},{6,8},{7,9},{8,10},{9,11},{10,... | collective-permute-start | bytes 786440 | tf_op jit(solution)/shard_map/ppermute | solution.py:399
  84.5 7.6 %collective-permute-start.21 = (bf16[512,256]{1,0:T(8,128)(2,1)S(1)}, bf16[512,256]{1,0:T(8,128)(2,1)S(1)}, u32[]{:S(2)}, u32[]{:S(2)}) collective-permute-start(bf16[512,256]{1,0:T(8,128)(2,1)S(1)} %fusion.8), channel_id=1, source_target_pairs={{0,14},{1,15},{2,0},{3,1},{4,2},{5,3},{6,4},{7,5},{8,6},{9,7},{10,... | collective-permute-start | bytes 786440 | tf_op jit(solution)/shard_map/ppermute | solution.py:401
  86.9 8.4 %collective-permute-start.20 = (bf16[512,256]{1,0:T(8,128)(2,1)S(1)}, bf16[512,256]{1,0:T(8,128)(2,1)S(1)}, u32[]{:S(2)}, u32[]{:S(2)}) collective-permute-start(bf16[512,256]{1,0:T(8,128)(2,1)S(1)} %fusion.7), channel_id=1, source_target_pairs={{0,2},{1,3},{2,4},{3,5},{4,6},{5,7},{6,8},{7,9},{8,10},{9,11},{10,... | collective-permute-start | bytes 786440 | tf_op jit(solution)/shard_map/ppermute | solution.py:399
  95.4 9.7 %collective-permute-start.23 = (bf16[512,256]{1,0:T(8,128)(2,1)S(1)}, bf16[512,256]{1,0:T(8,128)(2,1)S(1)}, u32[]{:S(2)}, u32[]{:S(2)}) collective-permute-start(bf16[512,256]{1,0:T(8,128)(2,1)S(1)} %get-tuple-element.138), channel_id=1, source_target_pairs={{0,14},{1,15},{2,0},{3,1},{4,2},{5,3},{6,4},{7,5},{8,6},{9,7},{10,... | collective-permute-start | bytes 786440 | tf_op jit(solution)/shard_map/ppermute | solution.py:401
  98.4 7.8 %collective-permute-start.22 = (bf16[512,256]{1,0:T(8,128)(2,1)S(1)}, bf16[512,256]{1,0:T(8,128)(2,1)S(1)}, u32[]{:S(2)}, u32[]{:S(2)}) collective-permute-start(bf16[512,256]{1,0:T(8,128)(2,1)S(1)} %get-tuple-element.137), channel_id=1, source_target_pairs={{0,2},{1,3},{2,4},{3,5},{4,6},{5,7},{6,8},{7,9},{8,10},{9,11},{10,... | collective-permute-start | bytes 786440 | tf_op jit(solution)/shard_map/ppermute | solution.py:399
  110.7 9.9 %collective-permute-start.30 = (bf16[128,1024]{1,0:T(8,128)(2,1)S(1)}, bf16[128,1024]{1,0:T(8,128)(2,1)S(1)}, u32[]{:S(2)}, u32[]{:S(2)}) collective-permute-start(bf16[128,1024]{1,0:T(8,128)(2,1)S(1)} %get-tuple-element.147), channel_id=1, source_target_pairs={{0,1},{1,0},{2,3},{3,2},{4,5},{5,4},{6,7},{7,6},{8,9},{9,8},{10,11... | collective-permute-start | bytes 786440 | tf_op jit(solution)/shard_map/ppermute | solution.py:403
  112.9 9.8 %collective-permute-start.25 = (bf16[512,256]{1,0:T(8,128)(2,1)S(1)}, bf16[512,256]{1,0:T(8,128)(2,1)S(1)}, u32[]{:S(2)}, u32[]{:S(2)}) collective-permute-start(bf16[512,256]{1,0:T(8,128)(2,1)S(1)} %get-tuple-element.143), channel_id=1, source_target_pairs={{0,14},{1,15},{2,0},{3,1},{4,2},{5,3},{6,4},{7,5},{8,6},{9,7},{10,... | collective-permute-start | bytes 786440 | tf_op jit(solution)/shard_map/ppermute | solution.py:401
  117.1 8.7 %collective-permute-start.24 = (bf16[512,256]{1,0:T(8,128)(2,1)S(1)}, bf16[512,256]{1,0:T(8,128)(2,1)S(1)}, u32[]{:S(2)}, u32[]{:S(2)}) collective-permute-start(bf16[512,256]{1,0:T(8,128)(2,1)S(1)} %get-tuple-element.142), channel_id=1, source_target_pairs={{0,2},{1,3},{2,4},{3,5},{4,6},{5,7},{6,8},{7,9},{8,10},{9,11},{10,... | collective-permute-start | bytes 786440 | tf_op jit(solution)/shard_map/ppermute | solution.py:399
  120.1 8.9 %collective-permute-start.29 = (bf16[128,1024]{1,0:T(8,128)(2,1)S(1)}, bf16[128,1024]{1,0:T(8,128)(2,1)S(1)}, u32[]{:S(2)}, u32[]{:S(2)}) collective-permute-start(bf16[128,1024]{1,0:T(8,128)(2,1)S(1)} %get-tuple-element.145), channel_id=1, source_target_pairs={{0,1},{1,0},{2,3},{3,2},{4,5},{5,4},{6,7},{7,6},{8,9},{9,8},{10,11... | collective-permute-start | bytes 786440 | tf_op jit(solution)/shard_map/ppermute | solution.py:410
  120.6 11.9 %collective-permute-start.31 = (bf16[128,1024]{1,0:T(8,128)(2,1)S(1)}, bf16[128,1024]{1,0:T(8,128)(2,1)S(1)}, u32[]{:S(2)}, u32[]{:S(2)}) collective-permute-start(bf16[128,1024]{1,0:T(8,128)(2,1)S(1)} %add_convert_fusion), channel_id=1, source_target_pairs={{0,16},{1,17},{2,18},{3,19},{4,20},{5,21},{6,22},{7,23},{8,24},{9,... | collective-permute-start | bytes 786440 | tf_op jit(solution)/shard_map/ppermute | solution.py:405
  126.0 3.1 %collective-permute-start.26 = (bf16[128,256]{1,0:T(8,128)(2,1)S(1)}, bf16[128,256]{1,0:T(8,128)(2,1)S(1)}, u32[]{:S(2)}, u32[]{:S(2)}) collective-permute-start(bf16[128,256]{1,0:T(8,128)(2,1)S(1)} %get-tuple-element.157), channel_id=1, source_target_pairs={{0,1},{1,0},{2,3},{3,2},{4,5},{5,4},{6,7},{7,6},{8,9},{9,8},{10,11... | collective-permute-start | bytes 196616 | tf_op jit(solution)/shard_map/ppermute | solution.py:411
  127.3 3.5 %collective-permute-start.27 = (bf16[128,256]{1,0:T(8,128)(2,1)S(1)}, bf16[128,256]{1,0:T(8,128)(2,1)S(1)}, u32[]{:S(2)}, u32[]{:S(2)}) collective-permute-start(bf16[128,256]{1,0:T(8,128)(2,1)S(1)} %get-tuple-element.156), channel_id=1, source_target_pairs={{0,16},{1,17},{2,18},{3,19},{4,20},{5,21},{6,22},{7,23},{8,24},{9,... | collective-permute-start | bytes 196616 | tf_op jit(solution)/shard_map/ppermute | solution.py:411
  127.3 5.2 %collective-permute-start.28 = (bf16[128,256]{1,0:T(8,128)(2,1)S(1)}, bf16[128,256]{1,0:T(8,128)(2,1)S(1)}, u32[]{:S(2)}, u32[]{:S(2)}) collective-permute-start(bf16[128,256]{1,0:T(8,128)(2,1)S(1)} %get-tuple-element.155), channel_id=1, source_target_pairs={{0,17},{1,16},{2,19},{3,18},{4,21},{5,20},{6,23},{7,22},{8,25},{9,... | collective-permute-start | bytes 196616 | tf_op jit(solution)/shard_map/ppermute | solution.py:411
where the time goes:
time: 134 us
  Pallas kernels  47.9 us (36%)
  starting transfers between devices  46.6 us (35%)
  waiting for transfers between devices  34.4 us (26%)
  local copies, waits for them, and re-layouts  2.61 us (2%)
  other arithmetic  1.49 us (1%)
    pallas_call x6, Pallas kernels, grads(): call(functools.partial(grads_body, ks, rhos, first, last), ([piece, piece...  24.5 us
    pallas_call x5, Pallas kernels, per_device(): call(functools.partial(stats_body, ks), [stat, stat, shape((4 * n, NK, NQ...  17.3 us
    ppermute x4, waiting for transfers between devices, per_device(): up = hop(sends[0], perm=turn(1))  16.8 us
    ppermute x6, starting transfers between devices, per_device(): fwd, bwd = (hop(fwd, perm=turn(1)), hop(bwd, perm=turn(-1)))  11.2 us
    ppermute x3, starting transfers between devices, per_device(): down = hop(sends[1], perm=turn(-1))  9.6 us
    ppermute x4, starting transfers between devices, four(): return (x, hop(x, perm=flip(1)), other, hop(other, perm=flip(1)))  6.01 us
    ppermute x2, waiting for transfers between devices, four(): other = hop(x, perm=flip(2))  4.69 us
    ppermute x1, starting transfers between devices, per_device(): bwd = hop(bwd, perm=turn(-1))  4.42 us
  transfers between devices with their start and end apart: 32, of which 14 were waited for; matrix products, arithmetic and copies ran while one was open for 0% of the time, Pallas kernels for 28%

commit v1 on v0

--- a/solution.py
+++ b/solution.py
@@ -209,21 +209,25 @@
     n_sets = len(ks)
     tab, tag_ref, wide_ref = refs[:3]
     kvs = refs[5 : 5 + n_sets]
-    m_ref, l_ref, e_ref, t_ref, kv = refs[5 + n_sets :]
+    m_ref, l_ref, e_ref, t_ref, kv, sum_ref, top_ref = refs[5 + n_sets :]
     m_ref[...] = refs[3][...]
     l_ref[...] = refs[4][...]
     take_sets(kv, kvs)
 
-    def body(n, rho, half, size, kind, masked):
+    def inputs(n, rho, half, size, kind, masked):
         rows = pl.ds(pl.multiple_of(half * 256, 256), size)
-        keys = kv[n, rows, 0:HD]
-        if masked:
-            vis = visible_of(kv, n, half, *kind[:3], tag_ref[rho, :, 0:128])
+        vis = visible_of(kv, n, half, *kind[:3], tag_ref[rho, :, 0:128]) if masked else None
+        return rows, kv[n, rows, 0:HD], vis
+
+    def scores(keys, rho, cols, vis):
+        s = dot_nn(keys, wide_ref[rho, :, cols])
+        return s if vis is None else jnp.where(vis, s, NEG)
+
+    def first_body(n, rho, half, size, kind, masked):
+        rows, keys, vis = inputs(n, rho, half, size, kind, masked)
         for p in range(4):
             cols = slice(256 * p, 256 * p + 256)
-            s = dot_nn(keys, wide_ref[rho, :, cols])
-            if masked:
-                s = jnp.where(vis, s, NEG)
+            s = scores(keys, rho, cols, vis)
             m_old = m_ref[rho, :, cols]
             m_new = jnp.maximum(m_old, jnp.max(s, axis=0, keepdims=True))
             e = jnp.exp2((s - m_new) * C2)
@@ -236,7 +240,30 @@
             )
             m_ref[rho, :, cols] = m_new
 
-    items(ks, (0, 1, 2, 3), tab, body, True)
+    def later_body(n, rho, half, size, kind, masked):
+        rows, keys, vis = inputs(n, rho, half, size, kind, masked)
+        slot = (n * 4 + rho) * 2 + half
+        t_ref[slot] = m_ref[rho]
+        top_ref[...] = m_ref[rho]
+
+        def attempt(_):
+            ref = jnp.maximum(t_ref[slot], top_ref[...])
+            t_ref[slot] = ref
+            for p in range(4):
+                cols = slice(256 * p, 256 * p + 256)
+                s = scores(keys, rho, cols, vis)
+                e = jnp.exp2((s - t_ref[slot, :, cols]) * C2)
+                e_ref[n * 4 + rho, rows, cols] = e.astype(BF16)
+                sum_ref[:, cols] = jnp.sum(e, axis=0, keepdims=True)
+                top_ref[:, cols] = jnp.max(s, axis=0, keepdims=True)
+            return jnp.max((top_ref[...] - ref) * C2)
+
+        lax.while_loop(lambda over: over > 32.0, attempt, jnp.float32(64.0))
+        ref = t_ref[slot]
+        l_ref[rho] = l_ref[rho] * jnp.exp2((m_ref[rho] - ref) * C2) + sum_ref[...]
+        m_ref[rho] = ref
+
+    items(ks, (0, 1, 2, 3), tab, first_body if ks == (0,) else later_body, True)
 
 
 def grads_body(ks, rhos, first, last, *refs):
@@ -321,7 +348,8 @@
 
     def four(x):
         other = hop(x, perm=flip(2))
-        return (x, hop(x, perm=flip(1)), other, hop(other, perm=flip(1)))
+        last = hop(other, perm=flip(1))
+        return (x, hop(x, perm=flip(1)), other, last)
 
     q_four = four(q_own)
     g_own = call(cotangent_body, shape((NQ + 16, H * HD)), [VM] * 2, nbytes=MIB)(grad_out[0], saved_out[0])
@@ -348,10 +376,12 @@
             functools.partial(stats_body, ks),
             [stat, stat, shape((4 * n, NK, NQ * H)), shape((8 * n, 1, NQ * H), F32)],
             [SM] + [VM] * (4 + n), vmem=3,
-            scratch=[pltpu.VMEM((n, NK + 16, 256), BF16)], flops=n * (1 << 29), nbytes=2 * MIB,
+            scratch=[pltpu.VMEM((n, NK + 16, 256), BF16)] + [pltpu.VMEM((1, NQ * H), F32)] * 2,
+            flops=n * (1 << 29), nbytes=2 * MIB,
         )(tab, tag, q_wide, m, l, *[sets[k] for k in ks])
         if step < 4:
-            fwd, bwd, m, l = lax.optimization_barrier((fwd, bwd, m, l))
+            if step > 0:
+                fwd, bwd, m, l = lax.optimization_barrier((fwd, bwd, m, l))
             sets[step + 1] = bwd
             if step < 3:
                 sets[-step - 1] = fwd

time: 134 us -> 141 us (1.052)
  the two profiles are of different devices: /device:TPU:1 before, /device:TPU:17 now
where the time goes in v1:
time: 141 us; the launch traced here: 140 us
  Pallas kernels  52.5 us (37%)
  starting transfers between devices  47.8 us (34%)
  waiting for transfers between devices  35 us (25%)
  local copies, waits for them, and re-layouts  2.61 us (2%)
  other arithmetic  1.49 us (1%)
    pallas_call x6, Pallas kernels, grads(): call(functools.partial(grads_body, ks, rhos, first, last), ([piece, piece...  24.5 us
    pallas_call x5, Pallas kernels, per_device(): call(functools.partial(stats_body, ks), [stat, stat, shape((4 * n, NK, NQ...  21.8 us
    ppermute x3, starting transfers between devices, per_device(): down = hop(sends[1], perm=turn(-1))  14.3 us
    ppermute x4, waiting for transfers between devices, per_device(): up = hop(sends[0], perm=turn(1))  12.4 us
    ppermute x6, starting transfers between devices, per_device(): fwd, bwd = (hop(fwd, perm=turn(1)), hop(bwd, perm=turn(-1)))  11.2 us
    ppermute x3, waiting for transfers between devices, per_device(): got = [hop(parts[r], perm=flip(r)) for r in (1, 2, 3)]  8.51 us
    ppermute x6, waiting for transfers between devices, per_device(): fwd, bwd = (hop(fwd, perm=turn(1)), hop(bwd, perm=turn(-1)))  6.78 us
    ppermute x1, starting transfers between devices, per_device(): dq3 = hop(dq3, perm=flip(1))  3.94 us
  transfers between devices with their start and end apart: 32, of which 11 were waited for; matrix products, arithmetic and copies ran while one was open for 0% of the time, Pallas kernels for 30%

profile of v1, /device:TPU:17, one launch (start us, length us, event | category | flops | bytes accessed | tf_op | source)
XLA Modules:
  0.0 140.4 jit_solution(16632127825361244362)
XLA Ops:
  0.7 0.7 pad_add_fusion.tab.refs_0_
  1.3 2.6 %shard_map.96 = (bf16[144,256]{1,0:T(8,128)(2,1)}, bf16[144,256]{1,0:T(8,128)(2,1)}, bf16[144,256]{1,0:T(8,128)(2,1)}, bf16[144,256]{1,0:T(8,128)(2,1)}, bf16[144,1024]{1,0:T(8,128)(2,1)}) custom-call(s32[2]{0:T(128)} %pad_add_fusion.tab.refs_0_, bf16[512,128]{1,0:T(8,128)(2,1)} %bitcast.45, bf16[512,128]{1,0:T(8,128)(2,1)} %bitcast.46, s32[1,512]{1,0:T(1,128)} %seg_hbm.1, ...), custom_call_target="tpu_custom_call" | custom-call | bytes 1048576 | tf_op jit(solution)/shard_map/pallas_call | solution.py:338
  4.0 1.1 collective-permute-start.4
  5.0 1.0 collective-permute-start.6
  6.0 0.5 collective-permute-start.7
  6.5 1.2 collective-permute-start.8
  7.6 6.1 %collective-permute-done.7.p2 = bf16[144,256]{1,0:T(8,128)(2,1)S(1)} collective-permute-done((bf16[144,256]{1,0:T(8,128)(2,1)}, bf16[144,256]{1,0:T(8,128)(2,1)S(1)}, u32[]{:S(2)}, u32[]{:S(2)}) %collective-permute-start.7) | collective-permute-done | bytes 73760 | tf_op jit(solution)/shard_map/ppermute | solution.py:346
  13.7 2.4 %collective-permute-done.8.p3 = bf16[144,256]{1,0:T(8,128)(2,1)S(1)} collective-permute-done((bf16[144,256]{1,0:T(8,128)(2,1)}, bf16[144,256]{1,0:T(8,128)(2,1)S(1)}, u32[]{:S(2)}, u32[]{:S(2)}) %collective-permute-start.8) | collective-permute-done | bytes 73760 | tf_op jit(solution)/shard_map/ppermute | solution.py:346
  16.1 0.9 copy-done.3
  17.1 1.7 %collective-permute-start.9 = (bf16[528,256]{1,0:T(8,128)(2,1)S(1)}, bf16[528,256]{1,0:T(8,128)(2,1)S(1)}, u32[]{:S(2)}, u32[]{:S(2)}) collective-permute-start(bf16[528,256]{1,0:T(8,128)(2,1)S(1)} %shard_map.98.refs_5_.refs_8_), channel_id=1, source_target_pairs={{0,2},{1,3},{2,4},{3,5},{4,6},{5,7},{6,8},{7,9},{8,10},{9,11},{10,... | collective-permute-start | bytes 811016 | tf_op jit(solution)/shard_map/ppermute | solution.py:372
  18.8 4.0 %collective-permute-start.11 = (bf16[528,256]{1,0:T(8,128)(2,1)S(1)}, bf16[528,256]{1,0:T(8,128)(2,1)S(1)}, u32[]{:S(2)}, u32[]{:S(2)}) collective-permute-start(bf16[528,256]{1,0:T(8,128)(2,1)S(1)} %shard_map.98.refs_5_.refs_8_), channel_id=1, source_target_pairs={{0,14},{1,15},{2,0},{3,1},{4,2},{5,3},{6,4},{7,5},{8,6},{9,7},{10,... | collective-permute-start | bytes 811016 | tf_op jit(solution)/shard_map/ppermute | solution.py:372
  23.3 6.3 %collective-permute-done.9.refs_6_.refs_9_ = bf16[528,256]{1,0:T(8,128)(2,1)S(1)} collective-permute-done((bf16[528,256]{1,0:T(8,128)(2,1)S(1)}, bf16[528,256]{1,0:T(8,128)(2,1)S(1)}, u32[]{:S(2)}, u32[]{:S(2)}) %collective-permute-start.9) | collective-permute-done | bytes 270368 | tf_op jit(solution)/shard_map/ppermute | solution.py:372
  29.7 2.7 %collective-permute-start.12 = (bf16[528,256]{1,0:T(8,128)(2,1)S(1)}, bf16[528,256]{1,0:T(8,128)(2,1)S(1)}, u32[]{:S(2)}, u32[]{:S(2)}) collective-permute-start(bf16[528,256]{1,0:T(8,128)(2,1)S(1)} %collective-permute-done.11.refs_5_.refs_8_), channel_id=1, source_target_pairs={{0,14},{1,15},{2,0},{3,1},{4,2},{5,3},{6,4},{7,5},{8,6},{9,7},{10,... | collective-permute-start | bytes 811016 | tf_op jit(solution)/shard_map/ppermute | solution.py:372
  32.4 1.0 copy-done
  33.3 0.9 shard_map.97
  34.3 0.7 copy-done.4
  34.9 4.0 %shard_map.99 = (f32[4,1,1024]{2,1,0:T(1,128)S(1)}, f32[4,1,1024]{2,1,0:T(1,128)S(1)}, bf16[4,512,1024]{2,1,0:T(8,128)(2,1)S(1)}, f32[8,1,1024]{2,1,0:T(1,128)S(1)}) custom-call(s32[2]{0:T(128)S(1)} %copy-done.4, f32[4,1,1024]{2,1,0:T(1,128)S(1)} %get-tuple-element.75.refs_1_, bf16[4,128,1024]{2,1,0:T(8,128)(2,1)S(1)} %get-tuple-element.76.refs_2_, ...), custom_call_target="tpu_custom_call" | custom-call | flops 536870912 | bytes 2097152 | tf_op jit(solution)/shard_map/pallas_call | solution.py:375
  38.9 7.5 %shard_map.100 = (f32[4,1,1024]{2,1,0:T(1,128)S(1)}, f32[4,1,1024]{2,1,0:T(1,128)S(1)}, bf16[8,512,1024]{2,1,0:T(8,128)(2,1)S(1)}, f32[16,1,1024]{2,1,0:T(1,128)S(1)}) custom-call(s32[2]{0:T(128)S(1)} %copy-done.4, f32[4,1,1024]{2,1,0:T(1,128)S(1)} %get-tuple-element.75.refs_1_, bf16[4,128,1024]{2,1,0:T(8,128)(2,1)S(1)} %get-tuple-element.76.refs_2_, ...), custom_call_target="tpu_custom_call" | custom-call | flops 1073741824 | bytes 2097152 | tf_op jit(solution)/shard_map/pallas_call | solution.py:375
  46.7 2.4 %collective-permute-start.14 = (bf16[528,256]{1,0:T(8,128)(2,1)S(1)}, bf16[528,256]{1,0:T(8,128)(2,1)S(1)}, u32[]{:S(2)}, u32[]{:S(2)}) collective-permute-start(bf16[528,256]{1,0:T(8,128)(2,1)S(1)} %collective-permute-done.12.refs_5_.refs_8_), channel_id=1, source_target_pairs={{0,14},{1,15},{2,0},{3,1},{4,2},{5,3},{6,4},{7,5},{8,6},{9,7},{10,... | collective-permute-start | bytes 811016 | tf_op jit(solution)/shard_map/ppermute | solution.py:372
  49.5 4.2 %shard_map.101 = (f32[4,1,1024]{2,1,0:T(1,128)S(1)}, f32[4,1,1024]{2,1,0:T(1,128)S(1)}, bf16[8,512,1024]{2,1,0:T(8,128)(2,1)S(1)}, f32[16,1,1024]{2,1,0:T(1,128)S(1)}) custom-call(s32[2]{0:T(128)S(1)} %copy-done.5, f32[4,1,1024]{2,1,0:T(1,128)S(1)} %get-tuple-element.75.refs_1_, bf16[4,128,1024]{2,1,0:T(8,128)(2,1)S(1)} %get-tuple-element.76.refs_2_, ...), custom_call_target="tpu_custom_call" | custom-call | flops 1073741824 | bytes 2097152 | tf_op jit(solution)/shard_map/pallas_call | solution.py:375
  54.2 3.5 %collective-permute-start.15 = (bf16[528,256]{1,0:T(8,128)(2,1)S(1)}, bf16[528,256]{1,0:T(8,128)(2,1)S(1)}, u32[]{:S(2)}, u32[]{:S(2)}) collective-permute-start(bf16[528,256]{1,0:T(8,128)(2,1)S(1)} %collective-permute-done.14.refs_5_.refs_8_), channel_id=1, source_target_pairs={{0,14},{1,15},{2,0},{3,1},{4,2},{5,3},{6,4},{7,5},{8,6},{9,7},{10,... | collective-permute-start | bytes 811016 | tf_op jit(solution)/shard_map/ppermute | solution.py:374
  57.7 3.6 %collective-permute-start = (bf16[144,1024]{1,0:T(8,128)(2,1)S(1)}, bf16[144,1024]{1,0:T(8,128)(2,1)S(1)}, u32[]{:S(2)}, u32[]{:S(2)}) collective-permute-start(bf16[144,1024]{1,0:T(8,128)(2,1)S(1)} %shard_map.94.q0), channel_id=1, source_target_pairs={{0,1},{1,0},{2,3},{3,2},{4,5},{5,4},{6,7},{7,6},{8,9},{9,8},{10,11... | collective-permute-start | bytes 884744 | tf_op jit(solution)/shard_map/ppermute | solution.py:352
  61.3 4.2 %shard_map.102 = (f32[4,1,1024]{2,1,0:T(1,128)S(1)}, f32[4,1,1024]{2,1,0:T(1,128)S(1)}, bf16[8,512,1024]{2,1,0:T(8,128)(2,1)S(1)}, f32[16,1,1024]{2,1,0:T(1,128)S(1)}) custom-call(s32[2]{0:T(128)S(1)} %copy-done.5, f32[4,1,1024]{2,1,0:T(1,128)S(1)} %get-tuple-element.75.refs_1_, bf16[4,128,1024]{2,1,0:T(8,128)(2,1)S(1)} %get-tuple-element.76.refs_2_, ...), custom_call_target="tpu_custom_call" | custom-call | flops 1073741824 | bytes 2097152 | tf_op jit(solution)/shard_map/pallas_call | solution.py:375
  65.5 1.9 %shard_map.103 = (f32[4,1,1024]{2,1,0:T(1,128)S(1)}, f32[4,1,1024]{2,1,0:T(1,128)S(1)}, bf16[4,512,1024]{2,1,0:T(8,128)(2,1)S(1)}, f32[8,1,1024]{2,1,0:T(1,128)S(1)}) custom-call(s32[2]{0:T(128)S(1)} %copy-done.5, f32[4,1,1024]{2,1,0:T(1,128)S(1)} %get-tuple-element.75.refs_1_, bf16[4,128,1024]{2,1,0:T(8,128)(2,1)S(1)} %get-tuple-element.76.refs_2_, ...), custom_call_target="tpu_custom_call" | custom-call | flops 536870912 | bytes 2097152 | tf_op jit(solution)/shard_map/pallas_call | solution.py:375
  67.5 1.8 %collective-permute-start.17 = (f32[8,1,1024]{2,1,0:T(1,128)S(1)}, f32[8,1,1024]{2,1,0:T(1,128)S(1)}, u32[]{:S(2)}, u32[]{:S(2)}) collective-permute-start(f32[8,1,1024]{2,1,0:T(1,128)S(1)} %constant_dynamic-update-slice_fusion), channel_id=1, source_target_pairs={{0,16},{1,17},{2,18},{3,19},{4,20},{5,21},{6,22},{7,23},{8,24},{9,... | collective-permute-start | bytes 98312 | tf_op jit(solution)/shard_map/ppermute | solution.py:395
  69.3 0.9 shard_map.95
  70.2 1.0 collective-permute-start.18
  71.7 2.0 %collective-permute-done.18 = f32[8,1,1024]{2,1,0:T(1,128)S(1)} collective-permute-done((f32[8,1,1024]{2,1,0:T(1,128)S(1)}, f32[8,1,1024]{2,1,0:T(1,128)S(1)}, u32[]{:S(2)}, u32[]{:S(2)}) %collective-permute-start.18) | collective-permute-done | bytes 32800 | tf_op jit(solution)/shard_map/ppermute | solution.py:395
  73.9 2.6 %shard_map.104 = (f32[4,128,1024]{2,1,0:T(8,128)S(1)}, f32[1,512,256]{2,1,0:T(8,128)S(1)}) custom-call(s32[2]{0:T(128)S(1)} %copy-done.5, f32[4,1,1024]{2,1,0:T(1,128)S(1)} %get-tuple-element.73.refs_1_, f32[4,1,1024]{2,1,0:T(1,128)S(1)} %multiply_add_fusion.refs_2_, bf16[4,1024,128]{2,1,0:T(8,128)(2,1)S(1)} %get-tuple-element.102.refs_3_, ...), custom_call_target="tpu_custom_call" | custom-call | flops 2684354560 | bytes 8388608 | tf_op jit(solution)/shard_map/pallas_call | solution.py:413
  76.5 4.0 %shard_map.105 = (f32[4,128,1024]{2,1,0:T(8,128)S(1)}, f32[2,512,256]{2,1,0:T(8,128)S(1)}) custom-call(s32[2]{0:T(128)S(1)} %copy-done.5, f32[4,1,1024]{2,1,0:T(1,128)S(1)} %get-tuple-element.73.refs_1_, f32[4,1,1024]{2,1,0:T(1,128)S(1)} %multiply_add_fusion.refs_2_, ...), custom_call_target="tpu_custom_call", output_to_operand_aliasing={{0}: (10, {})} | custom-call | flops 5368709120 | bytes 8388608 | tf_op jit(solution)/shard_map/pallas_call | solution.py:413
  80.6 6.8 %collective-permute-done.19 = bf16[512,256]{1,0:T(8,128)(2,1)S(1)} collective-permute-done((bf16[512,256]{1,0:T(8,128)(2,1)S(1)}, bf16[512,256]{1,0:T(8,128)(2,1)S(1)}, u32[]{:S(2)}, u32[]{:S(2)}) %collective-permute-start.19) | collective-permute-done | bytes 262176 | tf_op jit(solution)/shard_map/ppermute | solution.py:429
  87.5 4.2 %collective-permute-start.21 = (bf16[512,256]{1,0:T(8,128)(2,1)S(1)}, bf16[512,256]{1,0:T(8,128)(2,1)S(1)}, u32[]{:S(2)}, u32[]{:S(2)}) collective-permute-start(bf16[512,256]{1,0:T(8,128)(2,1)S(1)} %fusion.8), channel_id=1, source_target_pairs={{0,14},{1,15},{2,0},{3,1},{4,2},{5,3},{6,4},{7,5},{8,6},{9,7},{10,... | collective-permute-start | bytes 786440 | tf_op jit(solution)/shard_map/ppermute | solution.py:431
  91.7 4.0 %shard_map.106 = (f32[4,128,1024]{2,1,0:T(8,128)S(1)}, f32[2,512,256]{2,1,0:T(8,128)S(1)}) custom-call(s32[2]{0:T(128)S(1)} %copy-done.5, f32[4,1,1024]{2,1,0:T(1,128)S(1)} %get-tuple-element.73.refs_1_, f32[4,1,1024]{2,1,0:T(1,128)S(1)} %multiply_add_fusion.refs_2_, ...), custom_call_target="tpu_custom_call", output_to_operand_aliasing={{0}: (10, {})} | custom-call | flops 5368709120 | bytes 8388608 | tf_op jit(solution)/shard_map/pallas_call | solution.py:413
  95.7 2.4 %collective-permute-done.20 = bf16[512,256]{1,0:T(8,128)(2,1)S(1)} collective-permute-done((bf16[512,256]{1,0:T(8,128)(2,1)S(1)}, bf16[512,256]{1,0:T(8,128)(2,1)S(1)}, u32[]{:S(2)}, u32[]{:S(2)}) %collective-permute-start.20) | collective-permute-done | bytes 262176 | tf_op jit(solution)/shard_map/ppermute | solution.py:429
  98.3 4.9 %collective-permute-start.23 = (bf16[512,256]{1,0:T(8,128)(2,1)S(1)}, bf16[512,256]{1,0:T(8,128)(2,1)S(1)}, u32[]{:S(2)}, u32[]{:S(2)}) collective-permute-start(bf16[512,256]{1,0:T(8,128)(2,1)S(1)} %get-tuple-element.130), channel_id=1, source_target_pairs={{0,14},{1,15},{2,0},{3,1},{4,2},{5,3},{6,4},{7,5},{8,6},{9,7},{10,... | collective-permute-start | bytes 786440 | tf_op jit(solution)/shard_map/ppermute | solution.py:431
  103.2 6.6 %shard_map.107 = (f32[4,128,1024]{2,1,0:T(8,128)S(1)}, f32[2,512,256]{2,1,0:T(8,128)S(1)}) custom-call(s32[2]{0:T(128)S(1)} %copy-done.5, f32[4,1,1024]{2,1,0:T(1,128)S(1)} %get-tuple-element.73.refs_1_, f32[4,1,1024]{2,1,0:T(1,128)S(1)} %multiply_add_fusion.refs_2_, ...), custom_call_target="tpu_custom_call", output_to_operand_aliasing={{0}: (10, {})} | custom-call | flops 5368709120 | bytes 8388608 | tf_op jit(solution)/shard_map/pallas_call | solution.py:413
  110.0 4.3 %shard_map.108 = (bf16[128,1024]{1,0:T(8,128)(2,1)S(1)}, bf16[128,1024]{1,0:T(8,128)(2,1)S(1)}, f32[1,512,256]{2,1,0:T(8,128)S(1)}) custom-call(s32[2]{0:T(128)S(1)} %copy-done.5, f32[4,1,1024]{2,1,0:T(1,128)S(1)} %get-tuple-element.73.refs_1_, f32[4,1,1024]{2,1,0:T(1,128)S(1)} %multiply_add_fusion.refs_2_, ...), custom_call_target="tpu_custom_call" | custom-call | flops 2684354560 | bytes 8388608 | tf_op jit(solution)/shard_map/pallas_call | solution.py:413
  114.3 3.9 %collective-permute-start.30 = (bf16[128,1024]{1,0:T(8,128)(2,1)S(1)}, bf16[128,1024]{1,0:T(8,128)(2,1)S(1)}, u32[]{:S(2)}, u32[]{:S(2)}) collective-permute-start(bf16[128,1024]{1,0:T(8,128)(2,1)S(1)} %get-tuple-element.139), channel_id=1, source_target_pairs={{0,1},{1,0},{2,3},{3,2},{4,5},{5,4},{6,7},{7,6},{8,9},{9,8},{10,11... | collective-permute-start | bytes 786440 | tf_op jit(solution)/shard_map/ppermute | solution.py:433
  118.3 5.3 %collective-permute-start.25 = (bf16[512,256]{1,0:T(8,128)(2,1)S(1)}, bf16[512,256]{1,0:T(8,128)(2,1)S(1)}, u32[]{:S(2)}, u32[]{:S(2)}) collective-permute-start(bf16[512,256]{1,0:T(8,128)(2,1)S(1)} %get-tuple-element.135), channel_id=1, source_target_pairs={{0,14},{1,15},{2,0},{3,1},{4,2},{5,3},{6,4},{7,5},{8,6},{9,7},{10,... | collective-permute-start | bytes 786440 | tf_op jit(solution)/shard_map/ppermute | solution.py:431
  123.6 3.0 %shard_map.109 = (bf16[128,1024]{1,0:T(8,128)(2,1)S(1)}, bf16[128,1024]{1,0:T(8,128)(2,1)S(1)}, f32[1,512,256]{2,1,0:T(8,128)S(1)}) custom-call(s32[2]{0:T(128)S(1)} %copy-done.5, f32[4,1,1024]{2,1,0:T(1,128)S(1)} %get-tuple-element.73.refs_1_, f32[4,1,1024]{2,1,0:T(1,128)S(1)} %multiply_add_fusion.refs_2_, ...), custom_call_target="tpu_custom_call" | custom-call | flops 2684354560 | bytes 8388608 | tf_op jit(solution)/shard_map/pallas_call | solution.py:413
  126.6 0.5 collective-permute-start.29
  127.2 1.9 %collective-permute-done.25 = bf16[512,256]{1,0:T(8,128)(2,1)S(1)} collective-permute-done((bf16[512,256]{1,0:T(8,128)(2,1)S(1)}, bf16[512,256]{1,0:T(8,128)(2,1)S(1)}, u32[]{:S(2)}, u32[]{:S(2)}) %collective-permute-start.25) | collective-permute-done | bytes 262176 | tf_op jit(solution)/shard_map/ppermute | solution.py:431
  129.1 3.1 %collective-permute-done.24 = bf16[512,256]{1,0:T(8,128)(2,1)S(1)} collective-permute-done((bf16[512,256]{1,0:T(8,128)(2,1)S(1)}, bf16[512,256]{1,0:T(8,128)(2,1)S(1)}, u32[]{:S(2)}, u32[]{:S(2)}) %collective-permute-start.24) | collective-permute-done | bytes 262176 | tf_op jit(solution)/shard_map/ppermute | solution.py:429
  132.4 1.3 collective-permute-start.26
  133.7 1.7 %collective-permute-start.28 = (bf16[128,256]{1,0:T(8,128)(2,1)S(1)}, bf16[128,256]{1,0:T(8,128)(2,1)S(1)}, u32[]{:S(2)}, u32[]{:S(2)}) collective-permute-start(bf16[128,256]{1,0:T(8,128)(2,1)S(1)} %get-tuple-element.147), channel_id=1, source_target_pairs={{0,17},{1,16},{2,19},{3,18},{4,21},{5,20},{6,23},{7,22},{8,25},{9,... | collective-permute-start | bytes 196616 | tf_op jit(solution)/shard_map/ppermute | solution.py:441
  135.5 1.8 %collective-permute-done.27.a2 = bf16[128,256]{1,0:T(8,128)(2,1)S(1)} collective-permute-done((bf16[128,256]{1,0:T(8,128)(2,1)S(1)}, bf16[128,256]{1,0:T(8,128)(2,1)S(1)}, u32[]{:S(2)}, u32[]{:S(2)}) %collective-permute-start.27) | collective-permute-done | bytes 65568 | tf_op jit(solution)/shard_map/ppermute | solution.py:441
  137.3 1.7 %collective-permute-done.28.a3 = bf16[128,256]{1,0:T(8,128)(2,1)S(1)} collective-permute-done((bf16[128,256]{1,0:T(8,128)(2,1)S(1)}, bf16[128,256]{1,0:T(8,128)(2,1)S(1)}, u32[]{:S(2)}, u32[]{:S(2)}) %collective-permute-start.28) | collective-permute-done | bytes 65568 | tf_op jit(solution)/shard_map/ppermute | solution.py:441
  139.0 1.4 %shard_map.110 = (bf16[128,1024]{1,0:T(8,128)(2,1)}, bf16[512,128]{1,0:T(8,128)(2,1)}, bf16[512,128]{1,0:T(8,128)(2,1)}) custom-call(s32[2]{0:T(128)S(1)} %copy-done.5, bf16[128,256]{1,0:T(8,128)(2,1)S(1)} %get-tuple-element.150.a0, bf16[128,256]{1,0:T(8,128)(2,1)S(1)} %collective-permute-done.26.a1, bf16[128,256]{1,0:T(8,128)(2,1)S(1)} %collective-permute-done.27.a2, ...), custom_call_target="tpu_custom_call" | custom-call | bytes 2097152 | tf_op jit(solution)/shard_map/pallas_call | solution.py:442
  (63 shorter events, 3.2 us)
Async XLA Ops:
  0.6 48.5 %copy-start.1 = (bf16[1,128,1024]{2,1,0:T(8,128)(2,1)S(1)}, bf16[1,128,1024]{2,1,0:T(8,128)(2,1)}, u32[]{:S(2)}) copy-start(bf16[1,128,1024]{2,1,0:T(8,128)(2,1)} %param.10) | copy-start | bytes 786436
  0.6 48.5 %copy-start.2 = (bf16[1,128,1024]{2,1,0:T(8,128)(2,1)S(1)}, bf16[1,128,1024]{2,1,0:T(8,128)(2,1)}, u32[]{:S(2)}) copy-start(bf16[1,128,1024]{2,1,0:T(8,128)(2,1)} %param.11) | copy-start | bytes 786436
  4.0 19.0 %collective-permute-start.4 = (bf16[144,1024]{1,0:T(8,128)(2,1)}, bf16[144,1024]{1,0:T(8,128)(2,1)S(1)}, u32[]{:S(2)}, u32[]{:S(2)}) collective-permute-start(bf16[144,1024]{1,0:T(8,128)(2,1)} %get-tuple-element.74.q0), channel_id=1, source_target_pairs={{0,16},{1,17},{2,18},{3,19},{4,20},{5,21},{6,22},{7,23},{8,24},{9,... | collective-permute-start | bytes 884744 | tf_op jit(solution)/shard_map/ppermute | solution.py:350
  5.0 2.6 %collective-permute-start.6 = (bf16[144,256]{1,0:T(8,128)(2,1)}, bf16[144,256]{1,0:T(8,128)(2,1)S(1)}, u32[]{:S(2)}, u32[]{:S(2)}) collective-permute-start(bf16[144,256]{1,0:T(8,128)(2,1)} %get-tuple-element.78), channel_id=1, source_target_pairs={{0,1},{1,0},{2,3},{3,2},{4,5},{5,4},{6,7},{7,6},{8,9},{9,8},{10,11... | collective-permute-start | bytes 221192 | tf_op jit(solution)/shard_map/ppermute | solution.py:346
  6.0 7.7 %collective-permute-start.7 = (bf16[144,256]{1,0:T(8,128)(2,1)}, bf16[144,256]{1,0:T(8,128)(2,1)S(1)}, u32[]{:S(2)}, u32[]{:S(2)}) collective-permute-start(bf16[144,256]{1,0:T(8,128)(2,1)} %get-tuple-element.79), channel_id=1, source_target_pairs={{0,16},{1,17},{2,18},{3,19},{4,20},{5,21},{6,22},{7,23},{8,24},{9,... | collective-permute-start | bytes 221192 | tf_op jit(solution)/shard_map/ppermute | solution.py:346
  6.5 9.7 %collective-permute-start.8 = (bf16[144,256]{1,0:T(8,128)(2,1)}, bf16[144,256]{1,0:T(8,128)(2,1)S(1)}, u32[]{:S(2)}, u32[]{:S(2)}) collective-permute-start(bf16[144,256]{1,0:T(8,128)(2,1)} %get-tuple-element.80), channel_id=1, source_target_pairs={{0,17},{1,16},{2,19},{3,18},{4,21},{5,20},{6,23},{7,22},{8,25},{9,... | collective-permute-start | bytes 221192 | tf_op jit(solution)/shard_map/ppermute | solution.py:346
  16.1 0.9 copy-start.3
  17.0 32.5 %copy-start.5 = (s32[2]{0:T(128)S(1)}, s32[2]{0:T(128)}, u32[]{:S(2)}) copy-start(s32[2]{0:T(128)} %pad_add_fusion.tab.refs_0_) | copy-start | bytes 28
  17.1 12.6 %collective-permute-start.9 = (bf16[528,256]{1,0:T(8,128)(2,1)S(1)}, bf16[528,256]{1,0:T(8,128)(2,1)S(1)}, u32[]{:S(2)}, u32[]{:S(2)}) collective-permute-start(bf16[528,256]{1,0:T(8,128)(2,1)S(1)} %shard_map.98.refs_5_.refs_8_), channel_id=1, source_target_pairs={{0,2},{1,3},{2,4},{3,5},{4,6},{5,7},{6,8},{7,9},{8,10},{9,11},{10,... | collective-permute-start | bytes 811016 | tf_op jit(solution)/shard_map/ppermute | solution.py:372
  18.8 10.9 %collective-permute-start.11 = (bf16[528,256]{1,0:T(8,128)(2,1)S(1)}, bf16[528,256]{1,0:T(8,128)(2,1)S(1)}, u32[]{:S(2)}, u32[]{:S(2)}) collective-permute-start(bf16[528,256]{1,0:T(8,128)(2,1)S(1)} %shard_map.98.refs_5_.refs_8_), channel_id=1, source_target_pairs={{0,14},{1,15},{2,0},{3,1},{4,2},{5,3},{6,4},{7,5},{8,6},{9,7},{10,... | collective-permute-start | bytes 811016 | tf_op jit(solution)/shard_map/ppermute | solution.py:372
  22.8 9.5 %collective-permute-start.3 = (bf16[144,1024]{1,0:T(8,128)(2,1)}, bf16[144,1024]{1,0:T(8,128)(2,1)S(1)}, u32[]{:S(2)}, u32[]{:S(2)}) collective-permute-start(bf16[144,1024]{1,0:T(8,128)(2,1)} %get-tuple-element.74.q0), channel_id=1, source_target_pairs={{0,1},{1,0},{2,3},{3,2},{4,5},{5,4},{6,7},{7,6},{8,9},{9,8},{10,11... | collective-permute-start | bytes 884744 | tf_op jit(solution)/shard_map/ppermute | solution.py:352
  23.0 9.4 %collective-permute-start.5 = (bf16[144,1024]{1,0:T(8,128)(2,1)S(1)}, bf16[144,1024]{1,0:T(8,128)(2,1)S(1)}, u32[]{:S(2)}, u32[]{:S(2)}) collective-permute-start(bf16[144,1024]{1,0:T(8,128)(2,1)S(1)} %collective-permute-done.4.q2), channel_id=1, source_target_pairs={{0,1},{1,0},{2,3},{3,2},{4,5},{5,4},{6,7},{7,6},{8,9},{9,8},{10,11... | collective-permute-start | bytes 884744 | tf_op jit(solution)/shard_map/ppermute | solution.py:351
  29.7 16.7 %collective-permute-start.10 = (bf16[528,256]{1,0:T(8,128)(2,1)S(1)}, bf16[528,256]{1,0:T(8,128)(2,1)S(1)}, u32[]{:S(2)}, u32[]{:S(2)}) collective-permute-start(bf16[528,256]{1,0:T(8,128)(2,1)S(1)} %collective-permute-done.9.refs_6_.refs_9_), channel_id=1, source_target_pairs={{0,2},{1,3},{2,4},{3,5},{4,6},{5,7},{6,8},{7,9},{8,10},{9,11},{10,... | collective-permute-start | bytes 811016 | tf_op jit(solution)/shard_map/ppermute | solution.py:372
  29.7 16.7 %collective-permute-start.12 = (bf16[528,256]{1,0:T(8,128)(2,1)S(1)}, bf16[528,256]{1,0:T(8,128)(2,1)S(1)}, u32[]{:S(2)}, u32[]{:S(2)}) collective-permute-start(bf16[528,256]{1,0:T(8,128)(2,1)S(1)} %collective-permute-done.11.refs_5_.refs_8_), channel_id=1, source_target_pairs={{0,14},{1,15},{2,0},{3,1},{4,2},{5,3},{6,4},{7,5},{8,6},{9,7},{10,... | collective-permute-start | bytes 811016 | tf_op jit(solution)/shard_map/ppermute | solution.py:372
  32.4 1.0 copy-start
  34.3 0.7 copy-start.4
  46.4 7.8 %collective-permute-start.13 = (bf16[528,256]{1,0:T(8,128)(2,1)S(1)}, bf16[528,256]{1,0:T(8,128)(2,1)S(1)}, u32[]{:S(2)}, u32[]{:S(2)}) collective-permute-start(bf16[528,256]{1,0:T(8,128)(2,1)S(1)} %collective-permute-done.10.refs_6_.refs_9_), channel_id=1, source_target_pairs={{0,2},{1,3},{2,4},{3,5},{4,6},{5,7},{6,8},{7,9},{8,10},{9,11},{10,... | collective-permute-start | bytes 811016 | tf_op jit(solution)/shard_map/ppermute | solution.py:372
  46.7 7.4 %collective-permute-start.14 = (bf16[528,256]{1,0:T(8,128)(2,1)S(1)}, bf16[528,256]{1,0:T(8,128)(2,1)S(1)}, u32[]{:S(2)}, u32[]{:S(2)}) collective-permute-start(bf16[528,256]{1,0:T(8,128)(2,1)S(1)} %collective-permute-done.12.refs_5_.refs_8_), channel_id=1, source_target_pairs={{0,14},{1,15},{2,0},{3,1},{4,2},{5,3},{6,4},{7,5},{8,6},{9,7},{10,... | collective-permute-start | bytes 811016 | tf_op jit(solution)/shard_map/ppermute | solution.py:372
  49.4 11.9 %collective-permute-start.1 = (bf16[144,1024]{1,0:T(8,128)(2,1)S(1)}, bf16[144,1024]{1,0:T(8,128)(2,1)S(1)}, u32[]{:S(2)}, u32[]{:S(2)}) collective-permute-start(bf16[144,1024]{1,0:T(8,128)(2,1)S(1)} %shard_map.94.q0), channel_id=1, source_target_pairs={{0,16},{1,17},{2,18},{3,19},{4,20},{5,21},{6,22},{7,23},{8,24},{9,... | collective-permute-start | bytes 884744 | tf_op jit(solution)/shard_map/ppermute | solution.py:350
  54.2 11.4 %collective-permute-start.15 = (bf16[528,256]{1,0:T(8,128)(2,1)S(1)}, bf16[528,256]{1,0:T(8,128)(2,1)S(1)}, u32[]{:S(2)}, u32[]{:S(2)}) collective-permute-start(bf16[528,256]{1,0:T(8,128)(2,1)S(1)} %collective-permute-done.14.refs_5_.refs_8_), channel_id=1, source_target_pairs={{0,14},{1,15},{2,0},{3,1},{4,2},{5,3},{6,4},{7,5},{8,6},{9,7},{10,... | collective-permute-start | bytes 811016 | tf_op jit(solution)/shard_map/ppermute | solution.py:374
  57.7 11.6 %collective-permute-start = (bf16[144,1024]{1,0:T(8,128)(2,1)S(1)}, bf16[144,1024]{1,0:T(8,128)(2,1)S(1)}, u32[]{:S(2)}, u32[]{:S(2)}) collective-permute-start(bf16[144,1024]{1,0:T(8,128)(2,1)S(1)} %shard_map.94.q0), channel_id=1, source_target_pairs={{0,1},{1,0},{2,3},{3,2},{4,5},{5,4},{6,7},{7,6},{8,9},{9,8},{10,11... | collective-permute-start | bytes 884744 | tf_op jit(solution)/shard_map/ppermute | solution.py:352
  61.3 8.0 %collective-permute-start.2 = (bf16[144,1024]{1,0:T(8,128)(2,1)S(1)}, bf16[144,1024]{1,0:T(8,128)(2,1)S(1)}, u32[]{:S(2)}, u32[]{:S(2)}) collective-permute-start(bf16[144,1024]{1,0:T(8,128)(2,1)S(1)} %collective-permute-done.1.q2), channel_id=1, source_target_pairs={{0,1},{1,0},{2,3},{3,2},{4,5},{5,4},{6,7},{7,6},{8,9},{9,8},{10,11... | collective-permute-start | bytes 884744 | tf_op jit(solution)/shard_map/ppermute | solution.py:351
  67.5 4.2 %collective-permute-start.17 = (f32[8,1,1024]{2,1,0:T(1,128)S(1)}, f32[8,1,1024]{2,1,0:T(1,128)S(1)}, u32[]{:S(2)}, u32[]{:S(2)}) collective-permute-start(f32[8,1,1024]{2,1,0:T(1,128)S(1)} %constant_dynamic-update-slice_fusion), channel_id=1, source_target_pairs={{0,16},{1,17},{2,18},{3,19},{4,20},{5,21},{6,22},{7,23},{8,24},{9,... | collective-permute-start | bytes 98312 | tf_op jit(solution)/shard_map/ppermute | solution.py:395
  70.2 3.4 %collective-permute-start.18 = (f32[8,1,1024]{2,1,0:T(1,128)S(1)}, f32[8,1,1024]{2,1,0:T(1,128)S(1)}, u32[]{:S(2)}, u32[]{:S(2)}) collective-permute-start(f32[8,1,1024]{2,1,0:T(1,128)S(1)} %constant_dynamic-update-slice_fusion), channel_id=1, source_target_pairs={{0,17},{1,16},{2,19},{3,18},{4,21},{5,20},{6,23},{7,22},{8,25},{9,... | collective-permute-start | bytes 98312 | tf_op jit(solution)/shard_map/ppermute | solution.py:395
  71.2 2.4 %collective-permute-start.16 = (f32[8,1,1024]{2,1,0:T(1,128)S(1)}, f32[8,1,1024]{2,1,0:T(1,128)S(1)}, u32[]{:S(2)}, u32[]{:S(2)}) collective-permute-start(f32[8,1,1024]{2,1,0:T(1,128)S(1)} %constant_dynamic-update-slice_fusion), channel_id=1, source_target_pairs={{0,1},{1,0},{2,3},{3,2},{4,5},{5,4},{6,7},{7,6},{8,9},{9,8},{10,11... | collective-permute-start | bytes 98312 | tf_op jit(solution)/shard_map/ppermute | solution.py:395
  76.5 11.0 %collective-permute-start.19 = (bf16[512,256]{1,0:T(8,128)(2,1)S(1)}, bf16[512,256]{1,0:T(8,128)(2,1)S(1)}, u32[]{:S(2)}, u32[]{:S(2)}) collective-permute-start(bf16[512,256]{1,0:T(8,128)(2,1)S(1)} %convert_bitcast_fusion), channel_id=1, source_target_pairs={{0,2},{1,3},{2,4},{3,5},{4,6},{5,7},{6,8},{7,9},{8,10},{9,11},{10,... | collective-permute-start | bytes 786440 | tf_op jit(solution)/shard_map/ppermute | solution.py:429
  87.5 8.2 %collective-permute-start.21 = (bf16[512,256]{1,0:T(8,128)(2,1)S(1)}, bf16[512,256]{1,0:T(8,128)(2,1)S(1)}, u32[]{:S(2)}, u32[]{:S(2)}) collective-permute-start(bf16[512,256]{1,0:T(8,128)(2,1)S(1)} %fusion.8), channel_id=1, source_target_pairs={{0,14},{1,15},{2,0},{3,1},{4,2},{5,3},{6,4},{7,5},{8,6},{9,7},{10,... | collective-permute-start | bytes 786440 | tf_op jit(solution)/shard_map/ppermute | solution.py:431
  91.7 6.4 %collective-permute-start.20 = (bf16[512,256]{1,0:T(8,128)(2,1)S(1)}, bf16[512,256]{1,0:T(8,128)(2,1)S(1)}, u32[]{:S(2)}, u32[]{:S(2)}) collective-permute-start(bf16[512,256]{1,0:T(8,128)(2,1)S(1)} %fusion.7), channel_id=1, source_target_pairs={{0,2},{1,3},{2,4},{3,5},{4,6},{5,7},{6,8},{7,9},{8,10},{9,11},{10,... | collective-permute-start | bytes 786440 | tf_op jit(solution)/shard_map/ppermute | solution.py:429
  98.3 11.6 %collective-permute-start.23 = (bf16[512,256]{1,0:T(8,128)(2,1)S(1)}, bf16[512,256]{1,0:T(8,128)(2,1)S(1)}, u32[]{:S(2)}, u32[]{:S(2)}) collective-permute-start(bf16[512,256]{1,0:T(8,128)(2,1)S(1)} %get-tuple-element.130), channel_id=1, source_target_pairs={{0,14},{1,15},{2,0},{3,1},{4,2},{5,3},{6,4},{7,5},{8,6},{9,7},{10,... | collective-permute-start | bytes 786440 | tf_op jit(solution)/shard_map/ppermute | solution.py:431
  103.2 6.7 %collective-permute-start.22 = (bf16[512,256]{1,0:T(8,128)(2,1)S(1)}, bf16[512,256]{1,0:T(8,128)(2,1)S(1)}, u32[]{:S(2)}, u32[]{:S(2)}) collective-permute-start(bf16[512,256]{1,0:T(8,128)(2,1)S(1)} %get-tuple-element.129), channel_id=1, source_target_pairs={{0,2},{1,3},{2,4},{3,5},{4,6},{5,7},{6,8},{7,9},{8,10},{9,11},{10,... | collective-permute-start | bytes 786440 | tf_op jit(solution)/shard_map/ppermute | solution.py:429
  114.3 12.7 %collective-permute-start.30 = (bf16[128,1024]{1,0:T(8,128)(2,1)S(1)}, bf16[128,1024]{1,0:T(8,128)(2,1)S(1)}, u32[]{:S(2)}, u32[]{:S(2)}) collective-permute-start(bf16[128,1024]{1,0:T(8,128)(2,1)S(1)} %get-tuple-element.139), channel_id=1, source_target_pairs={{0,1},{1,0},{2,3},{3,2},{4,5},{5,4},{6,7},{7,6},{8,9},{9,8},{10,11... | collective-permute-start | bytes 786440 | tf_op jit(solution)/shard_map/ppermute | solution.py:433
  118.3 10.8 %collective-permute-start.25 = (bf16[512,256]{1,0:T(8,128)(2,1)S(1)}, bf16[512,256]{1,0:T(8,128)(2,1)S(1)}, u32[]{:S(2)}, u32[]{:S(2)}) collective-permute-start(bf16[512,256]{1,0:T(8,128)(2,1)S(1)} %get-tuple-element.135), channel_id=1, source_target_pairs={{0,14},{1,15},{2,0},{3,1},{4,2},{5,3},{6,4},{7,5},{8,6},{9,7},{10,... | collective-permute-start | bytes 786440 | tf_op jit(solution)/shard_map/ppermute | solution.py:431
  123.5 8.7 %collective-permute-start.24 = (bf16[512,256]{1,0:T(8,128)(2,1)S(1)}, bf16[512,256]{1,0:T(8,128)(2,1)S(1)}, u32[]{:S(2)}, u32[]{:S(2)}) collective-permute-start(bf16[512,256]{1,0:T(8,128)(2,1)S(1)} %get-tuple-element.134), channel_id=1, source_target_pairs={{0,2},{1,3},{2,4},{3,5},{4,6},{5,7},{6,8},{7,9},{8,10},{9,11},{10,... | collective-permute-start | bytes 786440 | tf_op jit(solution)/shard_map/ppermute | solution.py:429
  126.6 8.9 %collective-permute-start.29 = (bf16[128,1024]{1,0:T(8,128)(2,1)S(1)}, bf16[128,1024]{1,0:T(8,128)(2,1)S(1)}, u32[]{:S(2)}, u32[]{:S(2)}) collective-permute-start(bf16[128,1024]{1,0:T(8,128)(2,1)S(1)} %get-tuple-element.137), channel_id=1, source_target_pairs={{0,1},{1,0},{2,3},{3,2},{4,5},{5,4},{6,7},{7,6},{8,9},{9,8},{10,11... | collective-permute-start | bytes 786440 | tf_op jit(solution)/shard_map/ppermute | solution.py:440
  127.1 11.9 %collective-permute-start.31 = (bf16[128,1024]{1,0:T(8,128)(2,1)S(1)}, bf16[128,1024]{1,0:T(8,128)(2,1)S(1)}, u32[]{:S(2)}, u32[]{:S(2)}) collective-permute-start(bf16[128,1024]{1,0:T(8,128)(2,1)S(1)} %add_convert_fusion), channel_id=1, source_target_pairs={{0,16},{1,17},{2,18},{3,19},{4,20},{5,21},{6,22},{7,23},{8,24},{9,... | collective-permute-start | bytes 786440 | tf_op jit(solution)/shard_map/ppermute | solution.py:435
  132.4 3.1 %collective-permute-start.26 = (bf16[128,256]{1,0:T(8,128)(2,1)S(1)}, bf16[128,256]{1,0:T(8,128)(2,1)S(1)}, u32[]{:S(2)}, u32[]{:S(2)}) collective-permute-start(bf16[128,256]{1,0:T(8,128)(2,1)S(1)} %get-tuple-element.149), channel_id=1, source_target_pairs={{0,1},{1,0},{2,3},{3,2},{4,5},{5,4},{6,7},{7,6},{8,9},{9,8},{10,11... | collective-permute-start | bytes 196616 | tf_op jit(solution)/shard_map/ppermute | solution.py:441
  133.7 3.5 %collective-permute-start.27 = (bf16[128,256]{1,0:T(8,128)(2,1)S(1)}, bf16[128,256]{1,0:T(8,128)(2,1)S(1)}, u32[]{:S(2)}, u32[]{:S(2)}) collective-permute-start(bf16[128,256]{1,0:T(8,128)(2,1)S(1)} %get-tuple-element.148), channel_id=1, source_target_pairs={{0,16},{1,17},{2,18},{3,19},{4,20},{5,21},{6,22},{7,23},{8,24},{9,... | collective-permute-start | bytes 196616 | tf_op jit(solution)/shard_map/ppermute | solution.py:441
  133.7 5.2 %collective-permute-start.28 = (bf16[128,256]{1,0:T(8,128)(2,1)S(1)}, bf16[128,256]{1,0:T(8,128)(2,1)S(1)}, u32[]{:S(2)}, u32[]{:S(2)}) collective-permute-start(bf16[128,256]{1,0:T(8,128)(2,1)S(1)} %get-tuple-element.147), channel_id=1, source_target_pairs={{0,17},{1,16},{2,19},{3,18},{4,21},{5,20},{6,23},{7,22},{8,25},{9,... | collective-permute-start | bytes 196616 | tf_op jit(solution)/shard_map/ppermute | solution.py:441

commit v2 on v1

--- a/solution.py
+++ b/solution.py
@@ -209,7 +209,7 @@
     n_sets = len(ks)
     tab, tag_ref, wide_ref = refs[:3]
     kvs = refs[5 : 5 + n_sets]
-    m_ref, l_ref, e_ref, t_ref, kv, sum_ref, top_ref = refs[5 + n_sets :]
+    m_ref, l_ref, e_ref, t_ref, kv, sum_ref = refs[5 + n_sets :]
     m_ref[...] = refs[3][...]
     l_ref[...] = refs[4][...]
     take_sets(kv, kvs)
@@ -242,28 +242,26 @@
 
     def later_body(n, rho, half, size, kind, masked):
         rows, keys, vis = inputs(n, rho, half, size, kind, masked)
-        slot = (n * 4 + rho) * 2 + half
-        t_ref[slot] = m_ref[rho]
-        top_ref[...] = m_ref[rho]
-
-        def attempt(_):
-            ref = jnp.maximum(t_ref[slot], top_ref[...])
-            t_ref[slot] = ref
-            for p in range(4):
-                cols = slice(256 * p, 256 * p + 256)
-                s = scores(keys, rho, cols, vis)
-                e = jnp.exp2((s - t_ref[slot, :, cols]) * C2)
-                e_ref[n * 4 + rho, rows, cols] = e.astype(BF16)
-                sum_ref[:, cols] = jnp.sum(e, axis=0, keepdims=True)
-                top_ref[:, cols] = jnp.max(s, axis=0, keepdims=True)
-            return jnp.max((top_ref[...] - ref) * C2)
-
-        lax.while_loop(lambda over: over > 32.0, attempt, jnp.float32(64.0))
-        ref = t_ref[slot]
-        l_ref[rho] = l_ref[rho] * jnp.exp2((m_ref[rho] - ref) * C2) + sum_ref[...]
-        m_ref[rho] = ref
-
-    items(ks, (0, 1, 2, 3), tab, first_body if ks == (0,) else later_body, True)
+        t_ref[(n * 4 + rho) * 2 + half] = m_ref[rho]
+        for p in range(4):
+            cols = slice(256 * p, 256 * p + 256)
+            e = jnp.exp2((scores(keys, rho, cols, vis) - m_ref[rho, :, cols]) * C2)
+            e_ref[n * 4 + rho, rows, cols] = e.astype(BF16)
+            sum_ref[rho, :, cols] += jnp.sum(e, axis=0, keepdims=True)
+
+    def attempt(_):
+        sum_ref[...] = jnp.zeros_like(sum_ref)
+        items(ks, (0, 1, 2, 3), tab, later_body, True)
+        sums = sum_ref[...]
+        step = jnp.where(sums > 2.0**100, 80.0, jnp.where(sums > 2.0**40, 26.0, 0.0))
+        m_ref[...] += step * (1.0 / C2)
+        return jnp.max(step)
+
+    if ks == (0,):
+        items(ks, (0, 1, 2, 3), tab, first_body, True)
+    else:
+        lax.while_loop(lambda step: step > 0.0, attempt, jnp.float32(1.0))
+        l_ref[...] = l_ref[...] * jnp.exp2((refs[3][...] - m_ref[...]) * C2) + sum_ref[...]
 
 
 def grads_body(ks, rhos, first, last, *refs):
@@ -332,7 +330,11 @@
 def per_device(queries, keys, values, grad_out, saved_out, segment_ids, frame_flags):
     hop = functools.partial(lax.ppermute, axis_name="ctx")
     rank = lax.axis_index("ctx").astype(jnp.int32)
-    tab = jnp.stack([(rank >> 1) & 7, 2 * (rank >> 4) + (rank & 1)])
+
+    def place_of(rank):
+        return jnp.stack([(rank >> 1) & 7, 2 * (rank >> 4) + (rank & 1)])
+
+    tab = place_of(lax.optimization_barrier(rank))
     hbm = pl.BlockSpec(memory_space=pltpu.HBM)
 
     *parts, q_own = call(
@@ -342,7 +344,7 @@
             pltpu.VMEM((1, 128), jnp.int32), pltpu.SemaphoreType.DMA((5,)),
         ],
         vmem=58,
-    )(tab, keys[0], values[0], segment_ids, frame_flags, queries[0])
+    )(place_of(rank), keys[0], values[0], segment_ids, frame_flags, queries[0])
     got = [hop(parts[r], perm=flip(r)) for r in (1, 2, 3)]
     own_set = call(join_body, shape((NK + 16, 256)), [VM] * 4, nbytes=MIB)(parts[0], *got)
 
@@ -376,7 +378,7 @@
             functools.partial(stats_body, ks),
             [stat, stat, shape((4 * n, NK, NQ * H)), shape((8 * n, 1, NQ * H), F32)],
             [SM] + [VM] * (4 + n), vmem=3,
-            scratch=[pltpu.VMEM((n, NK + 16, 256), BF16)] + [pltpu.VMEM((1, NQ * H), F32)] * 2,
+            scratch=[pltpu.VMEM((n, NK + 16, 256), BF16)] + [pltpu.VMEM((4, 1, NQ * H), F32)],
             flops=n * (1 << 29), nbytes=2 * MIB,
         )(tab, tag, q_wide, m, l, *[sets[k] for k in ks])
         if step < 4:

time: 141 us -> 152 us (1.078)
  the two profiles are of different devices: /device:TPU:17 before, /device:TPU:5 now
where the time goes in v2:
time: 152 us
  starting transfers between devices  61.3 us (40%)
  Pallas kernels  50.3 us (33%)
  waiting for transfers between devices  36.2 us (24%)
  local copies, waits for them, and re-layouts  1.95 us (1%)
  other arithmetic  1.53 us (1%)
    pallas_call x6, Pallas kernels, grads(): call(functools.partial(grads_body, ks, rhos, first, last), ([piece, piece...  24.8 us
    pallas_call x5, Pallas kernels, per_device(): call(functools.partial(stats_body, ks), [stat, stat, shape((4 * n, NK, NQ...  19.4 us
    ppermute x3, starting transfers between devices, per_device(): down = hop(sends[1], perm=turn(-1))  14.4 us
    ppermute x6, starting transfers between devices, per_device(): fwd, bwd = (hop(fwd, perm=turn(1)), hop(bwd, perm=turn(-1)))  14.3 us
    ppermute x4, waiting for transfers between devices, per_device(): up = hop(sends[0], perm=turn(1))  14.2 us
    ppermute x2, starting transfers between devices, four(): return (x, hop(x, perm=flip(1)), other, last)  13.2 us
    ppermute x3, waiting for transfers between devices, per_device(): got = [hop(parts[r], perm=flip(r)) for r in (1, 2, 3)]  8.22 us
    ppermute x6, waiting for transfers between devices, per_device(): fwd, bwd = (hop(fwd, perm=turn(1)), hop(bwd, perm=turn(-1)))  6.36 us
  transfers between devices with their start and end apart: 32, of which 12 were waited for; matrix products, arithmetic and copies ran while one was open for 0% of the time, Pallas kernels for 26%

profile of v2, /device:TPU:5, one launch (start us, length us, event | category | flops | bytes accessed | tf_op | source)
XLA Modules:
  0.0 152.3 jit_solution(14356812482644232623)
XLA Ops:
  0.7 0.6 pad_add_fusion.1.tab
  1.3 2.6 %shard_map.96 = (bf16[144,256]{1,0:T(8,128)(2,1)}, bf16[144,256]{1,0:T(8,128)(2,1)}, bf16[144,256]{1,0:T(8,128)(2,1)}, bf16[144,256]{1,0:T(8,128)(2,1)}, bf16[144,1024]{1,0:T(8,128)(2,1)}) custom-call(s32[2]{0:T(128)} %pad_add_fusion.1.tab, bf16[512,128]{1,0:T(8,128)(2,1)} %bitcast.47, bf16[512,128]{1,0:T(8,128)(2,1)} %bitcast.48, s32[1,512]{1,0:T(1,128)} %seg_hbm.1, ...), custom_call_target="tpu_custom_call" | custom-call | bytes 1048576 | tf_op jit(solution)/shard_map/pallas_call | solution.py:340
  3.9 1.4 collective-permute-start.4
  5.3 1.0 collective-permute-start.6
  6.4 1.5 collective-permute-start.8
  7.9 5.8 %collective-permute-done.7.p2 = bf16[144,256]{1,0:T(8,128)(2,1)S(1)} collective-permute-done((bf16[144,256]{1,0:T(8,128)(2,1)}, bf16[144,256]{1,0:T(8,128)(2,1)S(1)}, u32[]{:S(2)}, u32[]{:S(2)}) %collective-permute-start.7) | collective-permute-done | bytes 73760 | tf_op jit(solution)/shard_map/ppermute | solution.py:348
  13.7 2.4 %collective-permute-done.8.p3 = bf16[144,256]{1,0:T(8,128)(2,1)S(1)} collective-permute-done((bf16[144,256]{1,0:T(8,128)(2,1)}, bf16[144,256]{1,0:T(8,128)(2,1)S(1)}, u32[]{:S(2)}, u32[]{:S(2)}) %collective-permute-start.8) | collective-permute-done | bytes 73760 | tf_op jit(solution)/shard_map/ppermute | solution.py:348
  16.1 0.9 copy-done.3
  17.0 1.7 %collective-permute-start.9 = (bf16[528,256]{1,0:T(8,128)(2,1)S(1)}, bf16[528,256]{1,0:T(8,128)(2,1)S(1)}, u32[]{:S(2)}, u32[]{:S(2)}) collective-permute-start(bf16[528,256]{1,0:T(8,128)(2,1)S(1)} %shard_map.98.refs_5_.refs_8_), channel_id=1, source_target_pairs={{0,2},{1,3},{2,4},{3,5},{4,6},{5,7},{6,8},{7,9},{8,10},{9,11},{10,... | collective-permute-start | bytes 811016 | tf_op jit(solution)/shard_map/ppermute | solution.py:374
  18.7 4.0 %collective-permute-start.11 = (bf16[528,256]{1,0:T(8,128)(2,1)S(1)}, bf16[528,256]{1,0:T(8,128)(2,1)S(1)}, u32[]{:S(2)}, u32[]{:S(2)}) collective-permute-start(bf16[528,256]{1,0:T(8,128)(2,1)S(1)} %shard_map.98.refs_5_.refs_8_), channel_id=1, source_target_pairs={{0,14},{1,15},{2,0},{3,1},{4,2},{5,3},{6,4},{7,5},{8,6},{9,7},{10,... | collective-permute-start | bytes 811016 | tf_op jit(solution)/shard_map/ppermute | solution.py:374
  23.3 6.3 %collective-permute-done.9.refs_6_.refs_9_ = bf16[528,256]{1,0:T(8,128)(2,1)S(1)} collective-permute-done((bf16[528,256]{1,0:T(8,128)(2,1)S(1)}, bf16[528,256]{1,0:T(8,128)(2,1)S(1)}, u32[]{:S(2)}, u32[]{:S(2)}) %collective-permute-start.9) | collective-permute-done | bytes 270368 | tf_op jit(solution)/shard_map/ppermute | solution.py:374
  29.6 2.7 %collective-permute-start.12 = (bf16[528,256]{1,0:T(8,128)(2,1)S(1)}, bf16[528,256]{1,0:T(8,128)(2,1)S(1)}, u32[]{:S(2)}, u32[]{:S(2)}) collective-permute-start(bf16[528,256]{1,0:T(8,128)(2,1)S(1)} %collective-permute-done.11.refs_5_.refs_8_), channel_id=1, source_target_pairs={{0,14},{1,15},{2,0},{3,1},{4,2},{5,3},{6,4},{7,5},{8,6},{9,7},{10,... | collective-permute-start | bytes 811016 | tf_op jit(solution)/shard_map/ppermute | solution.py:374
  32.4 1.0 copy-done
  33.3 0.9 shard_map.97
  34.3 4.0 %shard_map.99 = (f32[4,1,1024]{2,1,0:T(1,128)S(1)}, f32[4,1,1024]{2,1,0:T(1,128)S(1)}, bf16[4,512,1024]{2,1,0:T(8,128)(2,1)S(1)}, f32[8,1,1024]{2,1,0:T(1,128)S(1)}) custom-call(s32[2]{0:T(128)S(1)} %pad_add_fusion.refs_0_.tab, f32[4,1,1024]{2,1,0:T(1,128)S(1)} %get-tuple-element.75.refs_1_, bf16[4,128,1024]{2,1,0:T(8,128)(2,1)S(1)} %get-tuple-element.76.refs_2_, ...), custom_call_target="tpu_custom_call" | custom-call | flops 536870912 | bytes 2097152 | tf_op jit(solution)/shard_map/pallas_call | solution.py:377
  38.3 4.3 %shard_map.100 = (f32[4,1,1024]{2,1,0:T(1,128)S(1)}, f32[4,1,1024]{2,1,0:T(1,128)S(1)}, bf16[8,512,1024]{2,1,0:T(8,128)(2,1)S(1)}, f32[16,1,1024]{2,1,0:T(1,128)S(1)}) custom-call(s32[2]{0:T(128)S(1)} %pad_add_fusion.refs_0_.tab, f32[4,1,1024]{2,1,0:T(1,128)S(1)} %get-tuple-element.75.refs_1_, bf16[4,128,1024]{2,1,0:T(8,128)(2,1)S(1)} %get-tuple-element.76.refs_2_, ...), custom_call_target="tpu_custom_call" | custom-call | flops 1073741824 | bytes 2097152 | tf_op jit(solution)/shard_map/pallas_call | solution.py:377
  42.7 5.8 %collective-permute-start.14 = (bf16[528,256]{1,0:T(8,128)(2,1)S(1)}, bf16[528,256]{1,0:T(8,128)(2,1)S(1)}, u32[]{:S(2)}, u32[]{:S(2)}) collective-permute-start(bf16[528,256]{1,0:T(8,128)(2,1)S(1)} %collective-permute-done.12.refs_5_.refs_8_), channel_id=1, source_target_pairs={{0,14},{1,15},{2,0},{3,1},{4,2},{5,3},{6,4},{7,5},{8,6},{9,7},{10,... | collective-permute-start | bytes 811016 | tf_op jit(solution)/shard_map/ppermute | solution.py:374
  48.8 4.7 %shard_map.101 = (f32[4,1,1024]{2,1,0:T(1,128)S(1)}, f32[4,1,1024]{2,1,0:T(1,128)S(1)}, bf16[8,512,1024]{2,1,0:T(8,128)(2,1)S(1)}, f32[16,1,1024]{2,1,0:T(1,128)S(1)}) custom-call(s32[2]{0:T(128)S(1)} %pad_add_fusion.refs_0_.tab, f32[4,1,1024]{2,1,0:T(1,128)S(1)} %get-tuple-element.75.refs_1_, bf16[4,128,1024]{2,1,0:T(8,128)(2,1)S(1)} %get-tuple-element.76.refs_2_, ...), custom_call_target="tpu_custom_call" | custom-call | flops 1073741824 | bytes 2097152 | tf_op jit(solution)/shard_map/pallas_call | solution.py:377
  53.6 4.9 %collective-permute-start.15 = (bf16[528,256]{1,0:T(8,128)(2,1)S(1)}, bf16[528,256]{1,0:T(8,128)(2,1)S(1)}, u32[]{:S(2)}, u32[]{:S(2)}) collective-permute-start(bf16[528,256]{1,0:T(8,128)(2,1)S(1)} %collective-permute-done.14.refs_5_.refs_8_), channel_id=1, source_target_pairs={{0,14},{1,15},{2,0},{3,1},{4,2},{5,3},{6,4},{7,5},{8,6},{9,7},{10,... | collective-permute-start | bytes 811016 | tf_op jit(solution)/shard_map/ppermute | solution.py:376
  58.5 13.1 %collective-permute-start = (bf16[144,1024]{1,0:T(8,128)(2,1)S(1)}, bf16[144,1024]{1,0:T(8,128)(2,1)S(1)}, u32[]{:S(2)}, u32[]{:S(2)}) collective-permute-start(bf16[144,1024]{1,0:T(8,128)(2,1)S(1)} %shard_map.94.q0), channel_id=1, source_target_pairs={{0,1},{1,0},{2,3},{3,2},{4,5},{5,4},{6,7},{7,6},{8,9},{9,8},{10,11... | collective-permute-start | bytes 884744 | tf_op jit(solution)/shard_map/ppermute | solution.py:354
  71.5 4.7 %shard_map.102 = (f32[4,1,1024]{2,1,0:T(1,128)S(1)}, f32[4,1,1024]{2,1,0:T(1,128)S(1)}, bf16[8,512,1024]{2,1,0:T(8,128)(2,1)S(1)}, f32[16,1,1024]{2,1,0:T(1,128)S(1)}) custom-call(s32[2]{0:T(128)S(1)} %pad_add_fusion.refs_0_.tab, f32[4,1,1024]{2,1,0:T(1,128)S(1)} %get-tuple-element.75.refs_1_, bf16[4,128,1024]{2,1,0:T(8,128)(2,1)S(1)} %get-tuple-element.76.refs_2_, ...), custom_call_target="tpu_custom_call" | custom-call | flops 1073741824 | bytes 2097152 | tf_op jit(solution)/shard_map/pallas_call | solution.py:377
  76.3 1.7 %shard_map.103 = (f32[4,1,1024]{2,1,0:T(1,128)S(1)}, f32[4,1,1024]{2,1,0:T(1,128)S(1)}, bf16[4,512,1024]{2,1,0:T(8,128)(2,1)S(1)}, f32[8,1,1024]{2,1,0:T(1,128)S(1)}) custom-call(s32[2]{0:T(128)S(1)} %pad_add_fusion.refs_0_.tab, f32[4,1,1024]{2,1,0:T(1,128)S(1)} %get-tuple-element.75.refs_1_, bf16[4,128,1024]{2,1,0:T(8,128)(2,1)S(1)} %get-tuple-element.76.refs_2_, ...), custom_call_target="tpu_custom_call" | custom-call | flops 536870912 | bytes 2097152 | tf_op jit(solution)/shard_map/pallas_call | solution.py:377
  78.1 0.9 shard_map.95
  79.0 3.3 %collective-permute-start.18 = (f32[8,1,1024]{2,1,0:T(1,128)S(1)}, f32[8,1,1024]{2,1,0:T(1,128)S(1)}, u32[]{:S(2)}, u32[]{:S(2)}) collective-permute-start(f32[8,1,1024]{2,1,0:T(1,128)S(1)} %constant_dynamic-update-slice_fusion), channel_id=1, source_target_pairs={{0,17},{1,16},{2,19},{3,18},{4,21},{5,20},{6,23},{7,22},{8,25},{9,... | collective-permute-start | bytes 98312 | tf_op jit(solution)/shard_map/ppermute | solution.py:397
  82.3 1.6 %collective-permute-done.18 = f32[8,1,1024]{2,1,0:T(1,128)S(1)} collective-permute-done((f32[8,1,1024]{2,1,0:T(1,128)S(1)}, f32[8,1,1024]{2,1,0:T(1,128)S(1)}, u32[]{:S(2)}, u32[]{:S(2)}) %collective-permute-start.18) | collective-permute-done | bytes 32800 | tf_op jit(solution)/shard_map/ppermute | solution.py:397
  84.1 2.6 %shard_map.104 = (f32[4,128,1024]{2,1,0:T(8,128)S(1)}, f32[1,512,256]{2,1,0:T(8,128)S(1)}) custom-call(s32[2]{0:T(128)S(1)} %pad_add_fusion.refs_0_.tab, f32[4,1,1024]{2,1,0:T(1,128)S(1)} %get-tuple-element.73.refs_1_, f32[4,1,1024]{2,1,0:T(1,128)S(1)} %multiply_add_fusion.refs_2_, bf16[4,1024,128]{2,1,0:T(8,128)(2,1)S(1)} %get-tuple-element.102.refs_3_, ...), custom_call_target="tpu_custom_call" | custom-call | flops 2684354560 | bytes 8388608 | tf_op jit(solution)/shard_map/pallas_call | solution.py:415
  86.8 4.1 %shard_map.105 = (f32[4,128,1024]{2,1,0:T(8,128)S(1)}, f32[2,512,256]{2,1,0:T(8,128)S(1)}) custom-call(s32[2]{0:T(128)S(1)} %pad_add_fusion.refs_0_.tab, f32[4,1,1024]{2,1,0:T(1,128)S(1)} %get-tuple-element.73.refs_1_, f32[4,1,1024]{2,1,0:T(1,128)S(1)} %multiply_add_fusion.refs_2_, ...), custom_call_target="tpu_custom_call", output_to_operand_aliasing={{0}: (10, {})} | custom-call | flops 5368709120 | bytes 8388608 | tf_op jit(solution)/shard_map/pallas_call | solution.py:415
  90.9 7.3 %collective-permute-done.19 = bf16[512,256]{1,0:T(8,128)(2,1)S(1)} collective-permute-done((bf16[512,256]{1,0:T(8,128)(2,1)S(1)}, bf16[512,256]{1,0:T(8,128)(2,1)S(1)}, u32[]{:S(2)}, u32[]{:S(2)}) %collective-permute-start.19) | collective-permute-done | bytes 262176 | tf_op jit(solution)/shard_map/ppermute | solution.py:431
  98.3 6.2 %collective-permute-start.21 = (bf16[512,256]{1,0:T(8,128)(2,1)S(1)}, bf16[512,256]{1,0:T(8,128)(2,1)S(1)}, u32[]{:S(2)}, u32[]{:S(2)}) collective-permute-start(bf16[512,256]{1,0:T(8,128)(2,1)S(1)} %fusion.8), channel_id=1, source_target_pairs={{0,14},{1,15},{2,0},{3,1},{4,2},{5,3},{6,4},{7,5},{8,6},{9,7},{10,... | collective-permute-start | bytes 786440 | tf_op jit(solution)/shard_map/ppermute | solution.py:433
  104.5 4.0 %shard_map.106 = (f32[4,128,1024]{2,1,0:T(8,128)S(1)}, f32[2,512,256]{2,1,0:T(8,128)S(1)}) custom-call(s32[2]{0:T(128)S(1)} %pad_add_fusion.refs_0_.tab, f32[4,1,1024]{2,1,0:T(1,128)S(1)} %get-tuple-element.73.refs_1_, f32[4,1,1024]{2,1,0:T(1,128)S(1)} %multiply_add_fusion.refs_2_, ...), custom_call_target="tpu_custom_call", output_to_operand_aliasing={{0}: (10, {})} | custom-call | flops 5368709120 | bytes 8388608 | tf_op jit(solution)/shard_map/pallas_call | solution.py:415
  108.6 0.8 collective-permute-done.21
  109.4 3.1 %collective-permute-done.20 = bf16[512,256]{1,0:T(8,128)(2,1)S(1)} collective-permute-done((bf16[512,256]{1,0:T(8,128)(2,1)S(1)}, bf16[512,256]{1,0:T(8,128)(2,1)S(1)}, u32[]{:S(2)}, u32[]{:S(2)}) %collective-permute-start.20) | collective-permute-done | bytes 262176 | tf_op jit(solution)/shard_map/ppermute | solution.py:431
  112.7 3.5 %collective-permute-start.23 = (bf16[512,256]{1,0:T(8,128)(2,1)S(1)}, bf16[512,256]{1,0:T(8,128)(2,1)S(1)}, u32[]{:S(2)}, u32[]{:S(2)}) collective-permute-start(bf16[512,256]{1,0:T(8,128)(2,1)S(1)} %get-tuple-element.130), channel_id=1, source_target_pairs={{0,14},{1,15},{2,0},{3,1},{4,2},{5,3},{6,4},{7,5},{8,6},{9,7},{10,... | collective-permute-start | bytes 786440 | tf_op jit(solution)/shard_map/ppermute | solution.py:433
  116.2 6.8 %shard_map.107 = (f32[4,128,1024]{2,1,0:T(8,128)S(1)}, f32[2,512,256]{2,1,0:T(8,128)S(1)}) custom-call(s32[2]{0:T(128)S(1)} %pad_add_fusion.refs_0_.tab, f32[4,1,1024]{2,1,0:T(1,128)S(1)} %get-tuple-element.73.refs_1_, f32[4,1,1024]{2,1,0:T(1,128)S(1)} %multiply_add_fusion.refs_2_, ...), custom_call_target="tpu_custom_call", output_to_operand_aliasing={{0}: (10, {})} | custom-call | flops 5368709120 | bytes 8388608 | tf_op jit(solution)/shard_map/pallas_call | solution.py:415
  123.0 0.7 collective-permute-done.22
  123.8 4.3 %shard_map.108 = (bf16[128,1024]{1,0:T(8,128)(2,1)S(1)}, bf16[128,1024]{1,0:T(8,128)(2,1)S(1)}, f32[1,512,256]{2,1,0:T(8,128)S(1)}) custom-call(s32[2]{0:T(128)S(1)} %pad_add_fusion.refs_0_.tab, f32[4,1,1024]{2,1,0:T(1,128)S(1)} %get-tuple-element.73.refs_1_, f32[4,1,1024]{2,1,0:T(1,128)S(1)} %multiply_add_fusion.refs_2_, ...), custom_call_target="tpu_custom_call" | custom-call | flops 2684354560 | bytes 8388608 | tf_op jit(solution)/shard_map/pallas_call | solution.py:415
  128.2 2.6 %collective-permute-start.30 = (bf16[128,1024]{1,0:T(8,128)(2,1)S(1)}, bf16[128,1024]{1,0:T(8,128)(2,1)S(1)}, u32[]{:S(2)}, u32[]{:S(2)}) collective-permute-start(bf16[128,1024]{1,0:T(8,128)(2,1)S(1)} %get-tuple-element.139), channel_id=1, source_target_pairs={{0,1},{1,0},{2,3},{3,2},{4,5},{5,4},{6,7},{7,6},{8,9},{9,8},{10,11... | collective-permute-start | bytes 786440 | tf_op jit(solution)/shard_map/ppermute | solution.py:435
  130.7 4.7 %collective-permute-start.25 = (bf16[512,256]{1,0:T(8,128)(2,1)S(1)}, bf16[512,256]{1,0:T(8,128)(2,1)S(1)}, u32[]{:S(2)}, u32[]{:S(2)}) collective-permute-start(bf16[512,256]{1,0:T(8,128)(2,1)S(1)} %get-tuple-element.135), channel_id=1, source_target_pairs={{0,14},{1,15},{2,0},{3,1},{4,2},{5,3},{6,4},{7,5},{8,6},{9,7},{10,... | collective-permute-start | bytes 786440 | tf_op jit(solution)/shard_map/ppermute | solution.py:433
  135.4 3.0 %shard_map.109 = (bf16[128,1024]{1,0:T(8,128)(2,1)S(1)}, bf16[128,1024]{1,0:T(8,128)(2,1)S(1)}, f32[1,512,256]{2,1,0:T(8,128)S(1)}) custom-call(s32[2]{0:T(128)S(1)} %pad_add_fusion.refs_0_.tab, f32[4,1,1024]{2,1,0:T(1,128)S(1)} %get-tuple-element.73.refs_1_, f32[4,1,1024]{2,1,0:T(1,128)S(1)} %multiply_add_fusion.refs_2_, ...), custom_call_target="tpu_custom_call" | custom-call | flops 2684354560 | bytes 8388608 | tf_op jit(solution)/shard_map/pallas_call | solution.py:415
  138.5 0.5 collective-permute-start.29
  139.0 0.6 collective-permute-start.31
  139.6 1.4 collective-permute-done.25
  141.0 3.1 %collective-permute-done.24 = bf16[512,256]{1,0:T(8,128)(2,1)S(1)} collective-permute-done((bf16[512,256]{1,0:T(8,128)(2,1)S(1)}, bf16[512,256]{1,0:T(8,128)(2,1)S(1)}, u32[]{:S(2)}, u32[]{:S(2)}) %collective-permute-start.24) | collective-permute-done | bytes 262176 | tf_op jit(solution)/shard_map/ppermute | solution.py:431
  144.3 1.3 collective-permute-start.26
  145.6 1.7 %collective-permute-start.28 = (bf16[128,256]{1,0:T(8,128)(2,1)S(1)}, bf16[128,256]{1,0:T(8,128)(2,1)S(1)}, u32[]{:S(2)}, u32[]{:S(2)}) collective-permute-start(bf16[128,256]{1,0:T(8,128)(2,1)S(1)} %get-tuple-element.147), channel_id=1, source_target_pairs={{0,17},{1,16},{2,19},{3,18},{4,21},{5,20},{6,23},{7,22},{8,25},{9,... | collective-permute-start | bytes 196616 | tf_op jit(solution)/shard_map/ppermute | solution.py:443
  147.4 1.8 %collective-permute-done.27.a2 = bf16[128,256]{1,0:T(8,128)(2,1)S(1)} collective-permute-done((bf16[128,256]{1,0:T(8,128)(2,1)S(1)}, bf16[128,256]{1,0:T(8,128)(2,1)S(1)}, u32[]{:S(2)}, u32[]{:S(2)}) %collective-permute-start.27) | collective-permute-done | bytes 65568 | tf_op jit(solution)/shard_map/ppermute | solution.py:443
  149.2 1.7 %collective-permute-done.28.a3 = bf16[128,256]{1,0:T(8,128)(2,1)S(1)} collective-permute-done((bf16[128,256]{1,0:T(8,128)(2,1)S(1)}, bf16[128,256]{1,0:T(8,128)(2,1)S(1)}, u32[]{:S(2)}, u32[]{:S(2)}) %collective-permute-start.28) | collective-permute-done | bytes 65568 | tf_op jit(solution)/shard_map/ppermute | solution.py:443
  150.8 1.4 shard_map.110
  (60 shorter events, 2.4 us)
Async XLA Ops:
  0.6 47.9 %copy-start.1 = (bf16[1,128,1024]{2,1,0:T(8,128)(2,1)S(1)}, bf16[1,128,1024]{2,1,0:T(8,128)(2,1)}, u32[]{:S(2)}) copy-start(bf16[1,128,1024]{2,1,0:T(8,128)(2,1)} %param.10) | copy-start | bytes 786436
  0.6 47.8 %copy-start.2 = (bf16[1,128,1024]{2,1,0:T(8,128)(2,1)S(1)}, bf16[1,128,1024]{2,1,0:T(8,128)(2,1)}, u32[]{:S(2)}) copy-start(bf16[1,128,1024]{2,1,0:T(8,128)(2,1)} %param.11) | copy-start | bytes 786436
  3.9 19.0 %collective-permute-start.4 = (bf16[144,1024]{1,0:T(8,128)(2,1)}, bf16[144,1024]{1,0:T(8,128)(2,1)S(1)}, u32[]{:S(2)}, u32[]{:S(2)}) collective-permute-start(bf16[144,1024]{1,0:T(8,128)(2,1)} %get-tuple-element.74.q0), channel_id=1, source_target_pairs={{0,16},{1,17},{2,18},{3,19},{4,20},{5,21},{6,22},{7,23},{8,24},{9,... | collective-permute-start | bytes 884744 | tf_op jit(solution)/shard_map/ppermute | solution.py:352
  5.3 2.6 %collective-permute-start.6 = (bf16[144,256]{1,0:T(8,128)(2,1)}, bf16[144,256]{1,0:T(8,128)(2,1)S(1)}, u32[]{:S(2)}, u32[]{:S(2)}) collective-permute-start(bf16[144,256]{1,0:T(8,128)(2,1)} %get-tuple-element.78), channel_id=1, source_target_pairs={{0,1},{1,0},{2,3},{3,2},{4,5},{5,4},{6,7},{7,6},{8,9},{9,8},{10,11... | collective-permute-start | bytes 221192 | tf_op jit(solution)/shard_map/ppermute | solution.py:348
  6.2 7.4 %collective-permute-start.7 = (bf16[144,256]{1,0:T(8,128)(2,1)}, bf16[144,256]{1,0:T(8,128)(2,1)S(1)}, u32[]{:S(2)}, u32[]{:S(2)}) collective-permute-start(bf16[144,256]{1,0:T(8,128)(2,1)} %get-tuple-element.79), channel_id=1, source_target_pairs={{0,16},{1,17},{2,18},{3,19},{4,20},{5,21},{6,22},{7,23},{8,24},{9,... | collective-permute-start | bytes 221192 | tf_op jit(solution)/shard_map/ppermute | solution.py:348
  6.4 9.7 %collective-permute-start.8 = (bf16[144,256]{1,0:T(8,128)(2,1)}, bf16[144,256]{1,0:T(8,128)(2,1)S(1)}, u32[]{:S(2)}, u32[]{:S(2)}) collective-permute-start(bf16[144,256]{1,0:T(8,128)(2,1)} %get-tuple-element.80), channel_id=1, source_target_pairs={{0,17},{1,16},{2,19},{3,18},{4,21},{5,20},{6,23},{7,22},{8,25},{9,... | collective-permute-start | bytes 221192 | tf_op jit(solution)/shard_map/ppermute | solution.py:348
  16.1 0.9 copy-start.3
  17.0 12.6 %collective-permute-start.9 = (bf16[528,256]{1,0:T(8,128)(2,1)S(1)}, bf16[528,256]{1,0:T(8,128)(2,1)S(1)}, u32[]{:S(2)}, u32[]{:S(2)}) collective-permute-start(bf16[528,256]{1,0:T(8,128)(2,1)S(1)} %shard_map.98.refs_5_.refs_8_), channel_id=1, source_target_pairs={{0,2},{1,3},{2,4},{3,5},{4,6},{5,7},{6,8},{7,9},{8,10},{9,11},{10,... | collective-permute-start | bytes 811016 | tf_op jit(solution)/shard_map/ppermute | solution.py:374
  18.7 10.9 %collective-permute-start.11 = (bf16[528,256]{1,0:T(8,128)(2,1)S(1)}, bf16[528,256]{1,0:T(8,128)(2,1)S(1)}, u32[]{:S(2)}, u32[]{:S(2)}) collective-permute-start(bf16[528,256]{1,0:T(8,128)(2,1)S(1)} %shard_map.98.refs_5_.refs_8_), channel_id=1, source_target_pairs={{0,14},{1,15},{2,0},{3,1},{4,2},{5,3},{6,4},{7,5},{8,6},{9,7},{10,... | collective-permute-start | bytes 811016 | tf_op jit(solution)/shard_map/ppermute | solution.py:374
  22.7 9.6 %collective-permute-start.3 = (bf16[144,1024]{1,0:T(8,128)(2,1)}, bf16[144,1024]{1,0:T(8,128)(2,1)S(1)}, u32[]{:S(2)}, u32[]{:S(2)}) collective-permute-start(bf16[144,1024]{1,0:T(8,128)(2,1)} %get-tuple-element.74.q0), channel_id=1, source_target_pairs={{0,1},{1,0},{2,3},{3,2},{4,5},{5,4},{6,7},{7,6},{8,9},{9,8},{10,11... | collective-permute-start | bytes 884744 | tf_op jit(solution)/shard_map/ppermute | solution.py:354
  22.9 9.4 %collective-permute-start.5 = (bf16[144,1024]{1,0:T(8,128)(2,1)S(1)}, bf16[144,1024]{1,0:T(8,128)(2,1)S(1)}, u32[]{:S(2)}, u32[]{:S(2)}) collective-permute-start(bf16[144,1024]{1,0:T(8,128)(2,1)S(1)} %collective-permute-done.4.q2), channel_id=1, source_target_pairs={{0,1},{1,0},{2,3},{3,2},{4,5},{5,4},{6,7},{7,6},{8,9},{9,8},{10,11... | collective-permute-start | bytes 884744 | tf_op jit(solution)/shard_map/ppermute | solution.py:353
  29.6 13.0 %collective-permute-start.10 = (bf16[528,256]{1,0:T(8,128)(2,1)S(1)}, bf16[528,256]{1,0:T(8,128)(2,1)S(1)}, u32[]{:S(2)}, u32[]{:S(2)}) collective-permute-start(bf16[528,256]{1,0:T(8,128)(2,1)S(1)} %collective-permute-done.9.refs_6_.refs_9_), channel_id=1, source_target_pairs={{0,2},{1,3},{2,4},{3,5},{4,6},{5,7},{6,8},{7,9},{8,10},{9,11},{10,... | collective-permute-start | bytes 811016 | tf_op jit(solution)/shard_map/ppermute | solution.py:374
  29.6 13.0 %collective-permute-start.12 = (bf16[528,256]{1,0:T(8,128)(2,1)S(1)}, bf16[528,256]{1,0:T(8,128)(2,1)S(1)}, u32[]{:S(2)}, u32[]{:S(2)}) collective-permute-start(bf16[528,256]{1,0:T(8,128)(2,1)S(1)} %collective-permute-done.11.refs_5_.refs_8_), channel_id=1, source_target_pairs={{0,14},{1,15},{2,0},{3,1},{4,2},{5,3},{6,4},{7,5},{8,6},{9,7},{10,... | collective-permute-start | bytes 811016 | tf_op jit(solution)/shard_map/ppermute | solution.py:374
  32.4 1.0 copy-start
  42.6 10.9 %collective-permute-start.13 = (bf16[528,256]{1,0:T(8,128)(2,1)S(1)}, bf16[528,256]{1,0:T(8,128)(2,1)S(1)}, u32[]{:S(2)}, u32[]{:S(2)}) collective-permute-start(bf16[528,256]{1,0:T(8,128)(2,1)S(1)} %collective-permute-done.10.refs_6_.refs_9_), channel_id=1, source_target_pairs={{0,2},{1,3},{2,4},{3,5},{4,6},{5,7},{6,8},{7,9},{8,10},{9,11},{10,... | collective-permute-start | bytes 811016 | tf_op jit(solution)/shard_map/ppermute | solution.py:374
  42.7 10.8 %collective-permute-start.14 = (bf16[528,256]{1,0:T(8,128)(2,1)S(1)}, bf16[528,256]{1,0:T(8,128)(2,1)S(1)}, u32[]{:S(2)}, u32[]{:S(2)}) collective-permute-start(bf16[528,256]{1,0:T(8,128)(2,1)S(1)} %collective-permute-done.12.refs_5_.refs_8_), channel_id=1, source_target_pairs={{0,14},{1,15},{2,0},{3,1},{4,2},{5,3},{6,4},{7,5},{8,6},{9,7},{10,... | collective-permute-start | bytes 811016 | tf_op jit(solution)/shard_map/ppermute | solution.py:374
  48.7 22.8 %collective-permute-start.1 = (bf16[144,1024]{1,0:T(8,128)(2,1)S(1)}, bf16[144,1024]{1,0:T(8,128)(2,1)S(1)}, u32[]{:S(2)}, u32[]{:S(2)}) collective-permute-start(bf16[144,1024]{1,0:T(8,128)(2,1)S(1)} %shard_map.94.q0), channel_id=1, source_target_pairs={{0,16},{1,17},{2,18},{3,19},{4,20},{5,21},{6,22},{7,23},{8,24},{9,... | collective-permute-start | bytes 884744 | tf_op jit(solution)/shard_map/ppermute | solution.py:352
  53.6 22.7 %collective-permute-start.15 = (bf16[528,256]{1,0:T(8,128)(2,1)S(1)}, bf16[528,256]{1,0:T(8,128)(2,1)S(1)}, u32[]{:S(2)}, u32[]{:S(2)}) collective-permute-start(bf16[528,256]{1,0:T(8,128)(2,1)S(1)} %collective-permute-done.14.refs_5_.refs_8_), channel_id=1, source_target_pairs={{0,14},{1,15},{2,0},{3,1},{4,2},{5,3},{6,4},{7,5},{8,6},{9,7},{10,... | collective-permute-start | bytes 811016 | tf_op jit(solution)/shard_map/ppermute | solution.py:376
  58.5 19.6 %collective-permute-start = (bf16[144,1024]{1,0:T(8,128)(2,1)S(1)}, bf16[144,1024]{1,0:T(8,128)(2,1)S(1)}, u32[]{:S(2)}, u32[]{:S(2)}) collective-permute-start(bf16[144,1024]{1,0:T(8,128)(2,1)S(1)} %shard_map.94.q0), channel_id=1, source_target_pairs={{0,1},{1,0},{2,3},{3,2},{4,5},{5,4},{6,7},{7,6},{8,9},{9,8},{10,11... | collective-permute-start | bytes 884744 | tf_op jit(solution)/shard_map/ppermute | solution.py:354
  71.5 6.6 %collective-permute-start.2 = (bf16[144,1024]{1,0:T(8,128)(2,1)S(1)}, bf16[144,1024]{1,0:T(8,128)(2,1)S(1)}, u32[]{:S(2)}, u32[]{:S(2)}) collective-permute-start(bf16[144,1024]{1,0:T(8,128)(2,1)S(1)} %collective-permute-done.1.q2), channel_id=1, source_target_pairs={{0,1},{1,0},{2,3},{3,2},{4,5},{5,4},{6,7},{7,6},{8,9},{9,8},{10,11... | collective-permute-start | bytes 884744 | tf_op jit(solution)/shard_map/ppermute | solution.py:353
  78.0 4.3 %collective-permute-start.17 = (f32[8,1,1024]{2,1,0:T(1,128)S(1)}, f32[8,1,1024]{2,1,0:T(1,128)S(1)}, u32[]{:S(2)}, u32[]{:S(2)}) collective-permute-start(f32[8,1,1024]{2,1,0:T(1,128)S(1)} %constant_dynamic-update-slice_fusion), channel_id=1, source_target_pairs={{0,16},{1,17},{2,18},{3,19},{4,20},{5,21},{6,22},{7,23},{8,24},{9,... | collective-permute-start | bytes 98312 | tf_op jit(solution)/shard_map/ppermute | solution.py:397
  79.0 4.9 %collective-permute-start.18 = (f32[8,1,1024]{2,1,0:T(1,128)S(1)}, f32[8,1,1024]{2,1,0:T(1,128)S(1)}, u32[]{:S(2)}, u32[]{:S(2)}) collective-permute-start(f32[8,1,1024]{2,1,0:T(1,128)S(1)} %constant_dynamic-update-slice_fusion), channel_id=1, source_target_pairs={{0,17},{1,16},{2,19},{3,18},{4,21},{5,20},{6,23},{7,22},{8,25},{9,... | collective-permute-start | bytes 98312 | tf_op jit(solution)/shard_map/ppermute | solution.py:397
  82.3 1.6 %collective-permute-start.16 = (f32[8,1,1024]{2,1,0:T(1,128)S(1)}, f32[8,1,1024]{2,1,0:T(1,128)S(1)}, u32[]{:S(2)}, u32[]{:S(2)}) collective-permute-start(f32[8,1,1024]{2,1,0:T(1,128)S(1)} %constant_dynamic-update-slice_fusion), channel_id=1, source_target_pairs={{0,1},{1,0},{2,3},{3,2},{4,5},{5,4},{6,7},{7,6},{8,9},{9,8},{10,11... | collective-permute-start | bytes 98312 | tf_op jit(solution)/shard_map/ppermute | solution.py:397
  86.7 11.5 %collective-permute-start.19 = (bf16[512,256]{1,0:T(8,128)(2,1)S(1)}, bf16[512,256]{1,0:T(8,128)(2,1)S(1)}, u32[]{:S(2)}, u32[]{:S(2)}) collective-permute-start(bf16[512,256]{1,0:T(8,128)(2,1)S(1)} %convert_bitcast_fusion), channel_id=1, source_target_pairs={{0,2},{1,3},{2,4},{3,5},{4,6},{5,7},{6,8},{7,9},{8,10},{9,11},{10,... | collective-permute-start | bytes 786440 | tf_op jit(solution)/shard_map/ppermute | solution.py:431
  98.3 11.1 %collective-permute-start.21 = (bf16[512,256]{1,0:T(8,128)(2,1)S(1)}, bf16[512,256]{1,0:T(8,128)(2,1)S(1)}, u32[]{:S(2)}, u32[]{:S(2)}) collective-permute-start(bf16[512,256]{1,0:T(8,128)(2,1)S(1)} %fusion.8), channel_id=1, source_target_pairs={{0,14},{1,15},{2,0},{3,1},{4,2},{5,3},{6,4},{7,5},{8,6},{9,7},{10,... | collective-permute-start | bytes 786440 | tf_op jit(solution)/shard_map/ppermute | solution.py:433
  104.5 8.0 %collective-permute-start.20 = (bf16[512,256]{1,0:T(8,128)(2,1)S(1)}, bf16[512,256]{1,0:T(8,128)(2,1)S(1)}, u32[]{:S(2)}, u32[]{:S(2)}) collective-permute-start(bf16[512,256]{1,0:T(8,128)(2,1)S(1)} %fusion.7), channel_id=1, source_target_pairs={{0,2},{1,3},{2,4},{3,5},{4,6},{5,7},{6,8},{7,9},{8,10},{9,11},{10,... | collective-permute-start | bytes 786440 | tf_op jit(solution)/shard_map/ppermute | solution.py:431
  112.7 10.2 %collective-permute-start.23 = (bf16[512,256]{1,0:T(8,128)(2,1)S(1)}, bf16[512,256]{1,0:T(8,128)(2,1)S(1)}, u32[]{:S(2)}, u32[]{:S(2)}) collective-permute-start(bf16[512,256]{1,0:T(8,128)(2,1)S(1)} %get-tuple-element.130), channel_id=1, source_target_pairs={{0,14},{1,15},{2,0},{3,1},{4,2},{5,3},{6,4},{7,5},{8,6},{9,7},{10,... | collective-permute-start | bytes 786440 | tf_op jit(solution)/shard_map/ppermute | solution.py:433
  116.2 7.5 %collective-permute-start.22 = (bf16[512,256]{1,0:T(8,128)(2,1)S(1)}, bf16[512,256]{1,0:T(8,128)(2,1)S(1)}, u32[]{:S(2)}, u32[]{:S(2)}) collective-permute-start(bf16[512,256]{1,0:T(8,128)(2,1)S(1)} %get-tuple-element.129), channel_id=1, source_target_pairs={{0,2},{1,3},{2,4},{3,5},{4,6},{5,7},{6,8},{7,9},{8,10},{9,11},{10,... | collective-permute-start | bytes 786440 | tf_op jit(solution)/shard_map/ppermute | solution.py:431
  128.2 10.8 %collective-permute-start.30 = (bf16[128,1024]{1,0:T(8,128)(2,1)S(1)}, bf16[128,1024]{1,0:T(8,128)(2,1)S(1)}, u32[]{:S(2)}, u32[]{:S(2)}) collective-permute-start(bf16[128,1024]{1,0:T(8,128)(2,1)S(1)} %get-tuple-element.139), channel_id=1, source_target_pairs={{0,1},{1,0},{2,3},{3,2},{4,5},{5,4},{6,7},{7,6},{8,9},{9,8},{10,11... | collective-permute-start | bytes 786440 | tf_op jit(solution)/shard_map/ppermute | solution.py:435
  130.7 10.3 %collective-permute-start.25 = (bf16[512,256]{1,0:T(8,128)(2,1)S(1)}, bf16[512,256]{1,0:T(8,128)(2,1)S(1)}, u32[]{:S(2)}, u32[]{:S(2)}) collective-permute-start(bf16[512,256]{1,0:T(8,128)(2,1)S(1)} %get-tuple-element.135), channel_id=1, source_target_pairs={{0,14},{1,15},{2,0},{3,1},{4,2},{5,3},{6,4},{7,5},{8,6},{9,7},{10,... | collective-permute-start | bytes 786440 | tf_op jit(solution)/shard_map/ppermute | solution.py:433
  135.4 8.7 %collective-permute-start.24 = (bf16[512,256]{1,0:T(8,128)(2,1)S(1)}, bf16[512,256]{1,0:T(8,128)(2,1)S(1)}, u32[]{:S(2)}, u32[]{:S(2)}) collective-permute-start(bf16[512,256]{1,0:T(8,128)(2,1)S(1)} %get-tuple-element.134), channel_id=1, source_target_pairs={{0,2},{1,3},{2,4},{3,5},{4,6},{5,7},{6,8},{7,9},{8,10},{9,11},{10,... | collective-permute-start | bytes 786440 | tf_op jit(solution)/shard_map/ppermute | solution.py:431
  138.5 8.9 %collective-permute-start.29 = (bf16[128,1024]{1,0:T(8,128)(2,1)S(1)}, bf16[128,1024]{1,0:T(8,128)(2,1)S(1)}, u32[]{:S(2)}, u32[]{:S(2)}) collective-permute-start(bf16[128,1024]{1,0:T(8,128)(2,1)S(1)} %get-tuple-element.137), channel_id=1, source_target_pairs={{0,1},{1,0},{2,3},{3,2},{4,5},{5,4},{6,7},{7,6},{8,9},{9,8},{10,11... | collective-permute-start | bytes 786440 | tf_op jit(solution)/shard_map/ppermute | solution.py:442
  139.0 11.8 %collective-permute-start.31 = (bf16[128,1024]{1,0:T(8,128)(2,1)S(1)}, bf16[128,1024]{1,0:T(8,128)(2,1)S(1)}, u32[]{:S(2)}, u32[]{:S(2)}) collective-permute-start(bf16[128,1024]{1,0:T(8,128)(2,1)S(1)} %add_convert_fusion), channel_id=1, source_target_pairs={{0,16},{1,17},{2,18},{3,19},{4,20},{5,21},{6,22},{7,23},{8,24},{9,... | collective-permute-start | bytes 786440 | tf_op jit(solution)/shard_map/ppermute | solution.py:437
  144.3 3.1 %collective-permute-start.26 = (bf16[128,256]{1,0:T(8,128)(2,1)S(1)}, bf16[128,256]{1,0:T(8,128)(2,1)S(1)}, u32[]{:S(2)}, u32[]{:S(2)}) collective-permute-start(bf16[128,256]{1,0:T(8,128)(2,1)S(1)} %get-tuple-element.149), channel_id=1, source_target_pairs={{0,1},{1,0},{2,3},{3,2},{4,5},{5,4},{6,7},{7,6},{8,9},{9,8},{10,11... | collective-permute-start | bytes 196616 | tf_op jit(solution)/shard_map/ppermute | solution.py:443
  145.6 3.5 %collective-permute-start.27 = (bf16[128,256]{1,0:T(8,128)(2,1)S(1)}, bf16[128,256]{1,0:T(8,128)(2,1)S(1)}, u32[]{:S(2)}, u32[]{:S(2)}) collective-permute-start(bf16[128,256]{1,0:T(8,128)(2,1)S(1)} %get-tuple-element.148), channel_id=1, source_target_pairs={{0,16},{1,17},{2,18},{3,19},{4,20},{5,21},{6,22},{7,23},{8,24},{9,... | collective-permute-start | bytes 196616 | tf_op jit(solution)/shard_map/ppermute | solution.py:443
  145.6 5.2 %collective-permute-start.28 = (bf16[128,256]{1,0:T(8,128)(2,1)S(1)}, bf16[128,256]{1,0:T(8,128)(2,1)S(1)}, u32[]{:S(2)}, u32[]{:S(2)}) collective-permute-start(bf16[128,256]{1,0:T(8,128)(2,1)S(1)} %get-tuple-element.147), channel_id=1, source_target_pairs={{0,17},{1,16},{2,19},{3,18},{4,21},{5,20},{6,23},{7,22},{8,25},{9,... | collective-permute-start | bytes 196616 | tf_op jit(solution)/shard_map/ppermute | solution.py:443

commit v3 on v2

--- a/solution.py
+++ b/solution.py
@@ -171,7 +171,7 @@
     return jnp.concatenate([both, both], axis=1) > 0.5
 
 
-def items(ks, rhos, tab, body, masks):
+def items(ks, rhos, tab, tag_ref, kv, body, masks):
     edge = 0 in ks or 1 in ks
     own = ks == (0,)
 
@@ -183,8 +183,16 @@
 
         def one(half, _):
             kind = item_kind(tab, z_keys, half, rho)
-            full, some = kind[3:]
+            p0, p1, first, full, some = kind
             if edge:
+
+                def framed():
+                    which = lax.broadcasted_iota(jnp.int32, (16, 128), 0) >> 1
+                    least = jnp.min(jnp.where(which == half, kv[n, NK:, 0:128].astype(F32), 1e9))
+                    return (least <= jnp.max(tag_ref[rho, :, 0:128])).astype(jnp.int32)
+
+                past = jnp.minimum(p0, p1) > first + NQ - 1
+                some = some & (lax.cond(some & past, framed, lambda: jnp.int32(1)) > 0)
                 pl.when(full | some)(lambda: body(n, rho, half, NK // 2, kind, masks))
             else:
                 pl.when(full)(lambda: body(n, rho, half, NK // 2, kind, False))
@@ -251,14 +259,14 @@
 
     def attempt(_):
         sum_ref[...] = jnp.zeros_like(sum_ref)
-        items(ks, (0, 1, 2, 3), tab, later_body, True)
+        items(ks, (0, 1, 2, 3), tab, tag_ref, kv, later_body, True)
         sums = sum_ref[...]
         step = jnp.where(sums > 2.0**100, 80.0, jnp.where(sums > 2.0**40, 26.0, 0.0))
         m_ref[...] += step * (1.0 / C2)
         return jnp.max(step)
 
     if ks == (0,):
-        items(ks, (0, 1, 2, 3), tab, first_body, True)
+        items(ks, (0, 1, 2, 3), tab, tag_ref, kv, first_body, True)
     else:
         lax.while_loop(lambda step: step > 0.0, attempt, jnp.float32(1.0))
         l_ref[...] = l_ref[...] * jnp.exp2((refs[3][...] - m_ref[...]) * C2) + sum_ref[...]
@@ -266,8 +274,8 @@
 
 def grads_body(ks, rhos, first, last, *refs):
     n_sets = len(ks)
-    tab, mean_ref, log_ref, qt_ref, gw_ref, gt_ref, e_ref, t_ref = refs[:8]
-    kvs, rest = refs[8 : 8 + n_sets], refs[8 + n_sets :]
+    tab, tag_ref, mean_ref, log_ref, qt_ref, gw_ref, gt_ref, e_ref, t_ref = refs[:9]
+    kvs, rest = refs[9 : 9 + n_sets], refs[9 + n_sets :]
     if first:
         dq_ref, acc, kv, p_all, d_all = rest
 
@@ -307,7 +315,7 @@
         acc[n, rows, HD:] += dot_nn(p_all[0:size, :], gt_ref[rho])
         dq_ref[rho - rhos[0]] += dot_tn(keys, d)
 
-    items(ks, rhos, tab, body, False)
+    items(ks, rhos, tab, tag_ref, kv, body, False)
     if last:
 
         def head(h):
@@ -373,7 +381,8 @@
         if step < 3:
             fwd, bwd = hop(fwd, perm=turn(1)), hop(bwd, perm=turn(-1))
         elif step == 3:
-            bwd = hop(bwd, perm=turn(-1))
+            low, high = hop(fwd[0:272], perm=turn(1)), hop(bwd[272:], perm=turn(-1))
+            fwd, bwd = low, high
         m, l, *kept[ks] = call(
             functools.partial(stats_body, ks),
             [stat, stat, shape((4 * n, NK, NQ * H)), shape((8 * n, 1, NQ * H), F32)],
@@ -384,9 +393,10 @@
         if step < 4:
             if step > 0:
                 fwd, bwd, m, l = lax.optimization_barrier((fwd, bwd, m, l))
-            sets[step + 1] = bwd
             if step < 3:
-                sets[-step - 1] = fwd
+                sets[step + 1], sets[-step - 1] = bwd, fwd
+            else:
+                sets[4] = jnp.concatenate([fwd, bwd], axis=0)
         if step == 0:
             g_four = four(g_own)
     g_tall, g_wide, mean = turned(g_four, 3)
@@ -408,7 +418,7 @@
     def grads(ks, rhos, dq):
         n = len(ks)
         first, last = dq is None, ks == (0,)
-        args = [tab, mean, log_total, q_tall, g_wide, g_tall, *kept[ks]] + [sets[k] for k in ks]
+        args = [tab, tag, mean, log_total, q_tall, g_wide, g_tall, *kept[ks]] + [sets[k] for k in ks]
         args += [] if first else [dq]
         piece = shape((NQ, H * HD))
         scratch = [pltpu.VMEM((n, NK + 16, 256), BF16)] + [pltpu.VMEM((NK, NQ * H), BF16)] * 2

time: 152 us -> 152 us (level)
  Pallas kernels: 50.3 us -> 47.5 us
  waiting for transfers between devices: 36.2 us -> 38.8 us
    ppermute x4, waiting for transfers between devices: 14.2 us -> 16.8 us  [per_device(): up = hop(sends[0], perm=turn(1))]
    pallas_call x6, Pallas kernels: 24.8 us -> 22.7 us  [grads(): call(functools.partial(grads_body, ks, rhos, first, last), ([piece, piece...]
    ppermute x1 -> x2, starting transfers between devices: 4.92 us -> 5.19 us  [per_device(): low, high = (hop(fwd[0:272], perm=turn(1)), hop(bwd[272:], perm=turn(-1)))]
  transfers between devices with their start and end apart: 32 -> 33, of which waited for: 12 -> 12; matrix products, arithmetic and copies ran while one was open for 0% -> 0% of each run, Pallas kernels for 26% -> 24%
where the time goes in v3:
time: 152 us
  starting transfers between devices  61 us (40%)
  Pallas kernels  47.5 us (31%)
  waiting for transfers between devices  38.8 us (26%)
  local copies, waits for them, and re-layouts  1.99 us (1%)
    pallas_call x6, Pallas kernels, grads(): call(functools.partial(grads_body, ks, rhos, first, last), ([piece, piece...  22.7 us
    pallas_call x5, Pallas kernels, per_device(): call(functools.partial(stats_body, ks), [stat, stat, shape((4 * n, NK, NQ...  18.6 us
    ppermute x4, waiting for transfers between devices, per_device(): up = hop(sends[0], perm=turn(1))  16.8 us
    ppermute x3, starting transfers between devices, per_device(): down = hop(sends[1], perm=turn(-1))  14.7 us
    ppermute x6, starting transfers between devices, per_device(): fwd, bwd = (hop(fwd, perm=turn(1)), hop(bwd, perm=turn(-1)))  14.3 us
    ppermute x2, starting transfers between devices, four(): return (x, hop(x, perm=flip(1)), other, last)  12.4 us
    ppermute x3, waiting for transfers between devices, per_device(): got = [hop(parts[r], perm=flip(r)) for r in (1, 2, 3)]  8.22 us
    ppermute x6, waiting for transfers between devices, per_device(): fwd, bwd = (hop(fwd, perm=turn(1)), hop(bwd, perm=turn(-1)))  6.36 us
  transfers between devices with their start and end apart: 33, of which 12 were waited for; matrix products, arithmetic and copies ran while one was open for 0% of the time, Pallas kernels for 24%

profile of v3, /device:TPU:5, one launch (start us, length us, event | category | flops | bytes accessed | tf_op | source)
XLA Modules:
  0.0 151.7 jit_solution(12705469496260064903)
XLA Ops:
  0.7 0.6 pad_add_fusion.1.tab
  1.3 2.6 %shard_map.94 = (bf16[144,256]{1,0:T(8,128)(2,1)}, bf16[144,256]{1,0:T(8,128)(2,1)}, bf16[144,256]{1,0:T(8,128)(2,1)}, bf16[144,256]{1,0:T(8,128)(2,1)}, bf16[144,1024]{1,0:T(8,128)(2,1)}) custom-call(s32[2]{0:T(128)} %pad_add_fusion.1.tab, bf16[512,128]{1,0:T(8,128)(2,1)} %bitcast.47, bf16[512,128]{1,0:T(8,128)(2,1)} %bitcast.48, s32[1,512]{1,0:T(1,128)} %seg_hbm.1, ...), custom_call_target="tpu_custom_call" | custom-call | bytes 1048576 | tf_op jit(solution)/shard_map/pallas_call | solution.py:348
  3.9 1.4 collective-permute-start.1
  5.3 1.0 collective-permute-start.6
  6.4 1.5 collective-permute-start.8
  7.9 5.8 %collective-permute-done.7.p2 = bf16[144,256]{1,0:T(8,128)(2,1)S(1)} collective-permute-done((bf16[144,256]{1,0:T(8,128)(2,1)}, bf16[144,256]{1,0:T(8,128)(2,1)S(1)}, u32[]{:S(2)}, u32[]{:S(2)}) %collective-permute-start.7) | collective-permute-done | bytes 73760 | tf_op jit(solution)/shard_map/ppermute | solution.py:356
  13.7 2.4 %collective-permute-done.8.p3 = bf16[144,256]{1,0:T(8,128)(2,1)S(1)} collective-permute-done((bf16[144,256]{1,0:T(8,128)(2,1)}, bf16[144,256]{1,0:T(8,128)(2,1)S(1)}, u32[]{:S(2)}, u32[]{:S(2)}) %collective-permute-start.8) | collective-permute-done | bytes 73760 | tf_op jit(solution)/shard_map/ppermute | solution.py:356
  16.1 0.9 copy-done.3
  17.0 1.7 %collective-permute-start.9 = (bf16[528,256]{1,0:T(8,128)(2,1)S(1)}, bf16[528,256]{1,0:T(8,128)(2,1)S(1)}, u32[]{:S(2)}, u32[]{:S(2)}) collective-permute-start(bf16[528,256]{1,0:T(8,128)(2,1)S(1)} %shard_map.98.refs_5_.refs_9_), channel_id=1, source_target_pairs={{0,2},{1,3},{2,4},{3,5},{4,6},{5,7},{6,8},{7,9},{8,10},{9,11},{10,... | collective-permute-start | bytes 811016 | tf_op jit(solution)/shard_map/ppermute | solution.py:382
  18.7 4.0 %collective-permute-start.11 = (bf16[528,256]{1,0:T(8,128)(2,1)S(1)}, bf16[528,256]{1,0:T(8,128)(2,1)S(1)}, u32[]{:S(2)}, u32[]{:S(2)}) collective-permute-start(bf16[528,256]{1,0:T(8,128)(2,1)S(1)} %shard_map.98.refs_5_.refs_9_), channel_id=1, source_target_pairs={{0,14},{1,15},{2,0},{3,1},{4,2},{5,3},{6,4},{7,5},{8,6},{9,7},{10,... | collective-permute-start | bytes 811016 | tf_op jit(solution)/shard_map/ppermute | solution.py:382
  23.2 6.3 %collective-permute-done.9.refs_6_.refs_10_ = bf16[528,256]{1,0:T(8,128)(2,1)S(1)} collective-permute-done((bf16[528,256]{1,0:T(8,128)(2,1)S(1)}, bf16[528,256]{1,0:T(8,128)(2,1)S(1)}, u32[]{:S(2)}, u32[]{:S(2)}) %collective-permute-start.9) | collective-permute-done | bytes 270368 | tf_op jit(solution)/shard_map/ppermute | solution.py:382
  29.6 2.7 %collective-permute-start.12 = (bf16[528,256]{1,0:T(8,128)(2,1)S(1)}, bf16[528,256]{1,0:T(8,128)(2,1)S(1)}, u32[]{:S(2)}, u32[]{:S(2)}) collective-permute-start(bf16[528,256]{1,0:T(8,128)(2,1)S(1)} %collective-permute-done.11.refs_5_.refs_9_), channel_id=1, source_target_pairs={{0,14},{1,15},{2,0},{3,1},{4,2},{5,3},{6,4},{7,5},{8,6},{9,7},{10,... | collective-permute-start | bytes 811016 | tf_op jit(solution)/shard_map/ppermute | solution.py:382
  32.4 1.0 copy-done
  33.3 0.9 shard_map.95
  34.3 4.1 %shard_map.99 = (f32[4,1,1024]{2,1,0:T(1,128)S(1)}, f32[4,1,1024]{2,1,0:T(1,128)S(1)}, bf16[4,512,1024]{2,1,0:T(8,128)(2,1)S(1)}, f32[8,1,1024]{2,1,0:T(1,128)S(1)}) custom-call(s32[2]{0:T(128)S(1)} %pad_add_fusion.refs_0_.tab, f32[4,1,1024]{2,1,0:T(1,128)S(1)} %get-tuple-element.75.refs_1_, bf16[4,128,1024]{2,1,0:T(8,128)(2,1)S(1)} %get-tuple-element.77.refs_2_, ...), custom_call_target="tpu_custom_call" | custom-call | flops 536870912 | bytes 2097152 | tf_op jit(solution)/shard_map/pallas_call | solution.py:386
  38.3 3.5 %shard_map.100 = (f32[4,1,1024]{2,1,0:T(1,128)S(1)}, f32[4,1,1024]{2,1,0:T(1,128)S(1)}, bf16[8,512,1024]{2,1,0:T(8,128)(2,1)S(1)}, f32[16,1,1024]{2,1,0:T(1,128)S(1)}) custom-call(s32[2]{0:T(128)S(1)} %pad_add_fusion.refs_0_.tab, f32[4,1,1024]{2,1,0:T(1,128)S(1)} %get-tuple-element.75.refs_1_, bf16[4,128,1024]{2,1,0:T(8,128)(2,1)S(1)} %get-tuple-element.77.refs_2_, ...), custom_call_target="tpu_custom_call" | custom-call | flops 1073741824 | bytes 2097152 | tf_op jit(solution)/shard_map/pallas_call | solution.py:386
  41.9 5.8 %collective-permute-start.14 = (bf16[528,256]{1,0:T(8,128)(2,1)S(1)}, bf16[528,256]{1,0:T(8,128)(2,1)S(1)}, u32[]{:S(2)}, u32[]{:S(2)}) collective-permute-start(bf16[528,256]{1,0:T(8,128)(2,1)S(1)} %collective-permute-done.12.refs_5_.refs_9_), channel_id=1, source_target_pairs={{0,14},{1,15},{2,0},{3,1},{4,2},{5,3},{6,4},{7,5},{8,6},{9,7},{10,... | collective-permute-start | bytes 811016 | tf_op jit(solution)/shard_map/ppermute | solution.py:382
  48.0 4.7 %shard_map.101 = (f32[4,1,1024]{2,1,0:T(1,128)S(1)}, f32[4,1,1024]{2,1,0:T(1,128)S(1)}, bf16[8,512,1024]{2,1,0:T(8,128)(2,1)S(1)}, f32[16,1,1024]{2,1,0:T(1,128)S(1)}) custom-call(s32[2]{0:T(128)S(1)} %pad_add_fusion.refs_0_.tab, f32[4,1,1024]{2,1,0:T(1,128)S(1)} %get-tuple-element.75.refs_1_, bf16[4,128,1024]{2,1,0:T(8,128)(2,1)S(1)} %get-tuple-element.77.refs_2_, ...), custom_call_target="tpu_custom_call" | custom-call | flops 1073741824 | bytes 2097152 | tf_op jit(solution)/shard_map/pallas_call | solution.py:386
  52.9 5.1 %collective-permute-start.16 = (bf16[256,256]{1,0:T(8,128)(2,1)S(1)}, bf16[256,256]{1,0:T(8,128)(2,1)S(1)}, u32[]{:S(2)}, u32[]{:S(2)}) collective-permute-start(bf16[256,256]{1,0:T(8,128)(2,1)S(1)} %slice.106), channel_id=1, source_target_pairs={{0,14},{1,15},{2,0},{3,1},{4,2},{5,3},{6,4},{7,5},{8,6},{9,7},{10,... | collective-permute-start | bytes 393224 | tf_op jit(solution)/shard_map/ppermute | solution.py:384
  58.0 12.2 %collective-permute-start.3 = (bf16[144,1024]{1,0:T(8,128)(2,1)S(1)}, bf16[144,1024]{1,0:T(8,128)(2,1)S(1)}, u32[]{:S(2)}, u32[]{:S(2)}) collective-permute-start(bf16[144,1024]{1,0:T(8,128)(2,1)S(1)} %shard_map.96.q0), channel_id=1, source_target_pairs={{0,1},{1,0},{2,3},{3,2},{4,5},{5,4},{6,7},{7,6},{8,9},{9,8},{10,11... | collective-permute-start | bytes 884744 | tf_op jit(solution)/shard_map/ppermute | solution.py:362
  70.2 4.7 %shard_map.102 = (f32[4,1,1024]{2,1,0:T(1,128)S(1)}, f32[4,1,1024]{2,1,0:T(1,128)S(1)}, bf16[8,512,1024]{2,1,0:T(8,128)(2,1)S(1)}, f32[16,1,1024]{2,1,0:T(1,128)S(1)}) custom-call(s32[2]{0:T(128)S(1)} %pad_add_fusion.refs_0_.tab, f32[4,1,1024]{2,1,0:T(1,128)S(1)} %get-tuple-element.75.refs_1_, bf16[4,128,1024]{2,1,0:T(8,128)(2,1)S(1)} %get-tuple-element.77.refs_2_, ...), custom_call_target="tpu_custom_call" | custom-call | flops 1073741824 | bytes 2097152 | tf_op jit(solution)/shard_map/pallas_call | solution.py:386
  75.0 1.7 %shard_map.103 = (f32[4,1,1024]{2,1,0:T(1,128)S(1)}, f32[4,1,1024]{2,1,0:T(1,128)S(1)}, bf16[4,512,1024]{2,1,0:T(8,128)(2,1)S(1)}, f32[8,1,1024]{2,1,0:T(1,128)S(1)}) custom-call(s32[2]{0:T(128)S(1)} %pad_add_fusion.refs_0_.tab, f32[4,1,1024]{2,1,0:T(1,128)S(1)} %get-tuple-element.75.refs_1_, bf16[4,128,1024]{2,1,0:T(8,128)(2,1)S(1)} %get-tuple-element.77.refs_2_, ...), custom_call_target="tpu_custom_call" | custom-call | flops 536870912 | bytes 2097152 | tf_op jit(solution)/shard_map/pallas_call | solution.py:386
  76.9 0.9 shard_map.97
  77.8 3.3 %collective-permute-start.19 = (f32[8,1,1024]{2,1,0:T(1,128)S(1)}, f32[8,1,1024]{2,1,0:T(1,128)S(1)}, u32[]{:S(2)}, u32[]{:S(2)}) collective-permute-start(f32[8,1,1024]{2,1,0:T(1,128)S(1)} %constant_dynamic-update-slice_fusion.2), channel_id=1, source_target_pairs={{0,17},{1,16},{2,19},{3,18},{4,21},{5,20},{6,23},{7,22},{8,25},{9,... | collective-permute-start | bytes 98312 | tf_op jit(solution)/shard_map/ppermute | solution.py:407
  81.1 1.6 %collective-permute-done.19 = f32[8,1,1024]{2,1,0:T(1,128)S(1)} collective-permute-done((f32[8,1,1024]{2,1,0:T(1,128)S(1)}, f32[8,1,1024]{2,1,0:T(1,128)S(1)}, u32[]{:S(2)}, u32[]{:S(2)}) %collective-permute-start.19) | collective-permute-done | bytes 32800 | tf_op jit(solution)/shard_map/ppermute | solution.py:407
  82.9 2.6 %shard_map.104 = (f32[4,128,1024]{2,1,0:T(8,128)S(1)}, f32[1,512,256]{2,1,0:T(8,128)S(1)}) custom-call(s32[2]{0:T(128)S(1)} %pad_add_fusion.refs_0_.tab, f32[4,1,1024]{2,1,0:T(1,128)S(1)} %get-tuple-element.75.refs_1_, f32[4,1,1024]{2,1,0:T(1,128)S(1)} %get-tuple-element.76.refs_2_, f32[4,1,1024]{2,1,0:T(1,128)S(1)} %multiply_add_fusion.refs_3_, ...), custom_call_target="tpu_custom_call" | custom-call | flops 2684354560 | bytes 8388608 | tf_op jit(solution)/shard_map/pallas_call | solution.py:425
  85.6 4.0 %shard_map.105 = (f32[4,128,1024]{2,1,0:T(8,128)S(1)}, f32[2,512,256]{2,1,0:T(8,128)S(1)}) custom-call(s32[2]{0:T(128)S(1)} %pad_add_fusion.refs_0_.tab, f32[4,1,1024]{2,1,0:T(1,128)S(1)} %get-tuple-element.75.refs_1_, f32[4,1,1024]{2,1,0:T(1,128)S(1)} %get-tuple-element.76.refs_2_, ...), custom_call_target="tpu_custom_call", output_to_operand_aliasing={{0}: (11, {})} | custom-call | flops 5368709120 | bytes 8388608 | tf_op jit(solution)/shard_map/pallas_call | solution.py:425
  89.7 7.7 %collective-permute-done.20 = bf16[512,256]{1,0:T(8,128)(2,1)S(1)} collective-permute-done((bf16[512,256]{1,0:T(8,128)(2,1)S(1)}, bf16[512,256]{1,0:T(8,128)(2,1)S(1)}, u32[]{:S(2)}, u32[]{:S(2)}) %collective-permute-start.20) | collective-permute-done | bytes 262176 | tf_op jit(solution)/shard_map/ppermute | solution.py:441
  97.5 7.5 %collective-permute-start.22 = (bf16[512,256]{1,0:T(8,128)(2,1)S(1)}, bf16[512,256]{1,0:T(8,128)(2,1)S(1)}, u32[]{:S(2)}, u32[]{:S(2)}) collective-permute-start(bf16[512,256]{1,0:T(8,128)(2,1)S(1)} %fusion.8), channel_id=1, source_target_pairs={{0,14},{1,15},{2,0},{3,1},{4,2},{5,3},{6,4},{7,5},{8,6},{9,7},{10,... | collective-permute-start | bytes 786440 | tf_op jit(solution)/shard_map/ppermute | solution.py:443
  105.1 4.0 %shard_map.106 = (f32[4,128,1024]{2,1,0:T(8,128)S(1)}, f32[2,512,256]{2,1,0:T(8,128)S(1)}) custom-call(s32[2]{0:T(128)S(1)} %pad_add_fusion.refs_0_.tab, f32[4,1,1024]{2,1,0:T(1,128)S(1)} %get-tuple-element.75.refs_1_, f32[4,1,1024]{2,1,0:T(1,128)S(1)} %get-tuple-element.76.refs_2_, ...), custom_call_target="tpu_custom_call", output_to_operand_aliasing={{0}: (11, {})} | custom-call | flops 5368709120 | bytes 8388608 | tf_op jit(solution)/shard_map/pallas_call | solution.py:425
  109.1 0.9 collective-permute-done.22
  109.9 3.1 %collective-permute-done.21 = bf16[512,256]{1,0:T(8,128)(2,1)S(1)} collective-permute-done((bf16[512,256]{1,0:T(8,128)(2,1)S(1)}, bf16[512,256]{1,0:T(8,128)(2,1)S(1)}, u32[]{:S(2)}, u32[]{:S(2)}) %collective-permute-start.21) | collective-permute-done | bytes 262176 | tf_op jit(solution)/shard_map/ppermute | solution.py:441
  113.2 3.5 %collective-permute-start.24 = (bf16[512,256]{1,0:T(8,128)(2,1)S(1)}, bf16[512,256]{1,0:T(8,128)(2,1)S(1)}, u32[]{:S(2)}, u32[]{:S(2)}) collective-permute-start(bf16[512,256]{1,0:T(8,128)(2,1)S(1)} %get-tuple-element.132), channel_id=1, source_target_pairs={{0,14},{1,15},{2,0},{3,1},{4,2},{5,3},{6,4},{7,5},{8,6},{9,7},{10,... | collective-permute-start | bytes 786440 | tf_op jit(solution)/shard_map/ppermute | solution.py:443
  116.7 4.6 %shard_map.107 = (f32[4,128,1024]{2,1,0:T(8,128)S(1)}, f32[2,512,256]{2,1,0:T(8,128)S(1)}) custom-call(s32[2]{0:T(128)S(1)} %pad_add_fusion.refs_0_.tab, f32[4,1,1024]{2,1,0:T(1,128)S(1)} %get-tuple-element.75.refs_1_, f32[4,1,1024]{2,1,0:T(1,128)S(1)} %get-tuple-element.76.refs_2_, ...), custom_call_target="tpu_custom_call", output_to_operand_aliasing={{0}: (11, {})} | custom-call | flops 5368709120 | bytes 8388608 | tf_op jit(solution)/shard_map/pallas_call | solution.py:425
  121.3 2.8 %collective-permute-done.23 = bf16[512,256]{1,0:T(8,128)(2,1)S(1)} collective-permute-done((bf16[512,256]{1,0:T(8,128)(2,1)S(1)}, bf16[512,256]{1,0:T(8,128)(2,1)S(1)}, u32[]{:S(2)}, u32[]{:S(2)}) %collective-permute-start.23) | collective-permute-done | bytes 262176 | tf_op jit(solution)/shard_map/ppermute | solution.py:441
  124.3 4.4 %shard_map.108 = (bf16[128,1024]{1,0:T(8,128)(2,1)S(1)}, bf16[128,1024]{1,0:T(8,128)(2,1)S(1)}, f32[1,512,256]{2,1,0:T(8,128)S(1)}) custom-call(s32[2]{0:T(128)S(1)} %pad_add_fusion.refs_0_.tab, f32[4,1,1024]{2,1,0:T(1,128)S(1)} %get-tuple-element.75.refs_1_, f32[4,1,1024]{2,1,0:T(1,128)S(1)} %get-tuple-element.76.refs_2_, ...), custom_call_target="tpu_custom_call" | custom-call | flops 2684354560 | bytes 8388608 | tf_op jit(solution)/shard_map/pallas_call | solution.py:425
  128.7 2.6 %collective-permute-start.31 = (bf16[128,1024]{1,0:T(8,128)(2,1)S(1)}, bf16[128,1024]{1,0:T(8,128)(2,1)S(1)}, u32[]{:S(2)}, u32[]{:S(2)}) collective-permute-start(bf16[128,1024]{1,0:T(8,128)(2,1)S(1)} %get-tuple-element.141), channel_id=1, source_target_pairs={{0,1},{1,0},{2,3},{3,2},{4,5},{5,4},{6,7},{7,6},{8,9},{9,8},{10,11... | collective-permute-start | bytes 786440 | tf_op jit(solution)/shard_map/ppermute | solution.py:445
  131.2 3.7 %collective-permute-start.26 = (bf16[512,256]{1,0:T(8,128)(2,1)S(1)}, bf16[512,256]{1,0:T(8,128)(2,1)S(1)}, u32[]{:S(2)}, u32[]{:S(2)}) collective-permute-start(bf16[512,256]{1,0:T(8,128)(2,1)S(1)} %get-tuple-element.137), channel_id=1, source_target_pairs={{0,14},{1,15},{2,0},{3,1},{4,2},{5,3},{6,4},{7,5},{8,6},{9,7},{10,... | collective-permute-start | bytes 786440 | tf_op jit(solution)/shard_map/ppermute | solution.py:443
  134.9 3.1 %shard_map.109 = (bf16[128,1024]{1,0:T(8,128)(2,1)S(1)}, bf16[128,1024]{1,0:T(8,128)(2,1)S(1)}, f32[1,512,256]{2,1,0:T(8,128)S(1)}) custom-call(s32[2]{0:T(128)S(1)} %pad_add_fusion.refs_0_.tab, f32[4,1,1024]{2,1,0:T(1,128)S(1)} %get-tuple-element.75.refs_1_, f32[4,1,1024]{2,1,0:T(1,128)S(1)} %get-tuple-element.76.refs_2_, ...), custom_call_target="tpu_custom_call" | custom-call | flops 2684354560 | bytes 8388608 | tf_op jit(solution)/shard_map/pallas_call | solution.py:425
  138.0 0.5 collective-permute-start.30
  138.5 0.5 collective-permute-start.32
  139.0 1.4 collective-permute-done.26
  140.5 3.1 %collective-permute-done.25 = bf16[512,256]{1,0:T(8,128)(2,1)S(1)} collective-permute-done((bf16[512,256]{1,0:T(8,128)(2,1)S(1)}, bf16[512,256]{1,0:T(8,128)(2,1)S(1)}, u32[]{:S(2)}, u32[]{:S(2)}) %collective-permute-start.25) | collective-permute-done | bytes 262176 | tf_op jit(solution)/shard_map/ppermute | solution.py:441
  143.8 1.3 collective-permute-start.27
  145.1 1.7 %collective-permute-start.29 = (bf16[128,256]{1,0:T(8,128)(2,1)S(1)}, bf16[128,256]{1,0:T(8,128)(2,1)S(1)}, u32[]{:S(2)}, u32[]{:S(2)}) collective-permute-start(bf16[128,256]{1,0:T(8,128)(2,1)S(1)} %get-tuple-element.149), channel_id=1, source_target_pairs={{0,17},{1,16},{2,19},{3,18},{4,21},{5,20},{6,23},{7,22},{8,25},{9,... | collective-permute-start | bytes 196616 | tf_op jit(solution)/shard_map/ppermute | solution.py:453
  146.8 1.8 %collective-permute-done.28.a2 = bf16[128,256]{1,0:T(8,128)(2,1)S(1)} collective-permute-done((bf16[128,256]{1,0:T(8,128)(2,1)S(1)}, bf16[128,256]{1,0:T(8,128)(2,1)S(1)}, u32[]{:S(2)}, u32[]{:S(2)}) %collective-permute-start.28) | collective-permute-done | bytes 65568 | tf_op jit(solution)/shard_map/ppermute | solution.py:453
  148.6 1.7 %collective-permute-done.29.a3 = bf16[128,256]{1,0:T(8,128)(2,1)S(1)} collective-permute-done((bf16[128,256]{1,0:T(8,128)(2,1)S(1)}, bf16[128,256]{1,0:T(8,128)(2,1)S(1)}, u32[]{:S(2)}, u32[]{:S(2)}) %collective-permute-start.29) | collective-permute-done | bytes 65568 | tf_op jit(solution)/shard_map/ppermute | solution.py:453
  150.3 1.4 shard_map.110
  (66 shorter events, 2.4 us)
Async XLA Ops:
  0.6 47.1 %copy-start.1 = (bf16[1,128,1024]{2,1,0:T(8,128)(2,1)S(1)}, bf16[1,128,1024]{2,1,0:T(8,128)(2,1)}, u32[]{:S(2)}) copy-start(bf16[1,128,1024]{2,1,0:T(8,128)(2,1)} %param.10) | copy-start | bytes 786436
  0.6 47.1 %copy-start.2 = (bf16[1,128,1024]{2,1,0:T(8,128)(2,1)S(1)}, bf16[1,128,1024]{2,1,0:T(8,128)(2,1)}, u32[]{:S(2)}) copy-start(bf16[1,128,1024]{2,1,0:T(8,128)(2,1)} %param.11) | copy-start | bytes 786436
  3.9 19.0 %collective-permute-start.1 = (bf16[144,1024]{1,0:T(8,128)(2,1)}, bf16[144,1024]{1,0:T(8,128)(2,1)S(1)}, u32[]{:S(2)}, u32[]{:S(2)}) collective-permute-start(bf16[144,1024]{1,0:T(8,128)(2,1)} %get-tuple-element.74.q0), channel_id=1, source_target_pairs={{0,16},{1,17},{2,18},{3,19},{4,20},{5,21},{6,22},{7,23},{8,24},{9,... | collective-permute-start | bytes 884744 | tf_op jit(solution)/shard_map/ppermute | solution.py:360
  5.3 2.6 %collective-permute-start.6 = (bf16[144,256]{1,0:T(8,128)(2,1)}, bf16[144,256]{1,0:T(8,128)(2,1)S(1)}, u32[]{:S(2)}, u32[]{:S(2)}) collective-permute-start(bf16[144,256]{1,0:T(8,128)(2,1)} %get-tuple-element.79), channel_id=1, source_target_pairs={{0,1},{1,0},{2,3},{3,2},{4,5},{5,4},{6,7},{7,6},{8,9},{9,8},{10,11... | collective-permute-start | bytes 221192 | tf_op jit(solution)/shard_map/ppermute | solution.py:356
  6.2 7.4 %collective-permute-start.7 = (bf16[144,256]{1,0:T(8,128)(2,1)}, bf16[144,256]{1,0:T(8,128)(2,1)S(1)}, u32[]{:S(2)}, u32[]{:S(2)}) collective-permute-start(bf16[144,256]{1,0:T(8,128)(2,1)} %get-tuple-element.80), channel_id=1, source_target_pairs={{0,16},{1,17},{2,18},{3,19},{4,20},{5,21},{6,22},{7,23},{8,24},{9,... | collective-permute-start | bytes 221192 | tf_op jit(solution)/shard_map/ppermute | solution.py:356
  6.4 9.7 %collective-permute-start.8 = (bf16[144,256]{1,0:T(8,128)(2,1)}, bf16[144,256]{1,0:T(8,128)(2,1)S(1)}, u32[]{:S(2)}, u32[]{:S(2)}) collective-permute-start(bf16[144,256]{1,0:T(8,128)(2,1)} %get-tuple-element.81), channel_id=1, source_target_pairs={{0,17},{1,16},{2,19},{3,18},{4,21},{5,20},{6,23},{7,22},{8,25},{9,... | collective-permute-start | bytes 221192 | tf_op jit(solution)/shard_map/ppermute | solution.py:356
  16.1 0.9 copy-start.3
  17.0 12.6 %collective-permute-start.9 = (bf16[528,256]{1,0:T(8,128)(2,1)S(1)}, bf16[528,256]{1,0:T(8,128)(2,1)S(1)}, u32[]{:S(2)}, u32[]{:S(2)}) collective-permute-start(bf16[528,256]{1,0:T(8,128)(2,1)S(1)} %shard_map.98.refs_5_.refs_9_), channel_id=1, source_target_pairs={{0,2},{1,3},{2,4},{3,5},{4,6},{5,7},{6,8},{7,9},{8,10},{9,11},{10,... | collective-permute-start | bytes 811016 | tf_op jit(solution)/shard_map/ppermute | solution.py:382
  18.7 10.9 %collective-permute-start.11 = (bf16[528,256]{1,0:T(8,128)(2,1)S(1)}, bf16[528,256]{1,0:T(8,128)(2,1)S(1)}, u32[]{:S(2)}, u32[]{:S(2)}) collective-permute-start(bf16[528,256]{1,0:T(8,128)(2,1)S(1)} %shard_map.98.refs_5_.refs_9_), channel_id=1, source_target_pairs={{0,14},{1,15},{2,0},{3,1},{4,2},{5,3},{6,4},{7,5},{8,6},{9,7},{10,... | collective-permute-start | bytes 811016 | tf_op jit(solution)/shard_map/ppermute | solution.py:382
  22.7 9.6 %collective-permute-start = (bf16[144,1024]{1,0:T(8,128)(2,1)}, bf16[144,1024]{1,0:T(8,128)(2,1)S(1)}, u32[]{:S(2)}, u32[]{:S(2)}) collective-permute-start(bf16[144,1024]{1,0:T(8,128)(2,1)} %get-tuple-element.74.q0), channel_id=1, source_target_pairs={{0,1},{1,0},{2,3},{3,2},{4,5},{5,4},{6,7},{7,6},{8,9},{9,8},{10,11... | collective-permute-start | bytes 884744 | tf_op jit(solution)/shard_map/ppermute | solution.py:362
  22.9 9.4 %collective-permute-start.2 = (bf16[144,1024]{1,0:T(8,128)(2,1)S(1)}, bf16[144,1024]{1,0:T(8,128)(2,1)S(1)}, u32[]{:S(2)}, u32[]{:S(2)}) collective-permute-start(bf16[144,1024]{1,0:T(8,128)(2,1)S(1)} %collective-permute-done.1.q2), channel_id=1, source_target_pairs={{0,1},{1,0},{2,3},{3,2},{4,5},{5,4},{6,7},{7,6},{8,9},{9,8},{10,11... | collective-permute-start | bytes 884744 | tf_op jit(solution)/shard_map/ppermute | solution.py:361
  29.6 12.2 %collective-permute-start.10 = (bf16[528,256]{1,0:T(8,128)(2,1)S(1)}, bf16[528,256]{1,0:T(8,128)(2,1)S(1)}, u32[]{:S(2)}, u32[]{:S(2)}) collective-permute-start(bf16[528,256]{1,0:T(8,128)(2,1)S(1)} %collective-permute-done.9.refs_6_.refs_10_), channel_id=1, source_target_pairs={{0,2},{1,3},{2,4},{3,5},{4,6},{5,7},{6,8},{7,9},{8,10},{9,11},{10,... | collective-permute-start | bytes 811016 | tf_op jit(solution)/shard_map/ppermute | solution.py:382
  29.6 12.2 %collective-permute-start.12 = (bf16[528,256]{1,0:T(8,128)(2,1)S(1)}, bf16[528,256]{1,0:T(8,128)(2,1)S(1)}, u32[]{:S(2)}, u32[]{:S(2)}) collective-permute-start(bf16[528,256]{1,0:T(8,128)(2,1)S(1)} %collective-permute-done.11.refs_5_.refs_9_), channel_id=1, source_target_pairs={{0,14},{1,15},{2,0},{3,1},{4,2},{5,3},{6,4},{7,5},{8,6},{9,7},{10,... | collective-permute-start | bytes 811016 | tf_op jit(solution)/shard_map/ppermute | solution.py:382
  32.4 1.0 copy-start
  41.8 10.9 %collective-permute-start.13 = (bf16[528,256]{1,0:T(8,128)(2,1)S(1)}, bf16[528,256]{1,0:T(8,128)(2,1)S(1)}, u32[]{:S(2)}, u32[]{:S(2)}) collective-permute-start(bf16[528,256]{1,0:T(8,128)(2,1)S(1)} %collective-permute-done.10.refs_6_.refs_10_), channel_id=1, source_target_pairs={{0,2},{1,3},{2,4},{3,5},{4,6},{5,7},{6,8},{7,9},{8,10},{9,11},{10,... | collective-permute-start | bytes 811016 | tf_op jit(solution)/shard_map/ppermute | solution.py:382
  41.9 10.8 %collective-permute-start.14 = (bf16[528,256]{1,0:T(8,128)(2,1)S(1)}, bf16[528,256]{1,0:T(8,128)(2,1)S(1)}, u32[]{:S(2)}, u32[]{:S(2)}) collective-permute-start(bf16[528,256]{1,0:T(8,128)(2,1)S(1)} %collective-permute-done.12.refs_5_.refs_9_), channel_id=1, source_target_pairs={{0,14},{1,15},{2,0},{3,1},{4,2},{5,3},{6,4},{7,5},{8,6},{9,7},{10,... | collective-permute-start | bytes 811016 | tf_op jit(solution)/shard_map/ppermute | solution.py:382
  47.9 22.3 %collective-permute-start.4 = (bf16[144,1024]{1,0:T(8,128)(2,1)S(1)}, bf16[144,1024]{1,0:T(8,128)(2,1)S(1)}, u32[]{:S(2)}, u32[]{:S(2)}) collective-permute-start(bf16[144,1024]{1,0:T(8,128)(2,1)S(1)} %shard_map.96.q0), channel_id=1, source_target_pairs={{0,16},{1,17},{2,18},{3,19},{4,20},{5,21},{6,22},{7,23},{8,24},{9,... | collective-permute-start | bytes 884744 | tf_op jit(solution)/shard_map/ppermute | solution.py:360
  52.8 22.2 %collective-permute-start.15 = (bf16[272,256]{1,0:T(8,128)(2,1)S(1)}, bf16[272,256]{1,0:T(8,128)(2,1)S(1)}, u32[]{:S(2)}, u32[]{:S(2)}) collective-permute-start(bf16[272,256]{1,0:T(8,128)(2,1)S(1)} %slice.105), channel_id=1, source_target_pairs={{0,2},{1,3},{2,4},{3,5},{4,6},{5,7},{6,8},{7,9},{8,10},{9,11},{10,... | collective-permute-start | bytes 417800 | tf_op jit(solution)/shard_map/ppermute | solution.py:384
  52.9 22.0 %collective-permute-start.16 = (bf16[256,256]{1,0:T(8,128)(2,1)S(1)}, bf16[256,256]{1,0:T(8,128)(2,1)S(1)}, u32[]{:S(2)}, u32[]{:S(2)}) collective-permute-start(bf16[256,256]{1,0:T(8,128)(2,1)S(1)} %slice.106), channel_id=1, source_target_pairs={{0,14},{1,15},{2,0},{3,1},{4,2},{5,3},{6,4},{7,5},{8,6},{9,7},{10,... | collective-permute-start | bytes 393224 | tf_op jit(solution)/shard_map/ppermute | solution.py:384
  58.0 18.8 %collective-permute-start.3 = (bf16[144,1024]{1,0:T(8,128)(2,1)S(1)}, bf16[144,1024]{1,0:T(8,128)(2,1)S(1)}, u32[]{:S(2)}, u32[]{:S(2)}) collective-permute-start(bf16[144,1024]{1,0:T(8,128)(2,1)S(1)} %shard_map.96.q0), channel_id=1, source_target_pairs={{0,1},{1,0},{2,3},{3,2},{4,5},{5,4},{6,7},{7,6},{8,9},{9,8},{10,11... | collective-permute-start | bytes 884744 | tf_op jit(solution)/shard_map/ppermute | solution.py:362
  70.2 6.6 %collective-permute-start.5 = (bf16[144,1024]{1,0:T(8,128)(2,1)S(1)}, bf16[144,1024]{1,0:T(8,128)(2,1)S(1)}, u32[]{:S(2)}, u32[]{:S(2)}) collective-permute-start(bf16[144,1024]{1,0:T(8,128)(2,1)S(1)} %collective-permute-done.4.q2), channel_id=1, source_target_pairs={{0,1},{1,0},{2,3},{3,2},{4,5},{5,4},{6,7},{7,6},{8,9},{9,8},{10,11... | collective-permute-start | bytes 884744 | tf_op jit(solution)/shard_map/ppermute | solution.py:361
  76.7 4.3 %collective-permute-start.18 = (f32[8,1,1024]{2,1,0:T(1,128)S(1)}, f32[8,1,1024]{2,1,0:T(1,128)S(1)}, u32[]{:S(2)}, u32[]{:S(2)}) collective-permute-start(f32[8,1,1024]{2,1,0:T(1,128)S(1)} %constant_dynamic-update-slice_fusion.2), channel_id=1, source_target_pairs={{0,16},{1,17},{2,18},{3,19},{4,20},{5,21},{6,22},{7,23},{8,24},{9,... | collective-permute-start | bytes 98312 | tf_op jit(solution)/shard_map/ppermute | solution.py:407
  77.8 4.9 %collective-permute-start.19 = (f32[8,1,1024]{2,1,0:T(1,128)S(1)}, f32[8,1,1024]{2,1,0:T(1,128)S(1)}, u32[]{:S(2)}, u32[]{:S(2)}) collective-permute-start(f32[8,1,1024]{2,1,0:T(1,128)S(1)} %constant_dynamic-update-slice_fusion.2), channel_id=1, source_target_pairs={{0,17},{1,16},{2,19},{3,18},{4,21},{5,20},{6,23},{7,22},{8,25},{9,... | collective-permute-start | bytes 98312 | tf_op jit(solution)/shard_map/ppermute | solution.py:407
  81.1 1.6 %collective-permute-start.17 = (f32[8,1,1024]{2,1,0:T(1,128)S(1)}, f32[8,1,1024]{2,1,0:T(1,128)S(1)}, u32[]{:S(2)}, u32[]{:S(2)}) collective-permute-start(f32[8,1,1024]{2,1,0:T(1,128)S(1)} %constant_dynamic-update-slice_fusion.2), channel_id=1, source_target_pairs={{0,1},{1,0},{2,3},{3,2},{4,5},{5,4},{6,7},{7,6},{8,9},{9,8},{10,11... | collective-permute-start | bytes 98312 | tf_op jit(solution)/shard_map/ppermute | solution.py:407
  85.5 11.9 %collective-permute-start.20 = (bf16[512,256]{1,0:T(8,128)(2,1)S(1)}, bf16[512,256]{1,0:T(8,128)(2,1)S(1)}, u32[]{:S(2)}, u32[]{:S(2)}) collective-permute-start(bf16[512,256]{1,0:T(8,128)(2,1)S(1)} %convert_bitcast_fusion), channel_id=1, source_target_pairs={{0,2},{1,3},{2,4},{3,5},{4,6},{5,7},{6,8},{7,9},{8,10},{9,11},{10,... | collective-permute-start | bytes 786440 | tf_op jit(solution)/shard_map/ppermute | solution.py:441
  97.5 12.4 %collective-permute-start.22 = (bf16[512,256]{1,0:T(8,128)(2,1)S(1)}, bf16[512,256]{1,0:T(8,128)(2,1)S(1)}, u32[]{:S(2)}, u32[]{:S(2)}) collective-permute-start(bf16[512,256]{1,0:T(8,128)(2,1)S(1)} %fusion.8), channel_id=1, source_target_pairs={{0,14},{1,15},{2,0},{3,1},{4,2},{5,3},{6,4},{7,5},{8,6},{9,7},{10,... | collective-permute-start | bytes 786440 | tf_op jit(solution)/shard_map/ppermute | solution.py:443
  105.1 8.0 %collective-permute-start.21 = (bf16[512,256]{1,0:T(8,128)(2,1)S(1)}, bf16[512,256]{1,0:T(8,128)(2,1)S(1)}, u32[]{:S(2)}, u32[]{:S(2)}) collective-permute-start(bf16[512,256]{1,0:T(8,128)(2,1)S(1)} %fusion.7), channel_id=1, source_target_pairs={{0,2},{1,3},{2,4},{3,5},{4,6},{5,7},{6,8},{7,9},{8,10},{9,11},{10,... | collective-permute-start | bytes 786440 | tf_op jit(solution)/shard_map/ppermute | solution.py:441
  113.2 8.1 %collective-permute-start.24 = (bf16[512,256]{1,0:T(8,128)(2,1)S(1)}, bf16[512,256]{1,0:T(8,128)(2,1)S(1)}, u32[]{:S(2)}, u32[]{:S(2)}) collective-permute-start(bf16[512,256]{1,0:T(8,128)(2,1)S(1)} %get-tuple-element.132), channel_id=1, source_target_pairs={{0,14},{1,15},{2,0},{3,1},{4,2},{5,3},{6,4},{7,5},{8,6},{9,7},{10,... | collective-permute-start | bytes 786440 | tf_op jit(solution)/shard_map/ppermute | solution.py:443
  116.7 7.5 %collective-permute-start.23 = (bf16[512,256]{1,0:T(8,128)(2,1)S(1)}, bf16[512,256]{1,0:T(8,128)(2,1)S(1)}, u32[]{:S(2)}, u32[]{:S(2)}) collective-permute-start(bf16[512,256]{1,0:T(8,128)(2,1)S(1)} %get-tuple-element.131), channel_id=1, source_target_pairs={{0,2},{1,3},{2,4},{3,5},{4,6},{5,7},{6,8},{7,9},{8,10},{9,11},{10,... | collective-permute-start | bytes 786440 | tf_op jit(solution)/shard_map/ppermute | solution.py:441
  128.7 9.8 %collective-permute-start.31 = (bf16[128,1024]{1,0:T(8,128)(2,1)S(1)}, bf16[128,1024]{1,0:T(8,128)(2,1)S(1)}, u32[]{:S(2)}, u32[]{:S(2)}) collective-permute-start(bf16[128,1024]{1,0:T(8,128)(2,1)S(1)} %get-tuple-element.141), channel_id=1, source_target_pairs={{0,1},{1,0},{2,3},{3,2},{4,5},{5,4},{6,7},{7,6},{8,9},{9,8},{10,11... | collective-permute-start | bytes 786440 | tf_op jit(solution)/shard_map/ppermute | solution.py:445
  131.2 9.2 %collective-permute-start.26 = (bf16[512,256]{1,0:T(8,128)(2,1)S(1)}, bf16[512,256]{1,0:T(8,128)(2,1)S(1)}, u32[]{:S(2)}, u32[]{:S(2)}) collective-permute-start(bf16[512,256]{1,0:T(8,128)(2,1)S(1)} %get-tuple-element.137), channel_id=1, source_target_pairs={{0,14},{1,15},{2,0},{3,1},{4,2},{5,3},{6,4},{7,5},{8,6},{9,7},{10,... | collective-permute-start | bytes 786440 | tf_op jit(solution)/shard_map/ppermute | solution.py:443
  134.9 8.7 %collective-permute-start.25 = (bf16[512,256]{1,0:T(8,128)(2,1)S(1)}, bf16[512,256]{1,0:T(8,128)(2,1)S(1)}, u32[]{:S(2)}, u32[]{:S(2)}) collective-permute-start(bf16[512,256]{1,0:T(8,128)(2,1)S(1)} %get-tuple-element.136), channel_id=1, source_target_pairs={{0,2},{1,3},{2,4},{3,5},{4,6},{5,7},{6,8},{7,9},{8,10},{9,11},{10,... | collective-permute-start | bytes 786440 | tf_op jit(solution)/shard_map/ppermute | solution.py:441
  138.0 8.8 %collective-permute-start.30 = (bf16[128,1024]{1,0:T(8,128)(2,1)S(1)}, bf16[128,1024]{1,0:T(8,128)(2,1)S(1)}, u32[]{:S(2)}, u32[]{:S(2)}) collective-permute-start(bf16[128,1024]{1,0:T(8,128)(2,1)S(1)} %get-tuple-element.139), channel_id=1, source_target_pairs={{0,1},{1,0},{2,3},{3,2},{4,5},{5,4},{6,7},{7,6},{8,9},{9,8},{10,11... | collective-permute-start | bytes 786440 | tf_op jit(solution)/shard_map/ppermute | solution.py:452
  138.5 11.8 %collective-permute-start.32 = (bf16[128,1024]{1,0:T(8,128)(2,1)S(1)}, bf16[128,1024]{1,0:T(8,128)(2,1)S(1)}, u32[]{:S(2)}, u32[]{:S(2)}) collective-permute-start(bf16[128,1024]{1,0:T(8,128)(2,1)S(1)} %add_convert_fusion), channel_id=1, source_target_pairs={{0,16},{1,17},{2,18},{3,19},{4,20},{5,21},{6,22},{7,23},{8,24},{9,... | collective-permute-start | bytes 786440 | tf_op jit(solution)/shard_map/ppermute | solution.py:447
  143.8 3.1 %collective-permute-start.27 = (bf16[128,256]{1,0:T(8,128)(2,1)S(1)}, bf16[128,256]{1,0:T(8,128)(2,1)S(1)}, u32[]{:S(2)}, u32[]{:S(2)}) collective-permute-start(bf16[128,256]{1,0:T(8,128)(2,1)S(1)} %get-tuple-element.151), channel_id=1, source_target_pairs={{0,1},{1,0},{2,3},{3,2},{4,5},{5,4},{6,7},{7,6},{8,9},{9,8},{10,11... | collective-permute-start | bytes 196616 | tf_op jit(solution)/shard_map/ppermute | solution.py:453
  145.1 3.5 %collective-permute-start.28 = (bf16[128,256]{1,0:T(8,128)(2,1)S(1)}, bf16[128,256]{1,0:T(8,128)(2,1)S(1)}, u32[]{:S(2)}, u32[]{:S(2)}) collective-permute-start(bf16[128,256]{1,0:T(8,128)(2,1)S(1)} %get-tuple-element.150), channel_id=1, source_target_pairs={{0,16},{1,17},{2,18},{3,19},{4,20},{5,21},{6,22},{7,23},{8,24},{9,... | collective-permute-start | bytes 196616 | tf_op jit(solution)/shard_map/ppermute | solution.py:453
  145.1 5.2 %collective-permute-start.29 = (bf16[128,256]{1,0:T(8,128)(2,1)S(1)}, bf16[128,256]{1,0:T(8,128)(2,1)S(1)}, u32[]{:S(2)}, u32[]{:S(2)}) collective-permute-start(bf16[128,256]{1,0:T(8,128)(2,1)S(1)} %get-tuple-element.149), channel_id=1, source_target_pairs={{0,17},{1,16},{2,19},{3,18},{4,21},{5,20},{6,23},{7,22},{8,25},{9,... | collective-permute-start | bytes 196616 | tf_op jit(solution)/shard_map/ppermute | solution.py:453

commit v4 on v3

--- a/solution.py
+++ b/solution.py
@@ -171,9 +171,8 @@
     return jnp.concatenate([both, both], axis=1) > 0.5
 
 
-def items(ks, rhos, tab, tag_ref, kv, body, masks):
+def items(ks, rhos, tab, tag_ref, kv, body, masks, wide=True):
     edge = 0 in ks or 1 in ks
-    own = ks == (0,)
 
     def item(t, _):
         n = t // len(rhos)
@@ -198,7 +197,7 @@
                 pl.when(full)(lambda: body(n, rho, half, NK // 2, kind, False))
             return 0
 
-        if own:
+        if not wide:
             lax.fori_loop(0, 2, one, 0)
         else:
             both = item_kind(tab, z_keys, 0, rho)[3] & item_kind(tab, z_keys, 1, rho)[3]
@@ -259,14 +258,14 @@
 
     def attempt(_):
         sum_ref[...] = jnp.zeros_like(sum_ref)
-        items(ks, (0, 1, 2, 3), tab, tag_ref, kv, later_body, True)
+        items(ks, (0, 1, 2, 3), tab, tag_ref, kv, later_body, True, ks[0] != 2)
         sums = sum_ref[...]
         step = jnp.where(sums > 2.0**100, 80.0, jnp.where(sums > 2.0**40, 26.0, 0.0))
         m_ref[...] += step * (1.0 / C2)
         return jnp.max(step)
 
     if ks == (0,):
-        items(ks, (0, 1, 2, 3), tab, tag_ref, kv, first_body, True)
+        items(ks, (0, 1, 2, 3), tab, tag_ref, kv, first_body, True, False)
     else:
         lax.while_loop(lambda step: step > 0.0, attempt, jnp.float32(1.0))
         l_ref[...] = l_ref[...] * jnp.exp2((refs[3][...] - m_ref[...]) * C2) + sum_ref[...]
@@ -284,10 +283,11 @@
 
         each(H, wipe)
     elif last:
-        dq_in, o0, o1, acc, kv, p_all, d_all, dq_ref = rest
+        dq_in, pieces, rest = rest[0], rest[1 : 1 + len(rhos)], rest[1 + len(rhos) :]
+        acc, kv, p_all, d_all, dq_ref = rest
 
         def fetch(t):
-            dq_ref[:, :, lanes(t)] = dq_in[rhos[0] : rhos[0] + 2, :, lanes(t)]
+            dq_ref[:, :, lanes(t)] = dq_in[rhos[0] : rhos[0] + len(rhos), :, lanes(t)]
 
         each(H, fetch)
     else:
@@ -315,11 +315,11 @@
         acc[n, rows, HD:] += dot_nn(p_all[0:size, :], gt_ref[rho])
         dq_ref[rho - rhos[0]] += dot_tn(keys, d)
 
-    items(ks, rhos, tab, tag_ref, kv, body, False)
+    items(ks, rhos, tab, tag_ref, kv, body, False, not last)
     if last:
 
         def head(h):
-            for r, out in enumerate((o0, o1)):
+            for r, out in enumerate(pieces):
                 out[:, lanes(h)] = (dq_ref[r, :, lanes(h)].T * SCALE).astype(BF16)
 
         each(H, head)
@@ -424,9 +424,9 @@
         scratch = [pltpu.VMEM((n, NK + 16, 256), BF16)] + [pltpu.VMEM((NK, NQ * H), BF16)] * 2
         return call(
             functools.partial(grads_body, ks, rhos, first, last),
-            ([piece, piece] if last else [dq_shape]) + [shape((n, NK, 2 * HD), F32)],
+            ([piece] * len(rhos) if last else [dq_shape]) + [shape((n, NK, 2 * HD), F32)],
             [SM] + [VM] * (len(args) - 1),
-            scratch=scratch + ([pltpu.VMEM((2, HD, NQ * H), F32)] if last else []),
+            scratch=scratch + ([pltpu.VMEM((len(rhos), HD, NQ * H), F32)] if last else []),
             vmem=5, flops=n * 5 * (1 << 29), nbytes=8 * MIB,
             alias={} if first or last else {len(args) - 1: 0},
         )(*args)
@@ -441,12 +441,13 @@
         up = hop(sends[0], perm=turn(1))
         if n == 2:
             down = hop(sends[1], perm=turn(-1))
-    dq2, dq3, far_adds = grads((0,), (2, 3), dq)
+    dq3, adds3 = grads((0,), (3,), dq)
     dq3 = hop(dq3, perm=flip(1))
+    dq2, adds2 = grads((0,), (2,), dq)
     across = (dq2.astype(F32) + dq3.astype(F32)).astype(BF16)
     dq_far = hop(across, perm=flip(2))
-    dq0, dq1, near_adds = grads((0,), (0, 1), dq)
-    own = far_adds[0] + near_adds[0] + up.astype(F32) + down.astype(F32)
+    dq0, dq1, adds0 = grads((0,), (0, 1), dq)
+    own = adds3[0] + adds2[0] + adds0[0] + up.astype(F32) + down.astype(F32)
     scales = jnp.where(jnp.arange(2 * HD) < HD, SCALE, 1.0).astype(F32)
     own = (own * scales[None, :]).astype(BF16)
     q_back = [dq0, hop(dq1, perm=flip(1)), dq_far]

time: 152 us -> 155 us (1.020)
  the two profiles are of different devices: /device:TPU:5 before, /device:TPU:27 now
where the time goes in v4:
time: 155 us
  starting transfers between devices  63.3 us (41%)
  Pallas kernels  45.7 us (29%)
  waiting for transfers between devices  41.6 us (27%)
  local copies, waits for them, and re-layouts  1.99 us (1%)
    pallas_call x7, Pallas kernels, grads(): call(functools.partial(grads_body, ks, rhos, first, last), ([piece] * len...  24.9 us
    ppermute x4, waiting for transfers between devices, per_device(): up = hop(sends[0], perm=turn(1))  18.1 us
    ppermute x3, starting transfers between devices, per_device(): down = hop(sends[1], perm=turn(-1))  15.1 us
    pallas_call x5, Pallas kernels, per_device(): call(functools.partial(stats_body, ks), [stat, stat, shape((4 * n, NK, NQ...  14.8 us
    ppermute x6, starting transfers between devices, per_device(): fwd, bwd = (hop(fwd, perm=turn(1)), hop(bwd, perm=turn(-1)))  11.2 us
    ppermute x2, starting transfers between devices, four(): other = hop(x, perm=flip(2))  10.3 us
    ppermute x3, waiting for transfers between devices, per_device(): got = [hop(parts[r], perm=flip(r)) for r in (1, 2, 3)]  9.05 us
    ppermute x6, waiting for transfers between devices, per_device(): fwd, bwd = (hop(fwd, perm=turn(1)), hop(bwd, perm=turn(-1)))  6.36 us
  transfers between devices with their start and end apart: 33, of which 11 were waited for; matrix products, arithmetic and copies ran while one was open for 0% of the time, Pallas kernels for 24%

profile of v4, /device:TPU:27, one launch (start us, length us, event | category | flops | bytes accessed | tf_op | source)
XLA Modules:
  0.0 155.3 jit_solution(6990525535923881288)
XLA Ops:
  0.7 0.7 pad_add_fusion.1.tab
  1.3 2.6 %shard_map.94 = (bf16[144,256]{1,0:T(8,128)(2,1)}, bf16[144,256]{1,0:T(8,128)(2,1)}, bf16[144,256]{1,0:T(8,128)(2,1)}, bf16[144,256]{1,0:T(8,128)(2,1)}, bf16[144,1024]{1,0:T(8,128)(2,1)}) custom-call(s32[2]{0:T(128)} %pad_add_fusion.1.tab, bf16[512,128]{1,0:T(8,128)(2,1)} %bitcast.47, bf16[512,128]{1,0:T(8,128)(2,1)} %bitcast.48, s32[1,512]{1,0:T(1,128)} %seg_hbm.1, ...), custom_call_target="tpu_custom_call" | custom-call | bytes 1048576 | tf_op jit(solution)/shard_map/pallas_call | solution.py:348
  4.5 1.0 collective-permute-start.6
  5.5 1.0 collective-permute-start.7
  6.5 0.6 collective-permute-start.8
  7.1 6.6 %collective-permute-done.7.p2 = bf16[144,256]{1,0:T(8,128)(2,1)S(1)} collective-permute-done((bf16[144,256]{1,0:T(8,128)(2,1)}, bf16[144,256]{1,0:T(8,128)(2,1)S(1)}, u32[]{:S(2)}, u32[]{:S(2)}) %collective-permute-start.7) | collective-permute-done | bytes 73760 | tf_op jit(solution)/shard_map/ppermute | solution.py:356
  13.7 2.4 %collective-permute-done.8.p3 = bf16[144,256]{1,0:T(8,128)(2,1)S(1)} collective-permute-done((bf16[144,256]{1,0:T(8,128)(2,1)}, bf16[144,256]{1,0:T(8,128)(2,1)S(1)}, u32[]{:S(2)}, u32[]{:S(2)}) %collective-permute-start.8) | collective-permute-done | bytes 73760 | tf_op jit(solution)/shard_map/ppermute | solution.py:356
  16.1 0.9 copy-done.3
  17.1 1.7 %collective-permute-start.9 = (bf16[528,256]{1,0:T(8,128)(2,1)S(1)}, bf16[528,256]{1,0:T(8,128)(2,1)S(1)}, u32[]{:S(2)}, u32[]{:S(2)}) collective-permute-start(bf16[528,256]{1,0:T(8,128)(2,1)S(1)} %shard_map.98.refs_5_.refs_9_), channel_id=1, source_target_pairs={{0,2},{1,3},{2,4},{3,5},{4,6},{5,7},{6,8},{7,9},{8,10},{9,11},{10,... | collective-permute-start | bytes 811016 | tf_op jit(solution)/shard_map/ppermute | solution.py:382
  18.8 4.0 %collective-permute-start.11 = (bf16[528,256]{1,0:T(8,128)(2,1)S(1)}, bf16[528,256]{1,0:T(8,128)(2,1)S(1)}, u32[]{:S(2)}, u32[]{:S(2)}) collective-permute-start(bf16[528,256]{1,0:T(8,128)(2,1)S(1)} %shard_map.98.refs_5_.refs_9_), channel_id=1, source_target_pairs={{0,14},{1,15},{2,0},{3,1},{4,2},{5,3},{6,4},{7,5},{8,6},{9,7},{10,... | collective-permute-start | bytes 811016 | tf_op jit(solution)/shard_map/ppermute | solution.py:382
  23.3 6.3 %collective-permute-done.9.refs_6_.refs_10_ = bf16[528,256]{1,0:T(8,128)(2,1)S(1)} collective-permute-done((bf16[528,256]{1,0:T(8,128)(2,1)S(1)}, bf16[528,256]{1,0:T(8,128)(2,1)S(1)}, u32[]{:S(2)}, u32[]{:S(2)}) %collective-permute-start.9) | collective-permute-done | bytes 270368 | tf_op jit(solution)/shard_map/ppermute | solution.py:382
  29.7 2.7 %collective-permute-start.12 = (bf16[528,256]{1,0:T(8,128)(2,1)S(1)}, bf16[528,256]{1,0:T(8,128)(2,1)S(1)}, u32[]{:S(2)}, u32[]{:S(2)}) collective-permute-start(bf16[528,256]{1,0:T(8,128)(2,1)S(1)} %collective-permute-done.11.refs_5_.refs_9_), channel_id=1, source_target_pairs={{0,14},{1,15},{2,0},{3,1},{4,2},{5,3},{6,4},{7,5},{8,6},{9,7},{10,... | collective-permute-start | bytes 811016 | tf_op jit(solution)/shard_map/ppermute | solution.py:382
  32.4 1.0 copy-done
  33.4 0.9 shard_map.95
  34.3 4.1 %shard_map.99 = (f32[4,1,1024]{2,1,0:T(1,128)S(1)}, f32[4,1,1024]{2,1,0:T(1,128)S(1)}, bf16[4,512,1024]{2,1,0:T(8,128)(2,1)S(1)}, f32[8,1,1024]{2,1,0:T(1,128)S(1)}) custom-call(s32[2]{0:T(128)S(1)} %pad_add_fusion.refs_0_.tab, f32[4,1,1024]{2,1,0:T(1,128)S(1)} %get-tuple-element.76.refs_1_, bf16[4,128,1024]{2,1,0:T(8,128)(2,1)S(1)} %get-tuple-element.78.refs_2_, ...), custom_call_target="tpu_custom_call" | custom-call | flops 536870912 | bytes 2097152 | tf_op jit(solution)/shard_map/pallas_call | solution.py:386
  38.4 3.8 %shard_map.100 = (f32[4,1,1024]{2,1,0:T(1,128)S(1)}, f32[4,1,1024]{2,1,0:T(1,128)S(1)}, bf16[8,512,1024]{2,1,0:T(8,128)(2,1)S(1)}, f32[16,1,1024]{2,1,0:T(1,128)S(1)}) custom-call(s32[2]{0:T(128)S(1)} %pad_add_fusion.refs_0_.tab, f32[4,1,1024]{2,1,0:T(1,128)S(1)} %get-tuple-element.76.refs_1_, bf16[4,128,1024]{2,1,0:T(8,128)(2,1)S(1)} %get-tuple-element.78.refs_2_, ...), custom_call_target="tpu_custom_call" | custom-call | flops 1073741824 | bytes 2097152 | tf_op jit(solution)/shard_map/pallas_call | solution.py:386
  42.4 2.7 %collective-permute-start.14 = (bf16[528,256]{1,0:T(8,128)(2,1)S(1)}, bf16[528,256]{1,0:T(8,128)(2,1)S(1)}, u32[]{:S(2)}, u32[]{:S(2)}) collective-permute-start(bf16[528,256]{1,0:T(8,128)(2,1)S(1)} %collective-permute-done.12.refs_5_.refs_9_), channel_id=1, source_target_pairs={{0,14},{1,15},{2,0},{3,1},{4,2},{5,3},{6,4},{7,5},{8,6},{9,7},{10,... | collective-permute-start | bytes 811016 | tf_op jit(solution)/shard_map/ppermute | solution.py:382
  45.2 9.8 %collective-permute-start.4 = (bf16[144,1024]{1,0:T(8,128)(2,1)S(1)}, bf16[144,1024]{1,0:T(8,128)(2,1)S(1)}, u32[]{:S(2)}, u32[]{:S(2)}) collective-permute-start(bf16[144,1024]{1,0:T(8,128)(2,1)S(1)} %shard_map.96.q0), channel_id=1, source_target_pairs={{0,16},{1,17},{2,18},{3,19},{4,20},{5,21},{6,22},{7,23},{8,24},{9,... | collective-permute-start | bytes 884744 | tf_op jit(solution)/shard_map/ppermute | solution.py:360
  55.0 2.5 %shard_map.101 = (f32[4,1,1024]{2,1,0:T(1,128)S(1)}, f32[4,1,1024]{2,1,0:T(1,128)S(1)}, bf16[8,512,1024]{2,1,0:T(8,128)(2,1)S(1)}, f32[16,1,1024]{2,1,0:T(1,128)S(1)}) custom-call(s32[2]{0:T(128)S(1)} %pad_add_fusion.refs_0_.tab, f32[4,1,1024]{2,1,0:T(1,128)S(1)} %get-tuple-element.76.refs_1_, bf16[4,128,1024]{2,1,0:T(8,128)(2,1)S(1)} %get-tuple-element.78.refs_2_, ...), custom_call_target="tpu_custom_call" | custom-call | flops 1073741824 | bytes 2097152 | tf_op jit(solution)/shard_map/pallas_call | solution.py:386
  57.7 4.2 %collective-permute-start.16 = (bf16[256,256]{1,0:T(8,128)(2,1)S(1)}, bf16[256,256]{1,0:T(8,128)(2,1)S(1)}, u32[]{:S(2)}, u32[]{:S(2)}) collective-permute-start(bf16[256,256]{1,0:T(8,128)(2,1)S(1)} %slice.106), channel_id=1, source_target_pairs={{0,14},{1,15},{2,0},{3,1},{4,2},{5,3},{6,4},{7,5},{8,6},{9,7},{10,... | collective-permute-start | bytes 393224 | tf_op jit(solution)/shard_map/ppermute | solution.py:384
  61.9 6.2 %collective-permute-start.3 = (bf16[144,1024]{1,0:T(8,128)(2,1)S(1)}, bf16[144,1024]{1,0:T(8,128)(2,1)S(1)}, u32[]{:S(2)}, u32[]{:S(2)}) collective-permute-start(bf16[144,1024]{1,0:T(8,128)(2,1)S(1)} %shard_map.96.q0), channel_id=1, source_target_pairs={{0,1},{1,0},{2,3},{3,2},{4,5},{5,4},{6,7},{7,6},{8,9},{9,8},{10,11... | collective-permute-start | bytes 884744 | tf_op jit(solution)/shard_map/ppermute | solution.py:362
  68.1 2.7 %shard_map.102 = (f32[4,1,1024]{2,1,0:T(1,128)S(1)}, f32[4,1,1024]{2,1,0:T(1,128)S(1)}, bf16[8,512,1024]{2,1,0:T(8,128)(2,1)S(1)}, f32[16,1,1024]{2,1,0:T(1,128)S(1)}) custom-call(s32[2]{0:T(128)S(1)} %pad_add_fusion.refs_0_.tab, f32[4,1,1024]{2,1,0:T(1,128)S(1)} %get-tuple-element.76.refs_1_, bf16[4,128,1024]{2,1,0:T(8,128)(2,1)S(1)} %get-tuple-element.78.refs_2_, ...), custom_call_target="tpu_custom_call" | custom-call | flops 1073741824 | bytes 2097152 | tf_op jit(solution)/shard_map/pallas_call | solution.py:386
  70.8 1.7 %shard_map.103 = (f32[4,1,1024]{2,1,0:T(1,128)S(1)}, f32[4,1,1024]{2,1,0:T(1,128)S(1)}, bf16[4,512,1024]{2,1,0:T(8,128)(2,1)S(1)}, f32[8,1,1024]{2,1,0:T(1,128)S(1)}) custom-call(s32[2]{0:T(128)S(1)} %pad_add_fusion.refs_0_.tab, f32[4,1,1024]{2,1,0:T(1,128)S(1)} %get-tuple-element.76.refs_1_, bf16[4,128,1024]{2,1,0:T(8,128)(2,1)S(1)} %get-tuple-element.78.refs_2_, ...), custom_call_target="tpu_custom_call" | custom-call | flops 536870912 | bytes 2097152 | tf_op jit(solution)/shard_map/pallas_call | solution.py:386
  72.5 3.8 %collective-permute-start.18 = (f32[8,1,1024]{2,1,0:T(1,128)S(1)}, f32[8,1,1024]{2,1,0:T(1,128)S(1)}, u32[]{:S(2)}, u32[]{:S(2)}) collective-permute-start(f32[8,1,1024]{2,1,0:T(1,128)S(1)} %constant_dynamic-update-slice_fusion.2), channel_id=1, source_target_pairs={{0,16},{1,17},{2,18},{3,19},{4,20},{5,21},{6,22},{7,23},{8,24},{9,... | collective-permute-start | bytes 98312 | tf_op jit(solution)/shard_map/ppermute | solution.py:407
  76.4 0.9 shard_map.97
  77.3 1.6 %collective-permute-start.19 = (f32[8,1,1024]{2,1,0:T(1,128)S(1)}, f32[8,1,1024]{2,1,0:T(1,128)S(1)}, u32[]{:S(2)}, u32[]{:S(2)}) collective-permute-start(f32[8,1,1024]{2,1,0:T(1,128)S(1)} %constant_dynamic-update-slice_fusion.2), channel_id=1, source_target_pairs={{0,17},{1,16},{2,19},{3,18},{4,21},{5,20},{6,23},{7,22},{8,25},{9,... | collective-permute-start | bytes 98312 | tf_op jit(solution)/shard_map/ppermute | solution.py:407
  78.9 1.8 %collective-permute-done.19 = f32[8,1,1024]{2,1,0:T(1,128)S(1)} collective-permute-done((f32[8,1,1024]{2,1,0:T(1,128)S(1)}, f32[8,1,1024]{2,1,0:T(1,128)S(1)}, u32[]{:S(2)}, u32[]{:S(2)}) %collective-permute-start.19) | collective-permute-done | bytes 32800 | tf_op jit(solution)/shard_map/ppermute | solution.py:407
  81.0 2.6 %shard_map.104 = (f32[4,128,1024]{2,1,0:T(8,128)S(1)}, f32[1,512,256]{2,1,0:T(8,128)S(1)}) custom-call(s32[2]{0:T(128)S(1)} %pad_add_fusion.refs_0_.tab, f32[4,1,1024]{2,1,0:T(1,128)S(1)} %get-tuple-element.76.refs_1_, f32[4,1,1024]{2,1,0:T(1,128)S(1)} %get-tuple-element.77.refs_2_, f32[4,1,1024]{2,1,0:T(1,128)S(1)} %multiply_add_fusion.refs_3_, ...), custom_call_target="tpu_custom_call" | custom-call | flops 2684354560 | bytes 8388608 | tf_op jit(solution)/shard_map/pallas_call | solution.py:425
  83.7 4.0 %shard_map.105 = (f32[4,128,1024]{2,1,0:T(8,128)S(1)}, f32[2,512,256]{2,1,0:T(8,128)S(1)}) custom-call(s32[2]{0:T(128)S(1)} %pad_add_fusion.refs_0_.tab, f32[4,1,1024]{2,1,0:T(1,128)S(1)} %get-tuple-element.76.refs_1_, f32[4,1,1024]{2,1,0:T(1,128)S(1)} %get-tuple-element.77.refs_2_, ...), custom_call_target="tpu_custom_call", output_to_operand_aliasing={{0}: (11, {})} | custom-call | flops 5368709120 | bytes 8388608 | tf_op jit(solution)/shard_map/pallas_call | solution.py:425
  87.8 11.5 %collective-permute-done.20 = bf16[512,256]{1,0:T(8,128)(2,1)S(1)} collective-permute-done((bf16[512,256]{1,0:T(8,128)(2,1)S(1)}, bf16[512,256]{1,0:T(8,128)(2,1)S(1)}, u32[]{:S(2)}, u32[]{:S(2)}) %collective-permute-start.20) | collective-permute-done | bytes 262176 | tf_op jit(solution)/shard_map/ppermute | solution.py:441
  99.3 4.3 %collective-permute-start.22 = (bf16[512,256]{1,0:T(8,128)(2,1)S(1)}, bf16[512,256]{1,0:T(8,128)(2,1)S(1)}, u32[]{:S(2)}, u32[]{:S(2)}) collective-permute-start(bf16[512,256]{1,0:T(8,128)(2,1)S(1)} %fusion.8), channel_id=1, source_target_pairs={{0,14},{1,15},{2,0},{3,1},{4,2},{5,3},{6,4},{7,5},{8,6},{9,7},{10,... | collective-permute-start | bytes 786440 | tf_op jit(solution)/shard_map/ppermute | solution.py:443
  103.6 4.0 %shard_map.106 = (f32[4,128,1024]{2,1,0:T(8,128)S(1)}, f32[2,512,256]{2,1,0:T(8,128)S(1)}) custom-call(s32[2]{0:T(128)S(1)} %pad_add_fusion.refs_0_.tab, f32[4,1,1024]{2,1,0:T(1,128)S(1)} %get-tuple-element.76.refs_1_, f32[4,1,1024]{2,1,0:T(1,128)S(1)} %get-tuple-element.77.refs_2_, ...), custom_call_target="tpu_custom_call", output_to_operand_aliasing={{0}: (11, {})} | custom-call | flops 5368709120 | bytes 8388608 | tf_op jit(solution)/shard_map/pallas_call | solution.py:425
  107.6 2.4 %collective-permute-done.21 = bf16[512,256]{1,0:T(8,128)(2,1)S(1)} collective-permute-done((bf16[512,256]{1,0:T(8,128)(2,1)S(1)}, bf16[512,256]{1,0:T(8,128)(2,1)S(1)}, u32[]{:S(2)}, u32[]{:S(2)}) %collective-permute-start.21) | collective-permute-done | bytes 262176 | tf_op jit(solution)/shard_map/ppermute | solution.py:441
  110.1 5.0 %collective-permute-start.24 = (bf16[512,256]{1,0:T(8,128)(2,1)S(1)}, bf16[512,256]{1,0:T(8,128)(2,1)S(1)}, u32[]{:S(2)}, u32[]{:S(2)}) collective-permute-start(bf16[512,256]{1,0:T(8,128)(2,1)S(1)} %get-tuple-element.133), channel_id=1, source_target_pairs={{0,14},{1,15},{2,0},{3,1},{4,2},{5,3},{6,4},{7,5},{8,6},{9,7},{10,... | collective-permute-start | bytes 786440 | tf_op jit(solution)/shard_map/ppermute | solution.py:443
  115.2 5.3 %shard_map.107 = (f32[4,128,1024]{2,1,0:T(8,128)S(1)}, f32[2,512,256]{2,1,0:T(8,128)S(1)}) custom-call(s32[2]{0:T(128)S(1)} %pad_add_fusion.refs_0_.tab, f32[4,1,1024]{2,1,0:T(1,128)S(1)} %get-tuple-element.76.refs_1_, f32[4,1,1024]{2,1,0:T(1,128)S(1)} %get-tuple-element.77.refs_2_, ...), custom_call_target="tpu_custom_call", output_to_operand_aliasing={{0}: (11, {})} | custom-call | flops 5368709120 | bytes 8388608 | tf_op jit(solution)/shard_map/pallas_call | solution.py:425
  120.5 1.1 collective-permute-done.23
  121.8 2.3 %shard_map.108 = (bf16[128,1024]{1,0:T(8,128)(2,1)S(1)}, f32[1,512,256]{2,1,0:T(8,128)S(1)}) custom-call(s32[2]{0:T(128)S(1)} %pad_add_fusion.refs_0_.tab, f32[4,1,1024]{2,1,0:T(1,128)S(1)} %get-tuple-element.76.refs_1_, f32[4,1,1024]{2,1,0:T(1,128)S(1)} %get-tuple-element.77.refs_2_, f32[4,1,1024]{2,1,0:T(1,128)S(1)} %multiply_add_fusion.refs_3_, ...), custom_call_target="tpu_custom_call" | custom-call | flops 2684354560 | bytes 8388608 | tf_op jit(solution)/shard_map/pallas_call | solution.py:425
  124.0 4.2 %collective-permute-start.31 = (bf16[128,1024]{1,0:T(8,128)(2,1)S(1)}, bf16[128,1024]{1,0:T(8,128)(2,1)S(1)}, u32[]{:S(2)}, u32[]{:S(2)}) collective-permute-start(bf16[128,1024]{1,0:T(8,128)(2,1)S(1)} %get-tuple-element.143), channel_id=1, source_target_pairs={{0,1},{1,0},{2,3},{3,2},{4,5},{5,4},{6,7},{7,6},{8,9},{9,8},{10,11... | collective-permute-start | bytes 786440 | tf_op jit(solution)/shard_map/ppermute | solution.py:445
  128.2 4.4 %shard_map.110 = (bf16[128,1024]{1,0:T(8,128)(2,1)S(1)}, bf16[128,1024]{1,0:T(8,128)(2,1)S(1)}, f32[1,512,256]{2,1,0:T(8,128)S(1)}) custom-call(s32[2]{0:T(128)S(1)} %pad_add_fusion.refs_0_.tab, f32[4,1,1024]{2,1,0:T(1,128)S(1)} %get-tuple-element.76.refs_1_, f32[4,1,1024]{2,1,0:T(1,128)S(1)} %get-tuple-element.77.refs_2_, ...), custom_call_target="tpu_custom_call" | custom-call | flops 2684354560 | bytes 8388608 | tf_op jit(solution)/shard_map/pallas_call | solution.py:425
  132.6 5.8 %collective-permute-start.26 = (bf16[512,256]{1,0:T(8,128)(2,1)S(1)}, bf16[512,256]{1,0:T(8,128)(2,1)S(1)}, u32[]{:S(2)}, u32[]{:S(2)}) collective-permute-start(bf16[512,256]{1,0:T(8,128)(2,1)S(1)} %get-tuple-element.139), channel_id=1, source_target_pairs={{0,14},{1,15},{2,0},{3,1},{4,2},{5,3},{6,4},{7,5},{8,6},{9,7},{10,... | collective-permute-start | bytes 786440 | tf_op jit(solution)/shard_map/ppermute | solution.py:443
  138.5 2.3 %shard_map.109 = (bf16[128,1024]{1,0:T(8,128)(2,1)S(1)}, f32[1,512,256]{2,1,0:T(8,128)S(1)}) custom-call(s32[2]{0:T(128)S(1)} %pad_add_fusion.refs_0_.tab, f32[4,1,1024]{2,1,0:T(1,128)S(1)} %get-tuple-element.76.refs_1_, f32[4,1,1024]{2,1,0:T(1,128)S(1)} %get-tuple-element.77.refs_2_, f32[4,1,1024]{2,1,0:T(1,128)S(1)} %multiply_add_fusion.refs_3_, ...), custom_call_target="tpu_custom_call" | custom-call | flops 2684354560 | bytes 8388608 | tf_op jit(solution)/shard_map/pallas_call | solution.py:425
  141.3 2.8 %collective-permute-done.26 = bf16[512,256]{1,0:T(8,128)(2,1)S(1)} collective-permute-done((bf16[512,256]{1,0:T(8,128)(2,1)S(1)}, bf16[512,256]{1,0:T(8,128)(2,1)S(1)}, u32[]{:S(2)}, u32[]{:S(2)}) %collective-permute-start.26) | collective-permute-done | bytes 262176 | tf_op jit(solution)/shard_map/ppermute | solution.py:443
  144.1 3.1 %collective-permute-done.25 = bf16[512,256]{1,0:T(8,128)(2,1)S(1)} collective-permute-done((bf16[512,256]{1,0:T(8,128)(2,1)S(1)}, bf16[512,256]{1,0:T(8,128)(2,1)S(1)}, u32[]{:S(2)}, u32[]{:S(2)}) %collective-permute-start.25) | collective-permute-done | bytes 262176 | tf_op jit(solution)/shard_map/ppermute | solution.py:441
  147.4 1.2 collective-permute-start.27
  148.7 1.7 %collective-permute-start.29 = (bf16[128,256]{1,0:T(8,128)(2,1)S(1)}, bf16[128,256]{1,0:T(8,128)(2,1)S(1)}, u32[]{:S(2)}, u32[]{:S(2)}) collective-permute-start(bf16[128,256]{1,0:T(8,128)(2,1)S(1)} %get-tuple-element.151), channel_id=1, source_target_pairs={{0,17},{1,16},{2,19},{3,18},{4,21},{5,20},{6,23},{7,22},{8,25},{9,... | collective-permute-start | bytes 196616 | tf_op jit(solution)/shard_map/ppermute | solution.py:454
  150.4 1.8 %collective-permute-done.28.a2 = bf16[128,256]{1,0:T(8,128)(2,1)S(1)} collective-permute-done((bf16[128,256]{1,0:T(8,128)(2,1)S(1)}, bf16[128,256]{1,0:T(8,128)(2,1)S(1)}, u32[]{:S(2)}, u32[]{:S(2)}) %collective-permute-start.28) | collective-permute-done | bytes 65568 | tf_op jit(solution)/shard_map/ppermute | solution.py:454
  152.2 1.7 %collective-permute-done.29.a3 = bf16[128,256]{1,0:T(8,128)(2,1)S(1)} collective-permute-done((bf16[128,256]{1,0:T(8,128)(2,1)S(1)}, bf16[128,256]{1,0:T(8,128)(2,1)S(1)}, u32[]{:S(2)}, u32[]{:S(2)}) %collective-permute-start.29) | collective-permute-done | bytes 65568 | tf_op jit(solution)/shard_map/ppermute | solution.py:454
  153.9 1.4 shard_map.111
  (67 shorter events, 3.1 us)
Async XLA Ops:
  0.6 44.4 %copy-start.1 = (bf16[1,128,1024]{2,1,0:T(8,128)(2,1)S(1)}, bf16[1,128,1024]{2,1,0:T(8,128)(2,1)}, u32[]{:S(2)}) copy-start(bf16[1,128,1024]{2,1,0:T(8,128)(2,1)} %param.10) | copy-start | bytes 786436
  0.6 44.4 %copy-start.2 = (bf16[1,128,1024]{2,1,0:T(8,128)(2,1)S(1)}, bf16[1,128,1024]{2,1,0:T(8,128)(2,1)}, u32[]{:S(2)}) copy-start(bf16[1,128,1024]{2,1,0:T(8,128)(2,1)} %param.11) | copy-start | bytes 786436
  4.0 19.0 %collective-permute-start.1 = (bf16[144,1024]{1,0:T(8,128)(2,1)}, bf16[144,1024]{1,0:T(8,128)(2,1)S(1)}, u32[]{:S(2)}, u32[]{:S(2)}) collective-permute-start(bf16[144,1024]{1,0:T(8,128)(2,1)} %get-tuple-element.75.q0), channel_id=1, source_target_pairs={{0,16},{1,17},{2,18},{3,19},{4,20},{5,21},{6,22},{7,23},{8,24},{9,... | collective-permute-start | bytes 884744 | tf_op jit(solution)/shard_map/ppermute | solution.py:360
  4.5 2.6 %collective-permute-start.6 = (bf16[144,256]{1,0:T(8,128)(2,1)}, bf16[144,256]{1,0:T(8,128)(2,1)S(1)}, u32[]{:S(2)}, u32[]{:S(2)}) collective-permute-start(bf16[144,256]{1,0:T(8,128)(2,1)} %get-tuple-element.80), channel_id=1, source_target_pairs={{0,1},{1,0},{2,3},{3,2},{4,5},{5,4},{6,7},{7,6},{8,9},{9,8},{10,11... | collective-permute-start | bytes 221192 | tf_op jit(solution)/shard_map/ppermute | solution.py:356
  5.5 8.3 %collective-permute-start.7 = (bf16[144,256]{1,0:T(8,128)(2,1)}, bf16[144,256]{1,0:T(8,128)(2,1)S(1)}, u32[]{:S(2)}, u32[]{:S(2)}) collective-permute-start(bf16[144,256]{1,0:T(8,128)(2,1)} %get-tuple-element.81), channel_id=1, source_target_pairs={{0,16},{1,17},{2,18},{3,19},{4,20},{5,21},{6,22},{7,23},{8,24},{9,... | collective-permute-start | bytes 221192 | tf_op jit(solution)/shard_map/ppermute | solution.py:356
  6.5 9.7 %collective-permute-start.8 = (bf16[144,256]{1,0:T(8,128)(2,1)}, bf16[144,256]{1,0:T(8,128)(2,1)S(1)}, u32[]{:S(2)}, u32[]{:S(2)}) collective-permute-start(bf16[144,256]{1,0:T(8,128)(2,1)} %get-tuple-element.82), channel_id=1, source_target_pairs={{0,17},{1,16},{2,19},{3,18},{4,21},{5,20},{6,23},{7,22},{8,25},{9,... | collective-permute-start | bytes 221192 | tf_op jit(solution)/shard_map/ppermute | solution.py:356
  16.1 0.9 copy-start.3
  17.1 12.6 %collective-permute-start.9 = (bf16[528,256]{1,0:T(8,128)(2,1)S(1)}, bf16[528,256]{1,0:T(8,128)(2,1)S(1)}, u32[]{:S(2)}, u32[]{:S(2)}) collective-permute-start(bf16[528,256]{1,0:T(8,128)(2,1)S(1)} %shard_map.98.refs_5_.refs_9_), channel_id=1, source_target_pairs={{0,2},{1,3},{2,4},{3,5},{4,6},{5,7},{6,8},{7,9},{8,10},{9,11},{10,... | collective-permute-start | bytes 811016 | tf_op jit(solution)/shard_map/ppermute | solution.py:382
  18.8 10.9 %collective-permute-start.11 = (bf16[528,256]{1,0:T(8,128)(2,1)S(1)}, bf16[528,256]{1,0:T(8,128)(2,1)S(1)}, u32[]{:S(2)}, u32[]{:S(2)}) collective-permute-start(bf16[528,256]{1,0:T(8,128)(2,1)S(1)} %shard_map.98.refs_5_.refs_9_), channel_id=1, source_target_pairs={{0,14},{1,15},{2,0},{3,1},{4,2},{5,3},{6,4},{7,5},{8,6},{9,7},{10,... | collective-permute-start | bytes 811016 | tf_op jit(solution)/shard_map/ppermute | solution.py:382
  22.8 9.6 %collective-permute-start = (bf16[144,1024]{1,0:T(8,128)(2,1)}, bf16[144,1024]{1,0:T(8,128)(2,1)S(1)}, u32[]{:S(2)}, u32[]{:S(2)}) collective-permute-start(bf16[144,1024]{1,0:T(8,128)(2,1)} %get-tuple-element.75.q0), channel_id=1, source_target_pairs={{0,1},{1,0},{2,3},{3,2},{4,5},{5,4},{6,7},{7,6},{8,9},{9,8},{10,11... | collective-permute-start | bytes 884744 | tf_op jit(solution)/shard_map/ppermute | solution.py:362
  23.0 9.4 %collective-permute-start.2 = (bf16[144,1024]{1,0:T(8,128)(2,1)S(1)}, bf16[144,1024]{1,0:T(8,128)(2,1)S(1)}, u32[]{:S(2)}, u32[]{:S(2)}) collective-permute-start(bf16[144,1024]{1,0:T(8,128)(2,1)S(1)} %collective-permute-done.1.q2), channel_id=1, source_target_pairs={{0,1},{1,0},{2,3},{3,2},{4,5},{5,4},{6,7},{7,6},{8,9},{9,8},{10,11... | collective-permute-start | bytes 884744 | tf_op jit(solution)/shard_map/ppermute | solution.py:361
  29.7 12.6 %collective-permute-start.10 = (bf16[528,256]{1,0:T(8,128)(2,1)S(1)}, bf16[528,256]{1,0:T(8,128)(2,1)S(1)}, u32[]{:S(2)}, u32[]{:S(2)}) collective-permute-start(bf16[528,256]{1,0:T(8,128)(2,1)S(1)} %collective-permute-done.9.refs_6_.refs_10_), channel_id=1, source_target_pairs={{0,2},{1,3},{2,4},{3,5},{4,6},{5,7},{6,8},{7,9},{8,10},{9,11},{10,... | collective-permute-start | bytes 811016 | tf_op jit(solution)/shard_map/ppermute | solution.py:382
  29.7 12.6 %collective-permute-start.12 = (bf16[528,256]{1,0:T(8,128)(2,1)S(1)}, bf16[528,256]{1,0:T(8,128)(2,1)S(1)}, u32[]{:S(2)}, u32[]{:S(2)}) collective-permute-start(bf16[528,256]{1,0:T(8,128)(2,1)S(1)} %collective-permute-done.11.refs_5_.refs_9_), channel_id=1, source_target_pairs={{0,14},{1,15},{2,0},{3,1},{4,2},{5,3},{6,4},{7,5},{8,6},{9,7},{10,... | collective-permute-start | bytes 811016 | tf_op jit(solution)/shard_map/ppermute | solution.py:382
  32.4 1.0 copy-start
  42.3 15.3 %collective-permute-start.13 = (bf16[528,256]{1,0:T(8,128)(2,1)S(1)}, bf16[528,256]{1,0:T(8,128)(2,1)S(1)}, u32[]{:S(2)}, u32[]{:S(2)}) collective-permute-start(bf16[528,256]{1,0:T(8,128)(2,1)S(1)} %collective-permute-done.10.refs_6_.refs_10_), channel_id=1, source_target_pairs={{0,2},{1,3},{2,4},{3,5},{4,6},{5,7},{6,8},{7,9},{8,10},{9,11},{10,... | collective-permute-start | bytes 811016 | tf_op jit(solution)/shard_map/ppermute | solution.py:382
  42.4 15.2 %collective-permute-start.14 = (bf16[528,256]{1,0:T(8,128)(2,1)S(1)}, bf16[528,256]{1,0:T(8,128)(2,1)S(1)}, u32[]{:S(2)}, u32[]{:S(2)}) collective-permute-start(bf16[528,256]{1,0:T(8,128)(2,1)S(1)} %collective-permute-done.12.refs_5_.refs_9_), channel_id=1, source_target_pairs={{0,14},{1,15},{2,0},{3,1},{4,2},{5,3},{6,4},{7,5},{8,6},{9,7},{10,... | collective-permute-start | bytes 811016 | tf_op jit(solution)/shard_map/ppermute | solution.py:382
  45.2 22.8 %collective-permute-start.4 = (bf16[144,1024]{1,0:T(8,128)(2,1)S(1)}, bf16[144,1024]{1,0:T(8,128)(2,1)S(1)}, u32[]{:S(2)}, u32[]{:S(2)}) collective-permute-start(bf16[144,1024]{1,0:T(8,128)(2,1)S(1)} %shard_map.96.q0), channel_id=1, source_target_pairs={{0,16},{1,17},{2,18},{3,19},{4,20},{5,21},{6,22},{7,23},{8,24},{9,... | collective-permute-start | bytes 884744 | tf_op jit(solution)/shard_map/ppermute | solution.py:360
  57.6 13.2 %collective-permute-start.15 = (bf16[272,256]{1,0:T(8,128)(2,1)S(1)}, bf16[272,256]{1,0:T(8,128)(2,1)S(1)}, u32[]{:S(2)}, u32[]{:S(2)}) collective-permute-start(bf16[272,256]{1,0:T(8,128)(2,1)S(1)} %slice.105), channel_id=1, source_target_pairs={{0,2},{1,3},{2,4},{3,5},{4,6},{5,7},{6,8},{7,9},{8,10},{9,11},{10,... | collective-permute-start | bytes 417800 | tf_op jit(solution)/shard_map/ppermute | solution.py:384
  57.7 13.0 %collective-permute-start.16 = (bf16[256,256]{1,0:T(8,128)(2,1)S(1)}, bf16[256,256]{1,0:T(8,128)(2,1)S(1)}, u32[]{:S(2)}, u32[]{:S(2)}) collective-permute-start(bf16[256,256]{1,0:T(8,128)(2,1)S(1)} %slice.106), channel_id=1, source_target_pairs={{0,14},{1,15},{2,0},{3,1},{4,2},{5,3},{6,4},{7,5},{8,6},{9,7},{10,... | collective-permute-start | bytes 393224 | tf_op jit(solution)/shard_map/ppermute | solution.py:384
  61.9 14.5 %collective-permute-start.3 = (bf16[144,1024]{1,0:T(8,128)(2,1)S(1)}, bf16[144,1024]{1,0:T(8,128)(2,1)S(1)}, u32[]{:S(2)}, u32[]{:S(2)}) collective-permute-start(bf16[144,1024]{1,0:T(8,128)(2,1)S(1)} %shard_map.96.q0), channel_id=1, source_target_pairs={{0,1},{1,0},{2,3},{3,2},{4,5},{5,4},{6,7},{7,6},{8,9},{9,8},{10,11... | collective-permute-start | bytes 884744 | tf_op jit(solution)/shard_map/ppermute | solution.py:362
  68.1 8.3 %collective-permute-start.5 = (bf16[144,1024]{1,0:T(8,128)(2,1)S(1)}, bf16[144,1024]{1,0:T(8,128)(2,1)S(1)}, u32[]{:S(2)}, u32[]{:S(2)}) collective-permute-start(bf16[144,1024]{1,0:T(8,128)(2,1)S(1)} %collective-permute-done.4.q2), channel_id=1, source_target_pairs={{0,1},{1,0},{2,3},{3,2},{4,5},{5,4},{6,7},{7,6},{8,9},{9,8},{10,11... | collective-permute-start | bytes 884744 | tf_op jit(solution)/shard_map/ppermute | solution.py:361
  72.5 6.4 %collective-permute-start.18 = (f32[8,1,1024]{2,1,0:T(1,128)S(1)}, f32[8,1,1024]{2,1,0:T(1,128)S(1)}, u32[]{:S(2)}, u32[]{:S(2)}) collective-permute-start(f32[8,1,1024]{2,1,0:T(1,128)S(1)} %constant_dynamic-update-slice_fusion.2), channel_id=1, source_target_pairs={{0,16},{1,17},{2,18},{3,19},{4,20},{5,21},{6,22},{7,23},{8,24},{9,... | collective-permute-start | bytes 98312 | tf_op jit(solution)/shard_map/ppermute | solution.py:407
  77.3 3.4 %collective-permute-start.19 = (f32[8,1,1024]{2,1,0:T(1,128)S(1)}, f32[8,1,1024]{2,1,0:T(1,128)S(1)}, u32[]{:S(2)}, u32[]{:S(2)}) collective-permute-start(f32[8,1,1024]{2,1,0:T(1,128)S(1)} %constant_dynamic-update-slice_fusion.2), channel_id=1, source_target_pairs={{0,17},{1,16},{2,19},{3,18},{4,21},{5,20},{6,23},{7,22},{8,25},{9,... | collective-permute-start | bytes 98312 | tf_op jit(solution)/shard_map/ppermute | solution.py:407
  78.9 1.8 %collective-permute-start.17 = (f32[8,1,1024]{2,1,0:T(1,128)S(1)}, f32[8,1,1024]{2,1,0:T(1,128)S(1)}, u32[]{:S(2)}, u32[]{:S(2)}) collective-permute-start(f32[8,1,1024]{2,1,0:T(1,128)S(1)} %constant_dynamic-update-slice_fusion.2), channel_id=1, source_target_pairs={{0,1},{1,0},{2,3},{3,2},{4,5},{5,4},{6,7},{7,6},{8,9},{9,8},{10,11... | collective-permute-start | bytes 98312 | tf_op jit(solution)/shard_map/ppermute | solution.py:407
  83.6 15.6 %collective-permute-start.20 = (bf16[512,256]{1,0:T(8,128)(2,1)S(1)}, bf16[512,256]{1,0:T(8,128)(2,1)S(1)}, u32[]{:S(2)}, u32[]{:S(2)}) collective-permute-start(bf16[512,256]{1,0:T(8,128)(2,1)S(1)} %convert_bitcast_fusion), channel_id=1, source_target_pairs={{0,2},{1,3},{2,4},{3,5},{4,6},{5,7},{6,8},{7,9},{8,10},{9,11},{10,... | collective-permute-start | bytes 786440 | tf_op jit(solution)/shard_map/ppermute | solution.py:441
  99.3 8.3 %collective-permute-start.22 = (bf16[512,256]{1,0:T(8,128)(2,1)S(1)}, bf16[512,256]{1,0:T(8,128)(2,1)S(1)}, u32[]{:S(2)}, u32[]{:S(2)}) collective-permute-start(bf16[512,256]{1,0:T(8,128)(2,1)S(1)} %fusion.8), channel_id=1, source_target_pairs={{0,14},{1,15},{2,0},{3,1},{4,2},{5,3},{6,4},{7,5},{8,6},{9,7},{10,... | collective-permute-start | bytes 786440 | tf_op jit(solution)/shard_map/ppermute | solution.py:443
  103.6 6.4 %collective-permute-start.21 = (bf16[512,256]{1,0:T(8,128)(2,1)S(1)}, bf16[512,256]{1,0:T(8,128)(2,1)S(1)}, u32[]{:S(2)}, u32[]{:S(2)}) collective-permute-start(bf16[512,256]{1,0:T(8,128)(2,1)S(1)} %fusion.7), channel_id=1, source_target_pairs={{0,2},{1,3},{2,4},{3,5},{4,6},{5,7},{6,8},{7,9},{8,10},{9,11},{10,... | collective-permute-start | bytes 786440 | tf_op jit(solution)/shard_map/ppermute | solution.py:441
  110.1 10.4 %collective-permute-start.24 = (bf16[512,256]{1,0:T(8,128)(2,1)S(1)}, bf16[512,256]{1,0:T(8,128)(2,1)S(1)}, u32[]{:S(2)}, u32[]{:S(2)}) collective-permute-start(bf16[512,256]{1,0:T(8,128)(2,1)S(1)} %get-tuple-element.133), channel_id=1, source_target_pairs={{0,14},{1,15},{2,0},{3,1},{4,2},{5,3},{6,4},{7,5},{8,6},{9,7},{10,... | collective-permute-start | bytes 786440 | tf_op jit(solution)/shard_map/ppermute | solution.py:443
  115.2 6.4 %collective-permute-start.23 = (bf16[512,256]{1,0:T(8,128)(2,1)S(1)}, bf16[512,256]{1,0:T(8,128)(2,1)S(1)}, u32[]{:S(2)}, u32[]{:S(2)}) collective-permute-start(bf16[512,256]{1,0:T(8,128)(2,1)S(1)} %get-tuple-element.132), channel_id=1, source_target_pairs={{0,2},{1,3},{2,4},{3,5},{4,6},{5,7},{6,8},{7,9},{8,10},{9,11},{10,... | collective-permute-start | bytes 786440 | tf_op jit(solution)/shard_map/ppermute | solution.py:441
  124.0 17.1 %collective-permute-start.31 = (bf16[128,1024]{1,0:T(8,128)(2,1)S(1)}, bf16[128,1024]{1,0:T(8,128)(2,1)S(1)}, u32[]{:S(2)}, u32[]{:S(2)}) collective-permute-start(bf16[128,1024]{1,0:T(8,128)(2,1)S(1)} %get-tuple-element.143), channel_id=1, source_target_pairs={{0,1},{1,0},{2,3},{3,2},{4,5},{5,4},{6,7},{7,6},{8,9},{9,8},{10,11... | collective-permute-start | bytes 786440 | tf_op jit(solution)/shard_map/ppermute | solution.py:445
  132.6 11.5 %collective-permute-start.26 = (bf16[512,256]{1,0:T(8,128)(2,1)S(1)}, bf16[512,256]{1,0:T(8,128)(2,1)S(1)}, u32[]{:S(2)}, u32[]{:S(2)}) collective-permute-start(bf16[512,256]{1,0:T(8,128)(2,1)S(1)} %get-tuple-element.139), channel_id=1, source_target_pairs={{0,14},{1,15},{2,0},{3,1},{4,2},{5,3},{6,4},{7,5},{8,6},{9,7},{10,... | collective-permute-start | bytes 786440 | tf_op jit(solution)/shard_map/ppermute | solution.py:443
  138.4 8.8 %collective-permute-start.25 = (bf16[512,256]{1,0:T(8,128)(2,1)S(1)}, bf16[512,256]{1,0:T(8,128)(2,1)S(1)}, u32[]{:S(2)}, u32[]{:S(2)}) collective-permute-start(bf16[512,256]{1,0:T(8,128)(2,1)S(1)} %get-tuple-element.138), channel_id=1, source_target_pairs={{0,2},{1,3},{2,4},{3,5},{4,6},{5,7},{6,8},{7,9},{8,10},{9,11},{10,... | collective-permute-start | bytes 786440 | tf_op jit(solution)/shard_map/ppermute | solution.py:441
  140.7 9.7 %collective-permute-start.30 = (bf16[128,1024]{1,0:T(8,128)(2,1)S(1)}, bf16[128,1024]{1,0:T(8,128)(2,1)S(1)}, u32[]{:S(2)}, u32[]{:S(2)}) collective-permute-start(bf16[128,1024]{1,0:T(8,128)(2,1)S(1)} %get-tuple-element.141), channel_id=1, source_target_pairs={{0,1},{1,0},{2,3},{3,2},{4,5},{5,4},{6,7},{7,6},{8,9},{9,8},{10,11... | collective-permute-start | bytes 786440 | tf_op jit(solution)/shard_map/ppermute | solution.py:453
  141.2 12.7 %collective-permute-start.32 = (bf16[128,1024]{1,0:T(8,128)(2,1)S(1)}, bf16[128,1024]{1,0:T(8,128)(2,1)S(1)}, u32[]{:S(2)}, u32[]{:S(2)}) collective-permute-start(bf16[128,1024]{1,0:T(8,128)(2,1)S(1)} %add_convert_fusion), channel_id=1, source_target_pairs={{0,16},{1,17},{2,18},{3,19},{4,20},{5,21},{6,22},{7,23},{8,24},{9,... | collective-permute-start | bytes 786440 | tf_op jit(solution)/shard_map/ppermute | solution.py:448
  147.4 3.0 %collective-permute-start.27 = (bf16[128,256]{1,0:T(8,128)(2,1)S(1)}, bf16[128,256]{1,0:T(8,128)(2,1)S(1)}, u32[]{:S(2)}, u32[]{:S(2)}) collective-permute-start(bf16[128,256]{1,0:T(8,128)(2,1)S(1)} %get-tuple-element.153), channel_id=1, source_target_pairs={{0,1},{1,0},{2,3},{3,2},{4,5},{5,4},{6,7},{7,6},{8,9},{9,8},{10,11... | collective-permute-start | bytes 196616 | tf_op jit(solution)/shard_map/ppermute | solution.py:454
  148.7 3.5 %collective-permute-start.28 = (bf16[128,256]{1,0:T(8,128)(2,1)S(1)}, bf16[128,256]{1,0:T(8,128)(2,1)S(1)}, u32[]{:S(2)}, u32[]{:S(2)}) collective-permute-start(bf16[128,256]{1,0:T(8,128)(2,1)S(1)} %get-tuple-element.152), channel_id=1, source_target_pairs={{0,16},{1,17},{2,18},{3,19},{4,20},{5,21},{6,22},{7,23},{8,24},{9,... | collective-permute-start | bytes 196616 | tf_op jit(solution)/shard_map/ppermute | solution.py:454
  148.7 5.2 %collective-permute-start.29 = (bf16[128,256]{1,0:T(8,128)(2,1)S(1)}, bf16[128,256]{1,0:T(8,128)(2,1)S(1)}, u32[]{:S(2)}, u32[]{:S(2)}) collective-permute-start(bf16[128,256]{1,0:T(8,128)(2,1)S(1)} %get-tuple-element.151), channel_id=1, source_target_pairs={{0,17},{1,16},{2,19},{3,18},{4,21},{5,20},{6,23},{7,22},{8,25},{9,... | collective-permute-start | bytes 196616 | tf_op jit(solution)/shard_map/ppermute | solution.py:454

commit v5 on v4

--- a/solution.py
+++ b/solution.py
@@ -258,7 +258,7 @@
 
     def attempt(_):
         sum_ref[...] = jnp.zeros_like(sum_ref)
-        items(ks, (0, 1, 2, 3), tab, tag_ref, kv, later_body, True, ks[0] != 2)
+        items(ks, (0, 1, 2, 3), tab, tag_ref, kv, later_body, True)
         sums = sum_ref[...]
         step = jnp.where(sums > 2.0**100, 80.0, jnp.where(sums > 2.0**40, 26.0, 0.0))
         m_ref[...] += step * (1.0 / C2)
@@ -441,17 +441,15 @@
         up = hop(sends[0], perm=turn(1))
         if n == 2:
             down = hop(sends[1], perm=turn(-1))
-    dq3, adds3 = grads((0,), (3,), dq)
-    dq3 = hop(dq3, perm=flip(1))
-    dq2, adds2 = grads((0,), (2,), dq)
-    across = (dq2.astype(F32) + dq3.astype(F32)).astype(BF16)
-    dq_far = hop(across, perm=flip(2))
-    dq0, dq1, adds0 = grads((0,), (0, 1), dq)
-    own = adds3[0] + adds2[0] + adds0[0] + up.astype(F32) + down.astype(F32)
+    *dq_four, adds0 = grads((0,), (0, 1, 2, 3), dq)
+    dq3 = hop(dq_four[3], perm=flip(1))
+    own = adds0[0] + up.astype(F32) + down.astype(F32)
     scales = jnp.where(jnp.arange(2 * HD) < HD, SCALE, 1.0).astype(F32)
     own = (own * scales[None, :]).astype(BF16)
-    q_back = [dq0, hop(dq1, perm=flip(1)), dq_far]
     a_back = [own[0:128]] + [hop(own[128 * r : 128 * r + 128], perm=flip(r)) for r in (1, 2, 3)]
+    across = (dq_four[2].astype(F32) + dq3.astype(F32)).astype(BF16)
+    dq_far = hop(across, perm=flip(2))
+    q_back = [dq_four[0], hop(dq_four[1], perm=flip(1)), dq_far]
     gq, gk, gv = call(
         place_body, [shape((NQ, H * HD)), shape((NK, HD)), shape((NK, HD))], [SM] + [VM] * 7,
         nbytes=2 * MIB,

time: 155 us -> 154 us (level)
  the two profiles are of different devices: /device:TPU:27 before, /device:TPU:5 now
where the time goes in v5:
time: 154 us
  starting transfers between devices  60.9 us (40%)
  Pallas kernels  46.3 us (30%)
  waiting for transfers between devices  42 us (27%)
  local copies, waits for them, and re-layouts  1.99 us (1%)
    pallas_call x5, Pallas kernels, grads(): call(functools.partial(grads_body, ks, rhos, first, last), ([piece] * len...  21.5 us
    pallas_call x5, Pallas kernels, per_device(): call(functools.partial(stats_body, ks), [stat, stat, shape((4 * n, NK, NQ...  18.6 us
    ppermute x4, waiting for transfers between devices, per_device(): up = hop(sends[0], perm=turn(1))  16.8 us
    ppermute x3, starting transfers between devices, per_device(): down = hop(sends[1], perm=turn(-1))  14.7 us
    ppermute x6, starting transfers between devices, per_device(): fwd, bwd = (hop(fwd, perm=turn(1)), hop(bwd, perm=turn(-1)))  14.3 us
    ppermute x2, starting transfers between devices, four(): return (x, hop(x, perm=flip(1)), other, last)  12.4 us
    ppermute x3, waiting for transfers between devices, per_device(): got = [hop(parts[r], perm=flip(r)) for r in (1, 2, 3)]  8.22 us
    ppermute x6, waiting for transfers between devices, per_device(): fwd, bwd = (hop(fwd, perm=turn(1)), hop(bwd, perm=turn(-1)))  6.36 us
  transfers between devices with their start and end apart: 33, of which 12 were waited for; matrix products, arithmetic and copies ran while one was open for 0% of the time, Pallas kernels for 22%

profile of v5, /device:TPU:5, one launch (start us, length us, event | category | flops | bytes accessed | tf_op | source)
XLA Modules:
  0.0 153.6 jit_solution(8019840714184823346)
XLA Ops:
  0.7 0.6 pad_add_fusion.1.tab
  1.3 2.6 %shard_map.94 = (bf16[144,256]{1,0:T(8,128)(2,1)}, bf16[144,256]{1,0:T(8,128)(2,1)}, bf16[144,256]{1,0:T(8,128)(2,1)}, bf16[144,256]{1,0:T(8,128)(2,1)}, bf16[144,1024]{1,0:T(8,128)(2,1)}) custom-call(s32[2]{0:T(128)} %pad_add_fusion.1.tab, bf16[512,128]{1,0:T(8,128)(2,1)} %bitcast.47, bf16[512,128]{1,0:T(8,128)(2,1)} %bitcast.48, s32[1,512]{1,0:T(1,128)} %seg_hbm.1, ...), custom_call_target="tpu_custom_call" | custom-call | bytes 1048576 | tf_op jit(solution)/shard_map/pallas_call | solution.py:348
  3.9 1.4 collective-permute-start.1
  5.3 1.0 collective-permute-start.6
  6.4 1.5 collective-permute-start.8
  7.9 5.8 %collective-permute-done.7.p2 = bf16[144,256]{1,0:T(8,128)(2,1)S(1)} collective-permute-done((bf16[144,256]{1,0:T(8,128)(2,1)}, bf16[144,256]{1,0:T(8,128)(2,1)S(1)}, u32[]{:S(2)}, u32[]{:S(2)}) %collective-permute-start.7) | collective-permute-done | bytes 73760 | tf_op jit(solution)/shard_map/ppermute | solution.py:356
  13.7 2.4 %collective-permute-done.8.p3 = bf16[144,256]{1,0:T(8,128)(2,1)S(1)} collective-permute-done((bf16[144,256]{1,0:T(8,128)(2,1)}, bf16[144,256]{1,0:T(8,128)(2,1)S(1)}, u32[]{:S(2)}, u32[]{:S(2)}) %collective-permute-start.8) | collective-permute-done | bytes 73760 | tf_op jit(solution)/shard_map/ppermute | solution.py:356
  16.1 0.9 copy-done.3
  17.0 1.7 %collective-permute-start.9 = (bf16[528,256]{1,0:T(8,128)(2,1)S(1)}, bf16[528,256]{1,0:T(8,128)(2,1)S(1)}, u32[]{:S(2)}, u32[]{:S(2)}) collective-permute-start(bf16[528,256]{1,0:T(8,128)(2,1)S(1)} %shard_map.98.refs_5_.refs_9_), channel_id=1, source_target_pairs={{0,2},{1,3},{2,4},{3,5},{4,6},{5,7},{6,8},{7,9},{8,10},{9,11},{10,... | collective-permute-start | bytes 811016 | tf_op jit(solution)/shard_map/ppermute | solution.py:382
  18.7 4.0 %collective-permute-start.11 = (bf16[528,256]{1,0:T(8,128)(2,1)S(1)}, bf16[528,256]{1,0:T(8,128)(2,1)S(1)}, u32[]{:S(2)}, u32[]{:S(2)}) collective-permute-start(bf16[528,256]{1,0:T(8,128)(2,1)S(1)} %shard_map.98.refs_5_.refs_9_), channel_id=1, source_target_pairs={{0,14},{1,15},{2,0},{3,1},{4,2},{5,3},{6,4},{7,5},{8,6},{9,7},{10,... | collective-permute-start | bytes 811016 | tf_op jit(solution)/shard_map/ppermute | solution.py:382
  23.3 6.3 %collective-permute-done.9.refs_6_.refs_10_ = bf16[528,256]{1,0:T(8,128)(2,1)S(1)} collective-permute-done((bf16[528,256]{1,0:T(8,128)(2,1)S(1)}, bf16[528,256]{1,0:T(8,128)(2,1)S(1)}, u32[]{:S(2)}, u32[]{:S(2)}) %collective-permute-start.9) | collective-permute-done | bytes 270368 | tf_op jit(solution)/shard_map/ppermute | solution.py:382
  29.6 2.7 %collective-permute-start.12 = (bf16[528,256]{1,0:T(8,128)(2,1)S(1)}, bf16[528,256]{1,0:T(8,128)(2,1)S(1)}, u32[]{:S(2)}, u32[]{:S(2)}) collective-permute-start(bf16[528,256]{1,0:T(8,128)(2,1)S(1)} %collective-permute-done.11.refs_5_.refs_9_), channel_id=1, source_target_pairs={{0,14},{1,15},{2,0},{3,1},{4,2},{5,3},{6,4},{7,5},{8,6},{9,7},{10,... | collective-permute-start | bytes 811016 | tf_op jit(solution)/shard_map/ppermute | solution.py:382
  32.4 1.0 copy-done
  33.3 0.9 shard_map.95
  34.3 4.1 %shard_map.99 = (f32[4,1,1024]{2,1,0:T(1,128)S(1)}, f32[4,1,1024]{2,1,0:T(1,128)S(1)}, bf16[4,512,1024]{2,1,0:T(8,128)(2,1)S(1)}, f32[8,1,1024]{2,1,0:T(1,128)S(1)}) custom-call(s32[2]{0:T(128)S(1)} %pad_add_fusion.refs_0_.tab, f32[4,1,1024]{2,1,0:T(1,128)S(1)} %get-tuple-element.74.refs_1_, bf16[4,128,1024]{2,1,0:T(8,128)(2,1)S(1)} %get-tuple-element.76.refs_2_, ...), custom_call_target="tpu_custom_call" | custom-call | flops 536870912 | bytes 2097152 | tf_op jit(solution)/shard_map/pallas_call | solution.py:386
  38.4 3.5 %shard_map.100 = (f32[4,1,1024]{2,1,0:T(1,128)S(1)}, f32[4,1,1024]{2,1,0:T(1,128)S(1)}, bf16[8,512,1024]{2,1,0:T(8,128)(2,1)S(1)}, f32[16,1,1024]{2,1,0:T(1,128)S(1)}) custom-call(s32[2]{0:T(128)S(1)} %pad_add_fusion.refs_0_.tab, f32[4,1,1024]{2,1,0:T(1,128)S(1)} %get-tuple-element.74.refs_1_, bf16[4,128,1024]{2,1,0:T(8,128)(2,1)S(1)} %get-tuple-element.76.refs_2_, ...), custom_call_target="tpu_custom_call" | custom-call | flops 1073741824 | bytes 2097152 | tf_op jit(solution)/shard_map/pallas_call | solution.py:386
  41.9 5.8 %collective-permute-start.14 = (bf16[528,256]{1,0:T(8,128)(2,1)S(1)}, bf16[528,256]{1,0:T(8,128)(2,1)S(1)}, u32[]{:S(2)}, u32[]{:S(2)}) collective-permute-start(bf16[528,256]{1,0:T(8,128)(2,1)S(1)} %collective-permute-done.12.refs_5_.refs_9_), channel_id=1, source_target_pairs={{0,14},{1,15},{2,0},{3,1},{4,2},{5,3},{6,4},{7,5},{8,6},{9,7},{10,... | collective-permute-start | bytes 811016 | tf_op jit(solution)/shard_map/ppermute | solution.py:382
  48.1 4.7 %shard_map.101 = (f32[4,1,1024]{2,1,0:T(1,128)S(1)}, f32[4,1,1024]{2,1,0:T(1,128)S(1)}, bf16[8,512,1024]{2,1,0:T(8,128)(2,1)S(1)}, f32[16,1,1024]{2,1,0:T(1,128)S(1)}) custom-call(s32[2]{0:T(128)S(1)} %pad_add_fusion.refs_0_.tab, f32[4,1,1024]{2,1,0:T(1,128)S(1)} %get-tuple-element.74.refs_1_, bf16[4,128,1024]{2,1,0:T(8,128)(2,1)S(1)} %get-tuple-element.76.refs_2_, ...), custom_call_target="tpu_custom_call" | custom-call | flops 1073741824 | bytes 2097152 | tf_op jit(solution)/shard_map/pallas_call | solution.py:386
  52.9 5.1 %collective-permute-start.16 = (bf16[256,256]{1,0:T(8,128)(2,1)S(1)}, bf16[256,256]{1,0:T(8,128)(2,1)S(1)}, u32[]{:S(2)}, u32[]{:S(2)}) collective-permute-start(bf16[256,256]{1,0:T(8,128)(2,1)S(1)} %slice.106), channel_id=1, source_target_pairs={{0,14},{1,15},{2,0},{3,1},{4,2},{5,3},{6,4},{7,5},{8,6},{9,7},{10,... | collective-permute-start | bytes 393224 | tf_op jit(solution)/shard_map/ppermute | solution.py:384
  58.0 12.2 %collective-permute-start.3 = (bf16[144,1024]{1,0:T(8,128)(2,1)S(1)}, bf16[144,1024]{1,0:T(8,128)(2,1)S(1)}, u32[]{:S(2)}, u32[]{:S(2)}) collective-permute-start(bf16[144,1024]{1,0:T(8,128)(2,1)S(1)} %shard_map.96.q0), channel_id=1, source_target_pairs={{0,1},{1,0},{2,3},{3,2},{4,5},{5,4},{6,7},{7,6},{8,9},{9,8},{10,11... | collective-permute-start | bytes 884744 | tf_op jit(solution)/shard_map/ppermute | solution.py:362
  70.2 4.7 %shard_map.102 = (f32[4,1,1024]{2,1,0:T(1,128)S(1)}, f32[4,1,1024]{2,1,0:T(1,128)S(1)}, bf16[8,512,1024]{2,1,0:T(8,128)(2,1)S(1)}, f32[16,1,1024]{2,1,0:T(1,128)S(1)}) custom-call(s32[2]{0:T(128)S(1)} %pad_add_fusion.refs_0_.tab, f32[4,1,1024]{2,1,0:T(1,128)S(1)} %get-tuple-element.74.refs_1_, bf16[4,128,1024]{2,1,0:T(8,128)(2,1)S(1)} %get-tuple-element.76.refs_2_, ...), custom_call_target="tpu_custom_call" | custom-call | flops 1073741824 | bytes 2097152 | tf_op jit(solution)/shard_map/pallas_call | solution.py:386
  75.0 1.7 %shard_map.103 = (f32[4,1,1024]{2,1,0:T(1,128)S(1)}, f32[4,1,1024]{2,1,0:T(1,128)S(1)}, bf16[4,512,1024]{2,1,0:T(8,128)(2,1)S(1)}, f32[8,1,1024]{2,1,0:T(1,128)S(1)}) custom-call(s32[2]{0:T(128)S(1)} %pad_add_fusion.refs_0_.tab, f32[4,1,1024]{2,1,0:T(1,128)S(1)} %get-tuple-element.74.refs_1_, bf16[4,128,1024]{2,1,0:T(8,128)(2,1)S(1)} %get-tuple-element.76.refs_2_, ...), custom_call_target="tpu_custom_call" | custom-call | flops 536870912 | bytes 2097152 | tf_op jit(solution)/shard_map/pallas_call | solution.py:386
  76.9 0.9 shard_map.97
  77.8 3.3 %collective-permute-start.19 = (f32[8,1,1024]{2,1,0:T(1,128)S(1)}, f32[8,1,1024]{2,1,0:T(1,128)S(1)}, u32[]{:S(2)}, u32[]{:S(2)}) collective-permute-start(f32[8,1,1024]{2,1,0:T(1,128)S(1)} %constant_dynamic-update-slice_fusion.2), channel_id=1, source_target_pairs={{0,17},{1,16},{2,19},{3,18},{4,21},{5,20},{6,23},{7,22},{8,25},{9,... | collective-permute-start | bytes 98312 | tf_op jit(solution)/shard_map/ppermute | solution.py:407
  81.1 1.6 %collective-permute-done.19 = f32[8,1,1024]{2,1,0:T(1,128)S(1)} collective-permute-done((f32[8,1,1024]{2,1,0:T(1,128)S(1)}, f32[8,1,1024]{2,1,0:T(1,128)S(1)}, u32[]{:S(2)}, u32[]{:S(2)}) %collective-permute-start.19) | collective-permute-done | bytes 32800 | tf_op jit(solution)/shard_map/ppermute | solution.py:407
  82.9 2.6 %shard_map.104 = (f32[4,128,1024]{2,1,0:T(8,128)S(1)}, f32[1,512,256]{2,1,0:T(8,128)S(1)}) custom-call(s32[2]{0:T(128)S(1)} %pad_add_fusion.refs_0_.tab, f32[4,1,1024]{2,1,0:T(1,128)S(1)} %get-tuple-element.74.refs_1_, f32[4,1,1024]{2,1,0:T(1,128)S(1)} %get-tuple-element.75.refs_2_, f32[4,1,1024]{2,1,0:T(1,128)S(1)} %multiply_add_fusion.refs_3_, ...), custom_call_target="tpu_custom_call" | custom-call | flops 2684354560 | bytes 8388608 | tf_op jit(solution)/shard_map/pallas_call | solution.py:425
  85.6 4.0 %shard_map.105 = (f32[4,128,1024]{2,1,0:T(8,128)S(1)}, f32[2,512,256]{2,1,0:T(8,128)S(1)}) custom-call(s32[2]{0:T(128)S(1)} %pad_add_fusion.refs_0_.tab, f32[4,1,1024]{2,1,0:T(1,128)S(1)} %get-tuple-element.74.refs_1_, f32[4,1,1024]{2,1,0:T(1,128)S(1)} %get-tuple-element.75.refs_2_, ...), custom_call_target="tpu_custom_call", output_to_operand_aliasing={{0}: (11, {})} | custom-call | flops 5368709120 | bytes 8388608 | tf_op jit(solution)/shard_map/pallas_call | solution.py:425
  89.7 7.7 %collective-permute-done.20 = bf16[512,256]{1,0:T(8,128)(2,1)S(1)} collective-permute-done((bf16[512,256]{1,0:T(8,128)(2,1)S(1)}, bf16[512,256]{1,0:T(8,128)(2,1)S(1)}, u32[]{:S(2)}, u32[]{:S(2)}) %collective-permute-start.20) | collective-permute-done | bytes 262176 | tf_op jit(solution)/shard_map/ppermute | solution.py:441
  97.5 7.5 %collective-permute-start.22 = (bf16[512,256]{1,0:T(8,128)(2,1)S(1)}, bf16[512,256]{1,0:T(8,128)(2,1)S(1)}, u32[]{:S(2)}, u32[]{:S(2)}) collective-permute-start(bf16[512,256]{1,0:T(8,128)(2,1)S(1)} %fusion.8), channel_id=1, source_target_pairs={{0,14},{1,15},{2,0},{3,1},{4,2},{5,3},{6,4},{7,5},{8,6},{9,7},{10,... | collective-permute-start | bytes 786440 | tf_op jit(solution)/shard_map/ppermute | solution.py:443
  105.1 4.0 %shard_map.106 = (f32[4,128,1024]{2,1,0:T(8,128)S(1)}, f32[2,512,256]{2,1,0:T(8,128)S(1)}) custom-call(s32[2]{0:T(128)S(1)} %pad_add_fusion.refs_0_.tab, f32[4,1,1024]{2,1,0:T(1,128)S(1)} %get-tuple-element.74.refs_1_, f32[4,1,1024]{2,1,0:T(1,128)S(1)} %get-tuple-element.75.refs_2_, ...), custom_call_target="tpu_custom_call", output_to_operand_aliasing={{0}: (11, {})} | custom-call | flops 5368709120 | bytes 8388608 | tf_op jit(solution)/shard_map/pallas_call | solution.py:425
  109.1 0.9 collective-permute-done.22
  110.0 3.1 %collective-permute-done.21 = bf16[512,256]{1,0:T(8,128)(2,1)S(1)} collective-permute-done((bf16[512,256]{1,0:T(8,128)(2,1)S(1)}, bf16[512,256]{1,0:T(8,128)(2,1)S(1)}, u32[]{:S(2)}, u32[]{:S(2)}) %collective-permute-start.21) | collective-permute-done | bytes 262176 | tf_op jit(solution)/shard_map/ppermute | solution.py:441
  113.2 3.5 %collective-permute-start.24 = (bf16[512,256]{1,0:T(8,128)(2,1)S(1)}, bf16[512,256]{1,0:T(8,128)(2,1)S(1)}, u32[]{:S(2)}, u32[]{:S(2)}) collective-permute-start(bf16[512,256]{1,0:T(8,128)(2,1)S(1)} %get-tuple-element.131), channel_id=1, source_target_pairs={{0,14},{1,15},{2,0},{3,1},{4,2},{5,3},{6,4},{7,5},{8,6},{9,7},{10,... | collective-permute-start | bytes 786440 | tf_op jit(solution)/shard_map/ppermute | solution.py:443
  116.7 4.6 %shard_map.107 = (f32[4,128,1024]{2,1,0:T(8,128)S(1)}, f32[2,512,256]{2,1,0:T(8,128)S(1)}) custom-call(s32[2]{0:T(128)S(1)} %pad_add_fusion.refs_0_.tab, f32[4,1,1024]{2,1,0:T(1,128)S(1)} %get-tuple-element.74.refs_1_, f32[4,1,1024]{2,1,0:T(1,128)S(1)} %get-tuple-element.75.refs_2_, ...), custom_call_target="tpu_custom_call", output_to_operand_aliasing={{0}: (11, {})} | custom-call | flops 5368709120 | bytes 8388608 | tf_op jit(solution)/shard_map/pallas_call | solution.py:425
  121.4 2.8 %collective-permute-done.23 = bf16[512,256]{1,0:T(8,128)(2,1)S(1)} collective-permute-done((bf16[512,256]{1,0:T(8,128)(2,1)S(1)}, bf16[512,256]{1,0:T(8,128)(2,1)S(1)}, u32[]{:S(2)}, u32[]{:S(2)}) %collective-permute-start.23) | collective-permute-done | bytes 262176 | tf_op jit(solution)/shard_map/ppermute | solution.py:441
  124.3 6.2 %shard_map.108 = (bf16[128,1024]{1,0:T(8,128)(2,1)S(1)}, bf16[128,1024]{1,0:T(8,128)(2,1)S(1)}, bf16[128,1024]{1,0:T(8,128)(2,1)S(1)}, bf16[128,1024]{1,0:T(8,128)(2,1)S(1)}, f32[1,512,256]{2,1,0:T(8,128)S(1)}) custom-call(s32[2]{0:T(128)S(1)} %pad_add_fusion.refs_0_.tab, f32[4,1,1024]{2,1,0:T(1,128)S(1)} %get-tuple-element.74.refs_1_, ...), custom_call_target="tpu_custom_call" | custom-call | flops 2684354560 | bytes 8388608 | tf_op jit(solution)/shard_map/pallas_call | solution.py:425
  130.5 2.6 %collective-permute-start.31 = (bf16[128,1024]{1,0:T(8,128)(2,1)S(1)}, bf16[128,1024]{1,0:T(8,128)(2,1)S(1)}, u32[]{:S(2)}, u32[]{:S(2)}) collective-permute-start(bf16[128,1024]{1,0:T(8,128)(2,1)S(1)} %get-tuple-element.139), channel_id=1, source_target_pairs={{0,1},{1,0},{2,3},{3,2},{4,5},{5,4},{6,7},{7,6},{8,9},{9,8},{10,11... | collective-permute-start | bytes 786440 | tf_op jit(solution)/shard_map/ppermute | solution.py:445
  133.1 3.7 %collective-permute-start.26 = (bf16[512,256]{1,0:T(8,128)(2,1)S(1)}, bf16[512,256]{1,0:T(8,128)(2,1)S(1)}, u32[]{:S(2)}, u32[]{:S(2)}) collective-permute-start(bf16[512,256]{1,0:T(8,128)(2,1)S(1)} %get-tuple-element.135), channel_id=1, source_target_pairs={{0,14},{1,15},{2,0},{3,1},{4,2},{5,3},{6,4},{7,5},{8,6},{9,7},{10,... | collective-permute-start | bytes 786440 | tf_op jit(solution)/shard_map/ppermute | solution.py:443
  136.8 0.4 collective-permute-start.30
  137.2 0.5 collective-permute-start.32
  137.7 4.6 %collective-permute-done.26 = bf16[512,256]{1,0:T(8,128)(2,1)S(1)} collective-permute-done((bf16[512,256]{1,0:T(8,128)(2,1)S(1)}, bf16[512,256]{1,0:T(8,128)(2,1)S(1)}, u32[]{:S(2)}, u32[]{:S(2)}) %collective-permute-start.26) | collective-permute-done | bytes 262176 | tf_op jit(solution)/shard_map/ppermute | solution.py:443
  142.3 3.1 %collective-permute-done.25 = bf16[512,256]{1,0:T(8,128)(2,1)S(1)} collective-permute-done((bf16[512,256]{1,0:T(8,128)(2,1)S(1)}, bf16[512,256]{1,0:T(8,128)(2,1)S(1)}, u32[]{:S(2)}, u32[]{:S(2)}) %collective-permute-start.25) | collective-permute-done | bytes 262176 | tf_op jit(solution)/shard_map/ppermute | solution.py:441
  145.6 1.3 collective-permute-start.27
  146.9 0.4 collective-permute-start.28
  147.4 1.3 collective-permute-start.29
  148.7 1.8 %collective-permute-done.28.a2 = bf16[128,256]{1,0:T(8,128)(2,1)S(1)} collective-permute-done((bf16[128,256]{1,0:T(8,128)(2,1)S(1)}, bf16[128,256]{1,0:T(8,128)(2,1)S(1)}, u32[]{:S(2)}, u32[]{:S(2)}) %collective-permute-start.28) | collective-permute-done | bytes 65568 | tf_op jit(solution)/shard_map/ppermute | solution.py:449
  150.5 1.7 %collective-permute-done.29.a3 = bf16[128,256]{1,0:T(8,128)(2,1)S(1)} collective-permute-done((bf16[128,256]{1,0:T(8,128)(2,1)S(1)}, bf16[128,256]{1,0:T(8,128)(2,1)S(1)}, u32[]{:S(2)}, u32[]{:S(2)}) %collective-permute-start.29) | collective-permute-done | bytes 65568 | tf_op jit(solution)/shard_map/ppermute | solution.py:449
  152.2 1.4 shard_map.109
  (65 shorter events, 2.4 us)
Async XLA Ops:
  0.6 47.1 %copy-start.1 = (bf16[1,128,1024]{2,1,0:T(8,128)(2,1)S(1)}, bf16[1,128,1024]{2,1,0:T(8,128)(2,1)}, u32[]{:S(2)}) copy-start(bf16[1,128,1024]{2,1,0:T(8,128)(2,1)} %param.10) | copy-start | bytes 786436
  0.6 47.1 %copy-start.2 = (bf16[1,128,1024]{2,1,0:T(8,128)(2,1)S(1)}, bf16[1,128,1024]{2,1,0:T(8,128)(2,1)}, u32[]{:S(2)}) copy-start(bf16[1,128,1024]{2,1,0:T(8,128)(2,1)} %param.11) | copy-start | bytes 786436
  3.9 19.0 %collective-permute-start.1 = (bf16[144,1024]{1,0:T(8,128)(2,1)}, bf16[144,1024]{1,0:T(8,128)(2,1)S(1)}, u32[]{:S(2)}, u32[]{:S(2)}) collective-permute-start(bf16[144,1024]{1,0:T(8,128)(2,1)} %get-tuple-element.73.q0), channel_id=1, source_target_pairs={{0,16},{1,17},{2,18},{3,19},{4,20},{5,21},{6,22},{7,23},{8,24},{9,... | collective-permute-start | bytes 884744 | tf_op jit(solution)/shard_map/ppermute | solution.py:360
  5.3 2.6 %collective-permute-start.6 = (bf16[144,256]{1,0:T(8,128)(2,1)}, bf16[144,256]{1,0:T(8,128)(2,1)S(1)}, u32[]{:S(2)}, u32[]{:S(2)}) collective-permute-start(bf16[144,256]{1,0:T(8,128)(2,1)} %get-tuple-element.78), channel_id=1, source_target_pairs={{0,1},{1,0},{2,3},{3,2},{4,5},{5,4},{6,7},{7,6},{8,9},{9,8},{10,11... | collective-permute-start | bytes 221192 | tf_op jit(solution)/shard_map/ppermute | solution.py:356
  6.2 7.4 %collective-permute-start.7 = (bf16[144,256]{1,0:T(8,128)(2,1)}, bf16[144,256]{1,0:T(8,128)(2,1)S(1)}, u32[]{:S(2)}, u32[]{:S(2)}) collective-permute-start(bf16[144,256]{1,0:T(8,128)(2,1)} %get-tuple-element.79), channel_id=1, source_target_pairs={{0,16},{1,17},{2,18},{3,19},{4,20},{5,21},{6,22},{7,23},{8,24},{9,... | collective-permute-start | bytes 221192 | tf_op jit(solution)/shard_map/ppermute | solution.py:356
  6.4 9.7 %collective-permute-start.8 = (bf16[144,256]{1,0:T(8,128)(2,1)}, bf16[144,256]{1,0:T(8,128)(2,1)S(1)}, u32[]{:S(2)}, u32[]{:S(2)}) collective-permute-start(bf16[144,256]{1,0:T(8,128)(2,1)} %get-tuple-element.80), channel_id=1, source_target_pairs={{0,17},{1,16},{2,19},{3,18},{4,21},{5,20},{6,23},{7,22},{8,25},{9,... | collective-permute-start | bytes 221192 | tf_op jit(solution)/shard_map/ppermute | solution.py:356
  16.1 0.9 copy-start.3
  17.0 12.6 %collective-permute-start.9 = (bf16[528,256]{1,0:T(8,128)(2,1)S(1)}, bf16[528,256]{1,0:T(8,128)(2,1)S(1)}, u32[]{:S(2)}, u32[]{:S(2)}) collective-permute-start(bf16[528,256]{1,0:T(8,128)(2,1)S(1)} %shard_map.98.refs_5_.refs_9_), channel_id=1, source_target_pairs={{0,2},{1,3},{2,4},{3,5},{4,6},{5,7},{6,8},{7,9},{8,10},{9,11},{10,... | collective-permute-start | bytes 811016 | tf_op jit(solution)/shard_map/ppermute | solution.py:382
  18.7 10.9 %collective-permute-start.11 = (bf16[528,256]{1,0:T(8,128)(2,1)S(1)}, bf16[528,256]{1,0:T(8,128)(2,1)S(1)}, u32[]{:S(2)}, u32[]{:S(2)}) collective-permute-start(bf16[528,256]{1,0:T(8,128)(2,1)S(1)} %shard_map.98.refs_5_.refs_9_), channel_id=1, source_target_pairs={{0,14},{1,15},{2,0},{3,1},{4,2},{5,3},{6,4},{7,5},{8,6},{9,7},{10,... | collective-permute-start | bytes 811016 | tf_op jit(solution)/shard_map/ppermute | solution.py:382
  22.7 9.6 %collective-permute-start = (bf16[144,1024]{1,0:T(8,128)(2,1)}, bf16[144,1024]{1,0:T(8,128)(2,1)S(1)}, u32[]{:S(2)}, u32[]{:S(2)}) collective-permute-start(bf16[144,1024]{1,0:T(8,128)(2,1)} %get-tuple-element.73.q0), channel_id=1, source_target_pairs={{0,1},{1,0},{2,3},{3,2},{4,5},{5,4},{6,7},{7,6},{8,9},{9,8},{10,11... | collective-permute-start | bytes 884744 | tf_op jit(solution)/shard_map/ppermute | solution.py:362
  22.9 9.4 %collective-permute-start.2 = (bf16[144,1024]{1,0:T(8,128)(2,1)S(1)}, bf16[144,1024]{1,0:T(8,128)(2,1)S(1)}, u32[]{:S(2)}, u32[]{:S(2)}) collective-permute-start(bf16[144,1024]{1,0:T(8,128)(2,1)S(1)} %collective-permute-done.1.q2), channel_id=1, source_target_pairs={{0,1},{1,0},{2,3},{3,2},{4,5},{5,4},{6,7},{7,6},{8,9},{9,8},{10,11... | collective-permute-start | bytes 884744 | tf_op jit(solution)/shard_map/ppermute | solution.py:361
  29.6 12.2 %collective-permute-start.10 = (bf16[528,256]{1,0:T(8,128)(2,1)S(1)}, bf16[528,256]{1,0:T(8,128)(2,1)S(1)}, u32[]{:S(2)}, u32[]{:S(2)}) collective-permute-start(bf16[528,256]{1,0:T(8,128)(2,1)S(1)} %collective-permute-done.9.refs_6_.refs_10_), channel_id=1, source_target_pairs={{0,2},{1,3},{2,4},{3,5},{4,6},{5,7},{6,8},{7,9},{8,10},{9,11},{10,... | collective-permute-start | bytes 811016 | tf_op jit(solution)/shard_map/ppermute | solution.py:382
  29.6 12.2 %collective-permute-start.12 = (bf16[528,256]{1,0:T(8,128)(2,1)S(1)}, bf16[528,256]{1,0:T(8,128)(2,1)S(1)}, u32[]{:S(2)}, u32[]{:S(2)}) collective-permute-start(bf16[528,256]{1,0:T(8,128)(2,1)S(1)} %collective-permute-done.11.refs_5_.refs_9_), channel_id=1, source_target_pairs={{0,14},{1,15},{2,0},{3,1},{4,2},{5,3},{6,4},{7,5},{8,6},{9,7},{10,... | collective-permute-start | bytes 811016 | tf_op jit(solution)/shard_map/ppermute | solution.py:382
  32.4 1.0 copy-start
  41.8 10.9 %collective-permute-start.13 = (bf16[528,256]{1,0:T(8,128)(2,1)S(1)}, bf16[528,256]{1,0:T(8,128)(2,1)S(1)}, u32[]{:S(2)}, u32[]{:S(2)}) collective-permute-start(bf16[528,256]{1,0:T(8,128)(2,1)S(1)} %collective-permute-done.10.refs_6_.refs_10_), channel_id=1, source_target_pairs={{0,2},{1,3},{2,4},{3,5},{4,6},{5,7},{6,8},{7,9},{8,10},{9,11},{10,... | collective-permute-start | bytes 811016 | tf_op jit(solution)/shard_map/ppermute | solution.py:382
  41.9 10.8 %collective-permute-start.14 = (bf16[528,256]{1,0:T(8,128)(2,1)S(1)}, bf16[528,256]{1,0:T(8,128)(2,1)S(1)}, u32[]{:S(2)}, u32[]{:S(2)}) collective-permute-start(bf16[528,256]{1,0:T(8,128)(2,1)S(1)} %collective-permute-done.12.refs_5_.refs_9_), channel_id=1, source_target_pairs={{0,14},{1,15},{2,0},{3,1},{4,2},{5,3},{6,4},{7,5},{8,6},{9,7},{10,... | collective-permute-start | bytes 811016 | tf_op jit(solution)/shard_map/ppermute | solution.py:382
  48.0 22.3 %collective-permute-start.4 = (bf16[144,1024]{1,0:T(8,128)(2,1)S(1)}, bf16[144,1024]{1,0:T(8,128)(2,1)S(1)}, u32[]{:S(2)}, u32[]{:S(2)}) collective-permute-start(bf16[144,1024]{1,0:T(8,128)(2,1)S(1)} %shard_map.96.q0), channel_id=1, source_target_pairs={{0,16},{1,17},{2,18},{3,19},{4,20},{5,21},{6,22},{7,23},{8,24},{9,... | collective-permute-start | bytes 884744 | tf_op jit(solution)/shard_map/ppermute | solution.py:360
  52.8 22.2 %collective-permute-start.15 = (bf16[272,256]{1,0:T(8,128)(2,1)S(1)}, bf16[272,256]{1,0:T(8,128)(2,1)S(1)}, u32[]{:S(2)}, u32[]{:S(2)}) collective-permute-start(bf16[272,256]{1,0:T(8,128)(2,1)S(1)} %slice.105), channel_id=1, source_target_pairs={{0,2},{1,3},{2,4},{3,5},{4,6},{5,7},{6,8},{7,9},{8,10},{9,11},{10,... | collective-permute-start | bytes 417800 | tf_op jit(solution)/shard_map/ppermute | solution.py:384
  52.9 22.0 %collective-permute-start.16 = (bf16[256,256]{1,0:T(8,128)(2,1)S(1)}, bf16[256,256]{1,0:T(8,128)(2,1)S(1)}, u32[]{:S(2)}, u32[]{:S(2)}) collective-permute-start(bf16[256,256]{1,0:T(8,128)(2,1)S(1)} %slice.106), channel_id=1, source_target_pairs={{0,14},{1,15},{2,0},{3,1},{4,2},{5,3},{6,4},{7,5},{8,6},{9,7},{10,... | collective-permute-start | bytes 393224 | tf_op jit(solution)/shard_map/ppermute | solution.py:384
  58.0 18.8 %collective-permute-start.3 = (bf16[144,1024]{1,0:T(8,128)(2,1)S(1)}, bf16[144,1024]{1,0:T(8,128)(2,1)S(1)}, u32[]{:S(2)}, u32[]{:S(2)}) collective-permute-start(bf16[144,1024]{1,0:T(8,128)(2,1)S(1)} %shard_map.96.q0), channel_id=1, source_target_pairs={{0,1},{1,0},{2,3},{3,2},{4,5},{5,4},{6,7},{7,6},{8,9},{9,8},{10,11... | collective-permute-start | bytes 884744 | tf_op jit(solution)/shard_map/ppermute | solution.py:362
  70.2 6.6 %collective-permute-start.5 = (bf16[144,1024]{1,0:T(8,128)(2,1)S(1)}, bf16[144,1024]{1,0:T(8,128)(2,1)S(1)}, u32[]{:S(2)}, u32[]{:S(2)}) collective-permute-start(bf16[144,1024]{1,0:T(8,128)(2,1)S(1)} %collective-permute-done.4.q2), channel_id=1, source_target_pairs={{0,1},{1,0},{2,3},{3,2},{4,5},{5,4},{6,7},{7,6},{8,9},{9,8},{10,11... | collective-permute-start | bytes 884744 | tf_op jit(solution)/shard_map/ppermute | solution.py:361
  76.8 4.3 %collective-permute-start.18 = (f32[8,1,1024]{2,1,0:T(1,128)S(1)}, f32[8,1,1024]{2,1,0:T(1,128)S(1)}, u32[]{:S(2)}, u32[]{:S(2)}) collective-permute-start(f32[8,1,1024]{2,1,0:T(1,128)S(1)} %constant_dynamic-update-slice_fusion.2), channel_id=1, source_target_pairs={{0,16},{1,17},{2,18},{3,19},{4,20},{5,21},{6,22},{7,23},{8,24},{9,... | collective-permute-start | bytes 98312 | tf_op jit(solution)/shard_map/ppermute | solution.py:407
  77.8 4.9 %collective-permute-start.19 = (f32[8,1,1024]{2,1,0:T(1,128)S(1)}, f32[8,1,1024]{2,1,0:T(1,128)S(1)}, u32[]{:S(2)}, u32[]{:S(2)}) collective-permute-start(f32[8,1,1024]{2,1,0:T(1,128)S(1)} %constant_dynamic-update-slice_fusion.2), channel_id=1, source_target_pairs={{0,17},{1,16},{2,19},{3,18},{4,21},{5,20},{6,23},{7,22},{8,25},{9,... | collective-permute-start | bytes 98312 | tf_op jit(solution)/shard_map/ppermute | solution.py:407
  81.1 1.6 %collective-permute-start.17 = (f32[8,1,1024]{2,1,0:T(1,128)S(1)}, f32[8,1,1024]{2,1,0:T(1,128)S(1)}, u32[]{:S(2)}, u32[]{:S(2)}) collective-permute-start(f32[8,1,1024]{2,1,0:T(1,128)S(1)} %constant_dynamic-update-slice_fusion.2), channel_id=1, source_target_pairs={{0,1},{1,0},{2,3},{3,2},{4,5},{5,4},{6,7},{7,6},{8,9},{9,8},{10,11... | collective-permute-start | bytes 98312 | tf_op jit(solution)/shard_map/ppermute | solution.py:407
  85.5 11.9 %collective-permute-start.20 = (bf16[512,256]{1,0:T(8,128)(2,1)S(1)}, bf16[512,256]{1,0:T(8,128)(2,1)S(1)}, u32[]{:S(2)}, u32[]{:S(2)}) collective-permute-start(bf16[512,256]{1,0:T(8,128)(2,1)S(1)} %convert_bitcast_fusion), channel_id=1, source_target_pairs={{0,2},{1,3},{2,4},{3,5},{4,6},{5,7},{6,8},{7,9},{8,10},{9,11},{10,... | collective-permute-start | bytes 786440 | tf_op jit(solution)/shard_map/ppermute | solution.py:441
  97.5 12.4 %collective-permute-start.22 = (bf16[512,256]{1,0:T(8,128)(2,1)S(1)}, bf16[512,256]{1,0:T(8,128)(2,1)S(1)}, u32[]{:S(2)}, u32[]{:S(2)}) collective-permute-start(bf16[512,256]{1,0:T(8,128)(2,1)S(1)} %fusion.8), channel_id=1, source_target_pairs={{0,14},{1,15},{2,0},{3,1},{4,2},{5,3},{6,4},{7,5},{8,6},{9,7},{10,... | collective-permute-start | bytes 786440 | tf_op jit(solution)/shard_map/ppermute | solution.py:443
  105.1 8.0 %collective-permute-start.21 = (bf16[512,256]{1,0:T(8,128)(2,1)S(1)}, bf16[512,256]{1,0:T(8,128)(2,1)S(1)}, u32[]{:S(2)}, u32[]{:S(2)}) collective-permute-start(bf16[512,256]{1,0:T(8,128)(2,1)S(1)} %fusion.7), channel_id=1, source_target_pairs={{0,2},{1,3},{2,4},{3,5},{4,6},{5,7},{6,8},{7,9},{8,10},{9,11},{10,... | collective-permute-start | bytes 786440 | tf_op jit(solution)/shard_map/ppermute | solution.py:441
  113.2 8.1 %collective-permute-start.24 = (bf16[512,256]{1,0:T(8,128)(2,1)S(1)}, bf16[512,256]{1,0:T(8,128)(2,1)S(1)}, u32[]{:S(2)}, u32[]{:S(2)}) collective-permute-start(bf16[512,256]{1,0:T(8,128)(2,1)S(1)} %get-tuple-element.131), channel_id=1, source_target_pairs={{0,14},{1,15},{2,0},{3,1},{4,2},{5,3},{6,4},{7,5},{8,6},{9,7},{10,... | collective-permute-start | bytes 786440 | tf_op jit(solution)/shard_map/ppermute | solution.py:443
  116.7 7.5 %collective-permute-start.23 = (bf16[512,256]{1,0:T(8,128)(2,1)S(1)}, bf16[512,256]{1,0:T(8,128)(2,1)S(1)}, u32[]{:S(2)}, u32[]{:S(2)}) collective-permute-start(bf16[512,256]{1,0:T(8,128)(2,1)S(1)} %get-tuple-element.130), channel_id=1, source_target_pairs={{0,2},{1,3},{2,4},{3,5},{4,6},{5,7},{6,8},{7,9},{8,10},{9,11},{10,... | collective-permute-start | bytes 786440 | tf_op jit(solution)/shard_map/ppermute | solution.py:441
  130.5 6.6 %collective-permute-start.31 = (bf16[128,1024]{1,0:T(8,128)(2,1)S(1)}, bf16[128,1024]{1,0:T(8,128)(2,1)S(1)}, u32[]{:S(2)}, u32[]{:S(2)}) collective-permute-start(bf16[128,1024]{1,0:T(8,128)(2,1)S(1)} %get-tuple-element.139), channel_id=1, source_target_pairs={{0,1},{1,0},{2,3},{3,2},{4,5},{5,4},{6,7},{7,6},{8,9},{9,8},{10,11... | collective-permute-start | bytes 786440 | tf_op jit(solution)/shard_map/ppermute | solution.py:445
  133.1 9.2 %collective-permute-start.26 = (bf16[512,256]{1,0:T(8,128)(2,1)S(1)}, bf16[512,256]{1,0:T(8,128)(2,1)S(1)}, u32[]{:S(2)}, u32[]{:S(2)}) collective-permute-start(bf16[512,256]{1,0:T(8,128)(2,1)S(1)} %get-tuple-element.135), channel_id=1, source_target_pairs={{0,14},{1,15},{2,0},{3,1},{4,2},{5,3},{6,4},{7,5},{8,6},{9,7},{10,... | collective-permute-start | bytes 786440 | tf_op jit(solution)/shard_map/ppermute | solution.py:443
  136.8 8.7 %collective-permute-start.25 = (bf16[512,256]{1,0:T(8,128)(2,1)S(1)}, bf16[512,256]{1,0:T(8,128)(2,1)S(1)}, u32[]{:S(2)}, u32[]{:S(2)}) collective-permute-start(bf16[512,256]{1,0:T(8,128)(2,1)S(1)} %get-tuple-element.134), channel_id=1, source_target_pairs={{0,2},{1,3},{2,4},{3,5},{4,6},{5,7},{6,8},{7,9},{8,10},{9,11},{10,... | collective-permute-start | bytes 786440 | tf_op jit(solution)/shard_map/ppermute | solution.py:441
  136.8 11.9 %collective-permute-start.30 = (bf16[128,1024]{1,0:T(8,128)(2,1)S(1)}, bf16[128,1024]{1,0:T(8,128)(2,1)S(1)}, u32[]{:S(2)}, u32[]{:S(2)}) collective-permute-start(bf16[128,1024]{1,0:T(8,128)(2,1)S(1)} %get-tuple-element.137), channel_id=1, source_target_pairs={{0,1},{1,0},{2,3},{3,2},{4,5},{5,4},{6,7},{7,6},{8,9},{9,8},{10,11... | collective-permute-start | bytes 786440 | tf_op jit(solution)/shard_map/ppermute | solution.py:452
  137.2 15.0 %collective-permute-start.32 = (bf16[128,1024]{1,0:T(8,128)(2,1)S(1)}, bf16[128,1024]{1,0:T(8,128)(2,1)S(1)}, u32[]{:S(2)}, u32[]{:S(2)}) collective-permute-start(bf16[128,1024]{1,0:T(8,128)(2,1)S(1)} %add_convert_fusion), channel_id=1, source_target_pairs={{0,16},{1,17},{2,18},{3,19},{4,20},{5,21},{6,22},{7,23},{8,24},{9,... | collective-permute-start | bytes 786440 | tf_op jit(solution)/shard_map/ppermute | solution.py:451
  145.6 3.1 %collective-permute-start.27 = (bf16[128,256]{1,0:T(8,128)(2,1)S(1)}, bf16[128,256]{1,0:T(8,128)(2,1)S(1)}, u32[]{:S(2)}, u32[]{:S(2)}) collective-permute-start(bf16[128,256]{1,0:T(8,128)(2,1)S(1)} %get-tuple-element.149), channel_id=1, source_target_pairs={{0,1},{1,0},{2,3},{3,2},{4,5},{5,4},{6,7},{7,6},{8,9},{9,8},{10,11... | collective-permute-start | bytes 196616 | tf_op jit(solution)/shard_map/ppermute | solution.py:449
  146.9 3.5 %collective-permute-start.28 = (bf16[128,256]{1,0:T(8,128)(2,1)S(1)}, bf16[128,256]{1,0:T(8,128)(2,1)S(1)}, u32[]{:S(2)}, u32[]{:S(2)}) collective-permute-start(bf16[128,256]{1,0:T(8,128)(2,1)S(1)} %get-tuple-element.148), channel_id=1, source_target_pairs={{0,16},{1,17},{2,18},{3,19},{4,20},{5,21},{6,22},{7,23},{8,24},{9,... | collective-permute-start | bytes 196616 | tf_op jit(solution)/shard_map/ppermute | solution.py:449
  147.4 4.8 %collective-permute-start.29 = (bf16[128,256]{1,0:T(8,128)(2,1)S(1)}, bf16[128,256]{1,0:T(8,128)(2,1)S(1)}, u32[]{:S(2)}, u32[]{:S(2)}) collective-permute-start(bf16[128,256]{1,0:T(8,128)(2,1)S(1)} %get-tuple-element.147), channel_id=1, source_target_pairs={{0,17},{1,16},{2,19},{3,18},{4,21},{5,20},{6,23},{7,22},{8,25},{9,... | collective-permute-start | bytes 196616 | tf_op jit(solution)/shard_map/ppermute | solution.py:449
